TPU v7x, 256 devices: a whole 4x4x8 slice. The times are simulated.
256 devices in a mesh: seq: 16 (over x_hi, z), rep: 16 (over y, x_lo, core).
Axes of the slice: x: 4 (x_hi: 2, x_lo: 2; x = x_hi * 2 + x_lo), y: 4, z: 8, core: 2. Of those that a mesh axis runs over, the one named last changes fastest.
Arguments:
- t_query: bfloat16 [16, 2048, 4096], P('rep', 'seq'), may hold values from -45 to 45
- t_key: bfloat16 [16, 2048, 512], P('rep', 'seq'), may hold values from -4 to 4
- t_value: bfloat16 [16, 2048, 512], P('rep', 'seq'), may hold values from -6 to 6
- s_query: bfloat16 [16, 2048, 2048], P('rep', 'seq'), may hold values from -45 to 45
- s_key: bfloat16 [16, 2048, 512], P('rep', 'seq'), may hold values from -4 to 4
- student_value: bfloat16 [16, 2048, 512], P('rep', 'seq'), may hold values from -6 to 6
- student_wo: bfloat16 [2048, 2048], P('seq'), may hold values from -0.125 to 0.125
- projection: bfloat16 [4096, 2048], P('seq'), may hold values from -0.09375 to 0.09375
- doc_ids: int32 [16, 2048], P('rep'), may hold values from 0 to 15, never falling along the last dimension, each value on 1 to 512 neighbouring positions
- span_order: int32 [16, 32], P('rep'), may hold values from 0 to 31, each once within a row
Outputs:
- seq_loss: float32 [16], P('rep')
- d_wo: float32 [2048, 2048], P('seq', 'rep')
- d_query: bfloat16 [16, 2048, 2048], P('rep', 'seq')
- d_key: bfloat16 [16, 2048, 512], P('rep', 'seq')
- d_value: bfloat16 [16, 2048, 512], P('rep', 'seq')
All inputs are finite; a program needn't handle non-finite values.
Results may differ from a plain program's by a relative error of at most 0.018.
The roundings to bfloat16 on the way count: a program that leaves them out, or rounds other values in their place, can miss the bound.
Values may be sent and summed in bfloat16 or wider, within the bound.
No kernel may reach another device: no remote copies, remote signals or barrier semaphores. Data moves between devices by JAX's collectives and lax.ppermute only.
A program may use at most 128 MiB of HBM per device.

v0:
```python
import math

import jax
import jax.numpy as jnp
from jax import lax
from jax.sharding import PartitionSpec as P

HEAD_WIDTH = 128


MASKED = -1e30


def stored_positions(order_row, length):
    half_len = length // order_row.shape[0]
    offsets = jnp.arange(half_len, dtype=jnp.int32)
    return (order_row[:, None] * half_len + offsets[None, :]).reshape(length)


def head_attention(queries, key_rows, val_rows, positions, stored_docs):
    length = queries.shape[0]
    row_block = math.gcd(length, 512)
    scaling = 1.0 / math.sqrt(HEAD_WIDTH)

    def one_block(block_id):
        first_row = block_id * row_block
        q_block = lax.dynamic_slice_in_dim(queries, first_row, row_block, 0)
        q_pos = lax.dynamic_slice_in_dim(positions, first_row, row_block, 0)
        q_docs = lax.dynamic_slice_in_dim(stored_docs, first_row, row_block, 0)
        allowed = (q_docs[:, None] == stored_docs[None, :]) & (positions[None, :] <= q_pos[:, None])
        scores = (
            jnp.einsum("qhd,kd->hqk", q_block, key_rows, preferred_element_type=jnp.float32)
            * scaling
        )
        scores = jnp.where(allowed, scores, MASKED)
        maximum = jnp.max(scores, axis=2, keepdims=True)
        weights = jnp.where(allowed, jnp.exp(scores - maximum), 0.0)
        totals = jnp.sum(weights, axis=2, keepdims=True)
        prob_rows = (weights / totals).astype(jnp.bfloat16)
        mixed_rows = jnp.einsum(
            "hqk,kd->qhd", prob_rows, val_rows, preferred_element_type=jnp.float32
        )
        return (prob_rows, mixed_rows.astype(jnp.bfloat16))

    block_ids = jnp.arange(length // row_block, dtype=jnp.int32)
    return lax.map(one_block, block_ids)


def shards(
    t_query,
    t_key,
    t_value,
    s_query,
    s_key,
    student_value,
    student_wo,
    projection,
    doc_ids,
    span_order,
):
    groups = lax.axis_size("seq")
    my_index = lax.axis_index("seq")
    tokens = t_query.shape[1]
    length = tokens * groups
    scaling = 1.0 / math.sqrt(HEAD_WIDTH)
    positions = stored_positions(span_order[0], length)
    stored_docs = jnp.take(doc_ids[0], positions)
    first_own = my_index * tokens
    own_pos = lax.dynamic_slice_in_dim(positions, first_own, tokens, 0)
    own_docs = lax.dynamic_slice_in_dim(stored_docs, first_own, tokens, 0)
    t_heads_all = t_query.shape[2] // HEAD_WIDTH
    t_kv = t_key.shape[2] // HEAD_WIDTH
    t_local = t_heads_all // groups
    t_share = t_heads_all // t_kv
    own_queries = t_query[0].reshape(tokens, t_kv, t_share, HEAD_WIDTH)
    start_state = (
        jnp.full((t_kv, t_share, tokens), MASKED, jnp.float32),
        jnp.zeros((t_kv, t_share, tokens), jnp.float32),
        jnp.zeros((t_kv, t_share, tokens, HEAD_WIDTH), jnp.float32),
    )
    carried = start_state
    key_piece = lax.all_gather(t_key[0], "seq", axis=0, tiled=True)
    val_piece = lax.all_gather(t_value[0], "seq", axis=0, tiled=True)
    row_count = key_piece.shape[0]
    sub_rows = math.gcd(row_count, 512)
    for offset in range(0, row_count, sub_rows):
        key_block = key_piece[offset : offset + sub_rows].reshape(sub_rows, t_kv, HEAD_WIDTH)
        val_block = val_piece[offset : offset + sub_rows].reshape(sub_rows, t_kv, HEAD_WIDTH)
        key_pos = lax.dynamic_slice_in_dim(positions, offset, sub_rows, 0)
        key_docs = lax.dynamic_slice_in_dim(stored_docs, offset, sub_rows, 0)
        allowed = (own_docs[:, None] == key_docs[None, :]) & (key_pos[None, :] <= own_pos[:, None])

        def absorb(states):
            running_max, running_sum, accumulated = states
            scores = (
                jnp.einsum(
                    "tkgd,skd->kgts", own_queries, key_block, preferred_element_type=jnp.float32
                )
                * scaling
            )
            scores = jnp.where(allowed, scores, MASKED)
            new_max = jnp.maximum(running_max, jnp.max(scores, axis=3))
            weights = jnp.where(allowed, jnp.exp(scores - new_max[..., None]), 0.0)
            factor = jnp.exp(running_max - new_max)
            running_sum = running_sum * factor + jnp.sum(weights, axis=3)
            accumulated = accumulated * factor[..., None] + jnp.einsum(
                "kgts,skd->kgtd",
                weights.astype(jnp.bfloat16),
                val_block,
                preferred_element_type=jnp.float32,
            )
            return (new_max, running_sum, accumulated)

        carried = lax.cond(jnp.any(allowed), absorb, lambda unchanged: unchanged, carried)
    running_max, running_sum, accumulated = carried
    teacher_rows = (accumulated / running_sum[..., None]).astype(jnp.bfloat16)
    teacher_rows = jnp.transpose(teacher_rows, (2, 0, 1, 3)).reshape(
        tokens, groups, t_local * HEAD_WIDTH
    )
    teacher_out = lax.all_to_all(
        teacher_rows, "seq", split_axis=1, concat_axis=0, tiled=True
    ).reshape(length, t_local * HEAD_WIDTH)
    s_heads_all = s_query.shape[2] // HEAD_WIDTH
    s_local = s_heads_all // groups
    s_kv = s_key.shape[2] // HEAD_WIDTH
    student_rows = s_query[0].reshape(tokens, groups, s_local * HEAD_WIDTH)
    student_heads = lax.all_to_all(student_rows, "seq", split_axis=1, concat_axis=0, tiled=True)
    all_keys, all_values = (
        lax.all_gather(s_key[0], "seq", axis=0, tiled=True),
        lax.all_gather(student_value[0], "seq", axis=0, tiled=True),
    )
    kv_index = my_index // (groups // s_kv)
    key_heads = lax.dynamic_slice_in_dim(all_keys, kv_index * HEAD_WIDTH, HEAD_WIDTH, 1)
    val_heads = lax.dynamic_slice_in_dim(all_values, kv_index * HEAD_WIDTH, HEAD_WIDTH, 1)
    prob_blocks, student_blocks = head_attention(
        student_heads, key_heads, val_heads, positions, stored_docs
    )
    student_out = student_blocks.reshape(length, s_local * HEAD_WIDTH)
    width_all = student_wo.shape[1]
    own_diff = lax.psum_scatter(
        (
            jnp.dot(student_out, student_wo, preferred_element_type=jnp.float32)
            - jnp.dot(teacher_out, projection, preferred_element_type=jnp.float32)
        ).astype(jnp.bfloat16),
        "seq",
        scatter_dimension=0,
        tiled=True,
    ).astype(jnp.float32)
    squares = lax.psum(jnp.sum(own_diff * own_diff), "seq")
    seq_loss = (squares / (length * width_all)).reshape(1)
    own_grad = own_diff.astype(jnp.bfloat16)
    piece_rows = lax.all_gather(own_grad, "seq", axis=0, tiled=True)
    attn_rows = jnp.einsum("rc,hc->rh", piece_rows, student_wo, preferred_element_type=jnp.float32)
    d_attn = attn_rows
    d_weight = jnp.einsum("rh,rc->hc", student_out, piece_rows, preferred_element_type=jnp.float32)
    d_attn, d_weight = (d_attn, d_weight)
    row_block = math.gcd(length, 512)
    blocks = length // row_block
    grad_blocks = d_attn.astype(jnp.bfloat16).reshape(blocks, row_block, s_local, HEAD_WIDTH)
    query_blocks = student_heads.reshape(blocks, row_block, s_local, HEAD_WIDTH)

    def back_block(carried, inputs):
        d_key, d_value = carried
        prob_block, out_block, grad_block, query_block = inputs
        row_delta = jnp.sum(grad_block.astype(jnp.float32) * out_block.astype(jnp.float32), axis=2)
        d_value = d_value + jnp.einsum(
            "hqk,qhd->kd", prob_block, grad_block, preferred_element_type=jnp.float32
        )
        d_prob = jnp.einsum(
            "qhd,kd->hqk", grad_block, val_heads, preferred_element_type=jnp.float32
        )
        d_score = (
            prob_block.astype(jnp.float32) * (d_prob - jnp.transpose(row_delta)[:, :, None])
        ).astype(jnp.bfloat16)
        d_query = (
            jnp.einsum("hqk,kd->qhd", d_score, key_heads, preferred_element_type=jnp.float32)
            * scaling
        ).astype(jnp.bfloat16)
        d_key = d_key + jnp.einsum(
            "hqk,qhd->kd", d_score, query_block, preferred_element_type=jnp.float32
        )
        return ((d_key, d_value), d_query)

    zero_rows = jnp.zeros((length, HEAD_WIDTH), jnp.float32)
    (d_key, d_value), d_query = lax.scan(
        back_block, (zero_rows, zero_rows), (prob_blocks, student_blocks, grad_blocks, query_blocks)
    )
    query_part = d_query.reshape(length, 1, s_local * HEAD_WIDTH)
    key_part = (d_key * scaling).astype(jnp.bfloat16).reshape(length, 1, HEAD_WIDTH)
    value_part = d_value.astype(jnp.bfloat16).reshape(length, 1, HEAD_WIDTH)
    back_query, back_key, back_value = (
        lax.all_to_all(query_part, "seq", split_axis=0, concat_axis=1, tiled=True),
        lax.all_to_all(key_part, "seq", split_axis=0, concat_axis=1, tiled=True),
        lax.all_to_all(value_part, "seq", split_axis=0, concat_axis=1, tiled=True),
    )
    repeat_count = groups // s_kv

    def merge_slots(slot_rows):
        summed = (
            slot_rows.reshape(tokens, s_kv, repeat_count, HEAD_WIDTH)
            .astype(jnp.float32)
            .sum(axis=2)
        )
        return summed.astype(jnp.bfloat16).reshape(1, tokens, s_kv * HEAD_WIDTH)

    weight_share = lax.psum_scatter(
        d_weight.astype(jnp.bfloat16), "rep", scatter_dimension=1, tiled=True
    ).astype(jnp.float32)
    return (
        seq_loss,
        weight_share,
        back_query.reshape(1, tokens, s_heads_all * HEAD_WIDTH),
        merge_slots(back_key),
        merge_slots(back_value),
    )


def solution(mesh):
    in_specs = (
        P("rep", "seq", None),
        P("rep", "seq", None),
        P("rep", "seq", None),
        P("rep", "seq", None),
        P("rep", "seq", None),
        P("rep", "seq", None),
        P("seq", None),
        P("seq", None),
        P("rep", None),
        P("rep", None),
    )
    out_specs = (
        P("rep"),
        P("seq", "rep"),
        P("rep", "seq", None),
        P("rep", "seq", None),
        P("rep", "seq", None),
    )
    return jax.shard_map(shards, mesh=mesh, in_specs=in_specs, out_specs=out_specs, check_vma=False)
```

profile of v0, /device:TPU:4, one launch (start us, length us, event | category | flops | bytes accessed | tf_op | source)
XLA Modules:
  0.0 965.3 jit_solution(540645325133309990)
XLA Ops:
  14.1 11.4 %all-to-all-start = ((bf16[128,16,128]{0,2,1:T(8,128)(2,1)}), bf16[128,16,128]{0,2,1:T(8,128)(2,1)S(1)}, u32[]{:S(2)}, u32[]{:S(2)}) async-start(bf16[128,16,128]{0,2,1:T(8,128)(2,1)} %bitcast.19), calls=%async_computation | async-start | bytes 1048576 | tf_op jit(solution)/shard_map/all_to_all | solution.py:127
  26.5 11.8 %gather_fusion = s32[2048]{0:T(1024)S(1)} fusion(s32[2048]{0:T(1024)S(1)} %bitcast.316, s32[2048]{0:T(1024)S(1)} %broadcast_clamp_fusion), kind=kCustom, calls=%fused_computation | custom fusion | bytes 24576 | tf_op jit(solution)/shard_map/jit(_take)/gather | solution.py:67
  45.3 55.4 %all-gather.16.cloned.1.call-done = bf16[1,2048,512]{1,2,0:T(8,128)(2,1)} async-done(((bf16[1,128,512]{1,2,0:T(8,128)(2,1)}), bf16[1,2048,512]{1,2,0:T(8,128)(2,1)}) %all-gather.16.cloned.1.call-update) | async-done | bytes 2097168 | tf_op jit(solution)/shard_map/all_gather | solution.py:82
  101.9 83.1 %all-gather.18.cloned.1.call-done = bf16[1,2048,512]{1,2,0:T(8,128)(2,1)} async-done(((bf16[1,128,512]{1,2,0:T(8,128)(2,1)}), bf16[1,2048,512]{1,2,0:T(8,128)(2,1)}) %all-gather.18.cloned.1.call-update) | async-done | bytes 2097168 | tf_op jit(solution)/shard_map/all_gather | solution.py:83
  187.1 10.2 %conditional.4 = (f32[4,8,128]{2,1,0:T(8,128)}, f32[4,8,128]{2,1,0:T(8,128)S(1)}, f32[4,8,128,128]{3,2,1,0:T(8,128)}) conditional(s32[]{:T(128)} %convert_element_type.124, () %tuple.44, (pred[128,512]{0,1:T(8,128)(4,1)S(1)}, bf16[512,4,128]{0,2,1:T(8,128)(2,1)S(1)}, bf16[128,4,8,128]{0,3,2,1:T(8,128)(2,1)S(1)}, ...), branch_computations={%region_8.9_spmd, %region_9.0_spmd} | conditional | flops 1101545472 | bytes 29736984 | solution.py:114
  197.3 11.0 %conditional.5 = ((f32[4,8,128]{2,1,0:T(8,128)}, f32[4,8,128]{2,1,0:T(8,128)S(1)}, f32[4,8,128,128]{3,2,1,0:T(8,128)})) conditional(s32[]{:T(128)} %convert_element_type.123, (f32[4,8,128]{2,1,0:T(8,128)}, f32[4,8,128]{2,1,0:T(8,128)S(1)}, f32[4,8,128,128]{3,2,1,0:T(8,128)}) %conditional.4, (pred[128,512]{0,1:T(8,128)(4,1)S(1)}, ...), branch_computations={%region_12.13_spmd, %region_13.16_spmd} | conditional | flops 1102061568 | bytes 34013244 | solution.py:114
  202.4 5.3 multiply_add_fusion
  208.3 13.3 %conditional.6 = ((f32[4,8,128]{2,1,0:T(8,128)}, f32[4,8,128]{2,1,0:T(8,128)S(1)}, f32[4,8,128,128]{3,2,1,0:T(8,128)})) conditional(s32[]{:T(128)} %convert_element_type.122, (f32[4,8,128]{2,1,0:T(8,128)}, f32[4,8,128]{2,1,0:T(8,128)S(1)}, f32[4,8,128,128]{3,2,1,0:T(8,128)}) %get-tuple-element.785, (pred[128,512]{0,1:T(8,128)(4,1)S(1)}, ...), branch_computations={%region_16.17_spmd, %region_17.20_spmd} | conditional | flops 1102061568 | bytes 34013216 | solution.py:114
  215.7 5.3 multiply_add_fusion.2
  224.8 19.7 %all-to-all-start.1 = ((bf16[128,16,256]{0,2,1:T(8,128)(2,1)}), bf16[128,16,256]{0,2,1:T(8,128)(2,1)S(1)}, u32[]{:S(2)}, u32[]{:S(2)}) async-start(bf16[128,16,256]{0,2,1:T(8,128)(2,1)} %bitcast.321), calls=%async_computation.1 | async-start | bytes 2097152 | tf_op jit(solution)/shard_map/all_to_all | solution.py:120
  244.8 35.5 %all-gather.14.cloned.1.call-done = bf16[1,2048,512]{2,1,0:T(8,128)(2,1)} async-done(((bf16[1,128,512]{2,1,0:T(8,128)(2,1)}), bf16[1,2048,512]{2,1,0:T(8,128)(2,1)}) %all-gather.14.cloned.1.call-update) | async-done | bytes 2097168 | tf_op jit(solution)/shard_map/all_gather | solution.py:130
  282.2 82.8 %all-gather.12.cloned.1.call-done = bf16[1,2048,512]{2,1,0:T(8,128)(2,1)} async-done(((bf16[1,128,512]{2,1,0:T(8,128)(2,1)}), bf16[1,2048,512]{2,1,0:T(8,128)(2,1)}) %all-gather.12.cloned.1.call-update) | async-done | bytes 2097168 | tf_op jit(solution)/shard_map/all_gather | solution.py:129
  367.8 48.5 %while.28 = (s32[]{:T(128)}, bf16[4,1,512,2048]{3,2,1,0:T(8,128)(2,1)}, bf16[4,512,1,128]{3,1,2,0:T(8,128)(2,1)}, s32[4]{0:T(128)S(1)}, s32[2048]{0:T(1024)S(1)}...) while((s32[]{:T(128)}, ...), condition=%wide.region_3.4_spmd.clone, body=%wide.region_0.3_spmd.clone.sunk | while | flops 570491904 | bytes 20315468 | solution.py:46
  416.3 9.1 fusion.98
  425.9 11.3 %subtract_convert_fusion = bf16[2048,2048]{1,0:T(8,128)(2,1)} fusion(f32[2048,2048]{1,0:T(8,128)} %fusion.98, bf16[2048,256]{1,0:T(8,128)(2,1)S(1)} %bitcast.323, bf16[256,2048]{1,0:T(8,128)(2,1)S(1)} %copy-done), kind=kOutput, calls=%fused_computation.101 | convolution fusion | flops 2155872256 | bytes 27262976 | tf_op jit(solution)/shard_map/dot_general | solution.py:143
  437.6 222.1 %reduce-scatter.5.cloned.1.call-done = bf16[128,2048]{1,0:T(8,128)(2,1)} async-done(((bf16[2048,2048]{1,0:T(8,128)(2,1)}), bf16[128,2048]{1,0:T(8,128)(2,1)}) %reduce-scatter.5.cloned.1.call-update) | async-done | bytes 524304 | tf_op jit(solution)/shard_map/reduce_scatter | solution.py:140
  659.7 135.8 %all-gather.10.cloned.1.call-done = bf16[2048,2048]{1,0:T(8,128)(2,1)} async-done(((bf16[128,2048]{1,0:T(8,128)(2,1)}), bf16[2048,2048]{1,0:T(8,128)(2,1)}) %all-gather.10.cloned.1.call-update) | async-done | bytes 8388624 | tf_op jit(solution)/shard_map/all_gather | solution.py:152
  795.5 6.5 convolution_convert_fusion
  802.9 46.5 %while.29 = (s32[]{:T(128)}, f32[2048,128]{1,0:T(8,128)}, f32[2048,128]{1,0:T(8,128)}, bf16[4,512,1,128]{3,1,2,0:T(8,128)(2,1)}, bf16[4,1,512,2048]{3,2,1,0:T(8,...) while((s32[]{:T(128)}, f32[2048,128]{1,0:T(8,128)}, ...), condition=%wide.region_30.31_spmd.clone, body=%wide.region_28.30_spmd.clone.sunk | while | flops 1079377408 | bytes 18619552 | solution.py:185
  853.7 7.3 all-to-all-start.4
  863.0 11.7 %all-to-all-done.4 = bf16[16,2,8192]{2,1,0:T(2,128)(2,1)S(1)} async-done(((bf16[16,2,8192]{2,1,0:T(2,128)(2,1)}), bf16[16,2,8192]{2,1,0:T(2,128)(2,1)S(1)}, u32[]{:S(2)}, u32[]{:S(2)}) %all-to-all-start.4) | async-done | bytes 524320 | tf_op jit(solution)/shard_map/all_to_all | solution.py:194
  874.6 7.4 all-to-all-start.3
  895.3 7.2 all-to-all-start.2
  903.4 43.3 %psum.7 = f32[]{:T(128)} all-reduce(f32[]{:T(128)} %multiply_reduce_fusion.1), channel_id=1, replica_groups=mesh['seq'=16,'rep'=16] {'seq'}, use_global_device_ids=true, to_apply=%region_26.27 | all-reduce | flops 1 | bytes 8 | tf_op jit(solution)/shard_map/psum | solution.py:149
  (174 shorter events, 173.1 us)
Async XLA Ops:
  7.2 418.8 %copy-start = (bf16[256,2048]{1,0:T(8,128)(2,1)S(1)}, bf16[256,2048]{1,0:T(8,128)(2,1)}, u32[]{:S(2)}) copy-start(bf16[256,2048]{1,0:T(8,128)(2,1)} %param.29) | copy-start | bytes 3145732
  7.2 19.3 %copy-start.1 = (s32[1,2048]{1,0:T(1,128)S(1)}, s32[1,2048]{1,0:T(1,128)}, u32[]{:S(2)}) copy-start(s32[1,2048]{1,0:T(1,128)} %param.30) | copy-start | bytes 24580
  7.2 93.5 %all-gather.16.cloned.1.call-start = ((), (), s32[]{:S(2)}) async-start(), calls=%async_computation.11 | async-start | bytes 2228224 | tf_op jit(solution)/shard_map/all_gather | solution.py:82
  9.0 176.1 %all-gather.18.cloned.1.call-start = ((), (), s32[]{:S(2)}) async-start(), calls=%async_computation.12 | async-start | bytes 2228224 | tf_op jit(solution)/shard_map/all_gather | solution.py:83
  10.7 269.6 %all-gather.14.cloned.1.call-start = ((), (), s32[]{:S(2)}) async-start(), calls=%async_computation.10 | async-start | bytes 2228224 | tf_op jit(solution)/shard_map/all_gather | solution.py:130
  11.5 353.6 %all-gather.12.cloned.1.call-start = ((), (), s32[]{:S(2)}) async-start(), calls=%async_computation.9 | async-start | bytes 2228224 | tf_op jit(solution)/shard_map/all_gather | solution.py:129
  14.1 30.2 %all-to-all-start = ((bf16[128,16,128]{0,2,1:T(8,128)(2,1)}), bf16[128,16,128]{0,2,1:T(8,128)(2,1)S(1)}, u32[]{:S(2)}, u32[]{:S(2)}) async-start(bf16[128,16,128]{0,2,1:T(8,128)(2,1)} %bitcast.19), calls=%async_computation | async-start | bytes 1048576 | tf_op jit(solution)/shard_map/all_to_all | solution.py:127
  199.5 2.9 copy-start.6
  224.8 200.6 %all-to-all-start.1 = ((bf16[128,16,256]{0,2,1:T(8,128)(2,1)}), bf16[128,16,256]{0,2,1:T(8,128)(2,1)S(1)}, u32[]{:S(2)}, u32[]{:S(2)}) async-start(bf16[128,16,256]{0,2,1:T(8,128)(2,1)} %bitcast.321), calls=%async_computation.1 | async-start | bytes 2097152 | tf_op jit(solution)/shard_map/all_to_all | solution.py:120
  244.6 415.1 %reduce-scatter.5.cloned.1.call-start = ((), (), s32[]{:S(2)}) async-start(), calls=%async_computation.7 | async-start | bytes 8912896 | tf_op jit(solution)/shard_map/reduce_scatter | solution.py:140
  367.8 48.5 %copy-start.3 = (bf16[128,2048]{1,0:T(8,128)(2,1)S(1)}, bf16[128,2048]{1,0:T(8,128)(2,1)}, u32[]{:S(2)}) copy-start(bf16[128,2048]{1,0:T(8,128)(2,1)} %param.28) | copy-start | bytes 1572868
  437.3 358.2 %copy-start.4 = (bf16[128,2048]{1,0:T(8,128)(2,1)S(1)}, bf16[128,2048]{1,0:T(8,128)(2,1)}, u32[]{:S(2)}) copy-start(bf16[128,2048]{1,0:T(8,128)(2,1)} %param.28) | copy-start | bytes 1572868
  437.3 358.2 %all-gather.10.cloned.1.call-start = ((), (), s32[]{:S(2)}) async-start(), calls=%async_computation.8 | async-start | bytes 8912896 | tf_op jit(solution)/shard_map/all_gather | solution.py:152
  806.6 2.8 copy-start.5
  817.7 3.2 copy-start.5
  829.5 3.2 copy-start.5
  841.3 3.2 copy-start.5
  853.7 21.0 %all-to-all-start.4 = ((bf16[16,2,8192]{2,1,0:T(2,128)(2,1)}), bf16[16,2,8192]{2,1,0:T(2,128)(2,1)S(1)}, u32[]{:S(2)}, u32[]{:S(2)}) async-start(bf16[16,2,8192]{2,1,0:T(2,128)(2,1)} %reshape.415), calls=%async_computation.5 | async-start | bytes 1048576 | tf_op jit(solution)/shard_map/all_to_all | solution.py:194
  874.6 20.7 %all-to-all-start.3 = ((bf16[16,2,8192]{2,1,0:T(2,128)(2,1)}), bf16[16,2,8192]{2,1,0:T(2,128)(2,1)S(1)}, u32[]{:S(2)}, u32[]{:S(2)}) async-start(bf16[16,2,8192]{2,1,0:T(2,128)(2,1)} %reshape.413), calls=%async_computation.4 | async-start | bytes 1048576 | tf_op jit(solution)/shard_map/all_to_all | solution.py:193
  882.0 73.3 %reduce-scatter.7.cloned.1.call-start = ((), (), s32[]{:S(2)}) async-start(), calls=%async_computation.13 | async-start | bytes 557056
  886.9 15.6 %copy-start.2 = (bf16[128,2048]{1,0:T(8,128)(2,1)S(1)}, bf16[128,2048]{1,0:T(8,128)(2,1)}, u32[]{:S(2)}) copy-start(bf16[128,2048]{1,0:T(8,128)(2,1)} %reduce-scatter.5.cloned.1.call-done) | copy-start | bytes 1572868
  895.3 55.2 %all-to-all-start.2 = ((bf16[16,2,8192]{2,1,0:T(2,128)(2,1)}), bf16[16,2,8192]{2,1,0:T(2,128)(2,1)}, u32[]{:S(2)}, u32[]{:S(2)}) async-start(bf16[16,2,8192]{2,1,0:T(2,128)(2,1)} %reshape.411), calls=%async_computation.3 | async-start | bytes 1048576 | tf_op jit(solution)/shard_map/all_to_all | solution.py:192
Sparse Core Ops, SparseCore 0:
  11.0 89.5 all-gather.15
  103.7 81.3 all-gather.17
  187.7 92.6 all-gather.13
  282.8 82.2 all-gather.11
  437.4 222.1 reduce-scatter.4
  662.1 133.3 all-gather.9
  888.1 67.2 reduce-scatter.6
where the time goes:
time: 976 us; the launch traced here: 965 us
  waiting for transfers between devices  633 us (65%)
  matrix products  117 us (12%)
  starting transfers between devices  53.8 us (6%)
  local copies, waits for them, and re-layouts  50.2 us (5%)
  other arithmetic  45.4 us (5%)
  blocking collectives  43.3 us (4%)
  between operations  19.1 us (2%)
    reduce_scatter x1, waiting for transfers between devices, shards(): lax.psum_scatter((jnp.dot(student_out, student_wo, preferred_element_type...  222 us
    all_gather x1, waiting for transfers between devices, shards(): piece_rows = lax.all_gather(own_grad, 'seq', axis=0, tiled=True)  136 us
    all_gather x1, waiting for transfers between devices, shards(): val_piece = lax.all_gather(t_value[0], 'seq', axis=0, tiled=True)  83.1 us
    all_gather x1, waiting for transfers between devices, shards(): lax.all_gather(s_key[0], 'seq', axis=0, tiled=True)  82.8 us
    all_gather x1, waiting for transfers between devices, shards(): key_piece = lax.all_gather(t_key[0], 'seq', axis=0, tiled=True)  55.4 us
    psum x1, blocking collectives, shards(): squares = lax.psum(jnp.sum(own_diff * own_diff), 'seq')  43.3 us
    all_gather x1, waiting for transfers between devices, shards(): lax.all_gather(student_value[0], 'seq', axis=0, tiled=True)  35.5 us
    all_to_all x1, starting transfers between devices, shards(): lax.all_to_all(teacher_rows, 'seq', split_axis=1, concat_axis=0, tiled=True)  19.7 us
  transfers between devices with their start and end apart: 12, of which 9 were waited for; matrix products, arithmetic and copies ran while one was open for 14% of the time, Pallas kernels for 0%

commit v1 on v0

v1 whole, which is shorter than its diff:
```python
import functools
import math

import jax
import jax.numpy as jnp
from jax import lax
from jax.experimental import pallas as pl
from jax.experimental.pallas import tpu as pltpu
from jax.sharding import PartitionSpec as P

D = 128
LENGTH = 2048
HALF = 64
SPANS = LENGTH // HALF
GROUPS = 16
TOKENS = LENGTH // GROUPS
WIDTH = 2048
ROWS = 256
BLOCKS = LENGTH // ROWS
STEP = 128
LIMIT = 512
SPAN = LIMIT + ROWS
STEPS = LIMIT // STEP + 1
SCALE = 1.0 / math.sqrt(D)
LOG2E = math.log2(math.e)
FAR = -1e30


def nt(a, b):
    return lax.dot_general(a, b, (((1,), (1,)), ((), ())), preferred_element_type=jnp.float32)


def nn(a, b):
    return lax.dot_general(a, b, (((1,), (0,)), ((), ())), preferred_element_type=jnp.float32)


def tn(a, b):
    return lax.dot_general(a, b, (((0,), (0,)), ((), ())), preferred_element_type=jnp.float32)


def key_steps(first_ref, block):
    return jnp.clip((block * ROWS - first_ref[block] + STEP - 1) // STEP, 0, STEPS - 1)


def each_window(first_ref, body):
    def one(block, carry):
        needed = key_steps(first_ref, block)
        for extra in range(STEPS):
            width = ROWS + extra * STEP

            @pl.when(needed == extra)
            def _():
                body(block, width)

        return carry

    lax.fori_loop(0, BLOCKS, one, 0)


def spread(order_ref, src_ref, first, dst, offset):
    cols = slice(first, first + dst.shape[1])
    if offset:
        dst[:offset, :] = jnp.zeros((offset, dst.shape[1]), dst.dtype)
    for slot in range(SPANS):
        place = pl.ds(pl.multiple_of(order_ref[slot] * HALF + offset, HALF), HALF)
        half = (slot % 2) * HALF
        dst[place, :] = src_ref[slot // 2, half : half + HALF, cols]


def window(start_ref, block, width):
    row = pl.multiple_of(block * ROWS, ROWS)
    keys = pl.ds(pl.multiple_of(row + SPAN - width, STEP), width)
    lane = lax.broadcasted_iota(jnp.int32, (ROWS, width), 1)
    line = lax.broadcasted_iota(jnp.int32, (ROWS, width), 0)
    begin = start_ref[pl.ds(row, ROWS), :] - (row + ROWS - width)
    allowed = (lane >= begin) & (lane - line <= width - ROWS)
    return pl.ds(row, ROWS), keys, jnp.where(allowed, 0.0, FAR)


def weights_of(queries, key_rows, bias):
    scores = nt(queries, key_rows) * (SCALE * LOG2E) + bias
    weights = jnp.exp2(scores - jnp.max(scores, axis=1, keepdims=True))
    return weights, jnp.sum(weights, axis=1, keepdims=True)


def put_stored(order_ref, src, out_ref, cols, offset=0, scale=None):
    for slot in range(SPANS):
        place = pl.ds(pl.multiple_of(order_ref[slot] * HALF + offset, HALF), HALF)
        value = src[place, :]
        if scale is not None:
            value = (value * scale).astype(out_ref.dtype)
        half = (slot % 2) * HALF
        out_ref[slot // 2, half : half + HALF, cols] = value


def teacher_kernel(order_ref, first_ref, start_ref, in_ref, out_ref, tq, tk, tv, to):
    spread(order_ref, in_ref, 0, tq, 0)
    spread(order_ref, in_ref, 2 * D, tk, LIMIT)
    spread(order_ref, in_ref, 3 * D, tv, LIMIT)

    def body(block, width):
        rows, keys, bias = window(start_ref, block, width)
        key_rows = tk[keys, :]
        val_rows = tv[keys, :]
        for head in range(2):
            cols = slice(head * D, (head + 1) * D)
            weights, totals = weights_of(tq[rows, cols], key_rows, bias)
            to[rows, cols] = (nn(weights.astype(jnp.bfloat16), val_rows) / totals).astype(jnp.bfloat16)

    each_window(first_ref, body)
    put_stored(order_ref, to, out_ref, slice(0, 2 * D))


def student_kernel(order_ref, first_ref, start_ref, in_ref, out_ref, probs_ref, sq, sk, sv, so):
    spread(order_ref, in_ref, 0, sq, 0)
    spread(order_ref, in_ref, D, sk, LIMIT)
    spread(order_ref, in_ref, 2 * D, sv, LIMIT)

    def body(block, width):
        rows, keys, bias = window(start_ref, block, width)
        weights, totals = weights_of(sq[rows, :], sk[keys, :], bias)
        probs = (weights * (1.0 / totals)).astype(jnp.bfloat16)
        probs_ref[block, :, SPAN - width :] = probs
        so[rows, :] = nn(probs, sv[keys, :]).astype(jnp.bfloat16)

    each_window(first_ref, body)
    put_stored(order_ref, so, out_ref, slice(0, D))


def backward_kernel(
    order_ref, first_ref, grad_ref, out_ref, in_ref, probs_ref, back_ref,
    go, so, sq, sk, sv, dq, dk, dv,
):
    spread(order_ref, grad_ref, 0, go, 0)
    spread(order_ref, out_ref, 0, so, 0)
    spread(order_ref, in_ref, 0, sq, 0)
    spread(order_ref, in_ref, D, sk, LIMIT)
    spread(order_ref, in_ref, 2 * D, sv, LIMIT)
    dk[...] = jnp.zeros_like(dk)
    dv[...] = jnp.zeros_like(dv)

    def body(block, width):
        row = pl.multiple_of(block * ROWS, ROWS)
        rows = pl.ds(row, ROWS)
        keys = pl.ds(pl.multiple_of(row + SPAN - width, STEP), width)
        probs = probs_ref[block, :, SPAN - width :]
        grads = go[rows, :]
        delta = jnp.sum(
            grads.astype(jnp.float32) * so[rows, :].astype(jnp.float32), axis=1, keepdims=True
        )
        d_probs = nt(grads, sv[keys, :])
        d_scores = (probs.astype(jnp.float32) * (d_probs - delta)).astype(jnp.bfloat16)
        dq[rows, :] = (nn(d_scores, sk[keys, :]) * SCALE).astype(jnp.bfloat16)
        dk[keys, :] += tn(d_scores, sq[rows, :])
        dv[keys, :] += tn(probs, grads)

    each_window(first_ref, body)
    put_stored(order_ref, dq, back_ref, slice(0, D))
    put_stored(order_ref, dk, back_ref, slice(D, 2 * D), LIMIT, SCALE)
    put_stored(order_ref, dv, back_ref, slice(2 * D, 3 * D), LIMIT, 1.0)


def difference_kernel(sout_ref, tout_ref, w_ref, grad_ref, attn_ref, loss_ref, attn):
    step = pl.program_id(0)
    total = None
    for group in range(GROUPS):
        wo = jnp.concatenate([w_ref[0, group, :D, :], w_ref[1, group, :D, :]], axis=1)
        pj = jnp.concatenate([w_ref[0, group, D:, :], w_ref[1, group, D:, :]], axis=1)
        term = nn(sout_ref[group], wo) - nn(tout_ref[group], pj)
        term = term.astype(jnp.bfloat16).astype(jnp.float32)
        total = term if total is None else total + term
    grad = total.astype(jnp.bfloat16)
    grad_ref[...] = grad
    loss_ref[...] = jnp.sum(total * total, axis=0, keepdims=True)
    for group in range(GROUPS):
        wo = jnp.concatenate([w_ref[0, group, :D, :], w_ref[1, group, :D, :]], axis=1)
        part = nt(grad, wo)

        @pl.when(step == 0)
        def _():
            attn[group] = part

        @pl.when(step > 0)
        def _():
            attn[group] += part

    @pl.when(step == pl.num_programs(0) - 1)
    def _():
        attn_ref[...] = attn[...].astype(jnp.bfloat16)


def weight_kernel(sout_ref, grad_ref, part_ref):
    for group in range(GROUPS):
        part = tn(sout_ref[group], grad_ref[...]).astype(jnp.bfloat16)
        part_ref[0, group] = part[:, :D]
        part_ref[1, group] = part[:, D:]


def merge_kernel(back_ref, dq_ref, dk_ref, dv_ref):
    share = GROUPS // 4
    for group in range(GROUPS):
        dq_ref[:, group * D : (group + 1) * D] = back_ref[group, :, :D]
    for head in range(4):
        cols = slice(head * D, (head + 1) * D)
        for ref, first in ((dk_ref, D), (dv_ref, 2 * D)):
            summed = back_ref[head * share, :, first : first + D].astype(jnp.float32)
            for other in range(1, share):
                summed += back_ref[head * share + other, :, first : first + D].astype(jnp.float32)
            ref[:, cols] = summed.astype(jnp.bfloat16)


def sum_kernel(parts_ref, out_ref):
    total = parts_ref[0].astype(jnp.float32)
    for group in range(1, GROUPS):
        total += parts_ref[group].astype(jnp.float32)
    out_ref[...] = total


def pack_kernel(sq_ref, sk_ref, sv_ref, tq_ref, tk_ref, tv_ref, s_ref, t_ref):
    share = GROUPS // 4
    for group in range(GROUPS):
        key = slice((group // share) * D, (group // share + 1) * D)
        s_ref[group, :, :D] = sq_ref[0, :, group * D : (group + 1) * D]
        s_ref[group, :, D : 2 * D] = sk_ref[0, :, key]
        s_ref[group, :, 2 * D :] = sv_ref[0, :, key]
        t_ref[group, :, : 2 * D] = tq_ref[0, :, 2 * group * D : 2 * (group + 1) * D]
        t_ref[group, :, 2 * D : 3 * D] = tk_ref[0, :, key]
        t_ref[group, :, 3 * D :] = tv_ref[0, :, key]


VM = pl.BlockSpec(memory_space=pltpu.VMEM)
SM = pl.BlockSpec(memory_space=pltpu.SMEM)


def bf(*shape):
    return jax.ShapeDtypeStruct(shape, jnp.bfloat16)


def fl(*shape):
    return jax.ShapeDtypeStruct(shape, jnp.float32)


def scratch(rows, cols, dtype=jnp.bfloat16):
    return pltpu.VMEM((rows, cols), dtype)


def call(kernel, outs, ins, scratches=(), scalars=0, interpret=False):
    specs = [SM] * scalars + [VM] * (len(ins) - scalars)
    single = not isinstance(outs, tuple)
    return pl.pallas_call(
        kernel,
        out_shape=outs,
        in_specs=specs,
        out_specs=VM if single else (VM,) * len(outs),
        scratch_shapes=list(scratches),
        name=kernel.__name__,
        interpret=interpret,
    )(*ins)


def difference(sout, tout, weights, interpret=False):
    return pl.pallas_call(
        difference_kernel,
        grid=(GROUPS // 2,),
        out_shape=(bf(TOKENS, WIDTH), bf(GROUPS, TOKENS, D), fl(1, WIDTH)),
        in_specs=[
            pl.BlockSpec((GROUPS, TOKENS, D), lambda r: (0, 0, 0)),
            pl.BlockSpec((GROUPS, TOKENS, 2 * D), lambda r: (0, 0, 0)),
            pl.BlockSpec((2, GROUPS, 3 * D, D), lambda r: (r, 0, 0, 0)),
        ],
        out_specs=(
            pl.BlockSpec((TOKENS, 2 * D), lambda r: (0, r)),
            pl.BlockSpec((GROUPS, TOKENS, D), lambda r: (0, 0, 0)),
            pl.BlockSpec((1, 2 * D), lambda r: (0, r)),
        ),
        scratch_shapes=[pltpu.VMEM((GROUPS, TOKENS, D), jnp.float32)],
        name="difference",
        interpret=interpret,
    )(sout, tout, weights)


def weight_parts(sout, grad, interpret=False):
    return pl.pallas_call(
        weight_kernel,
        grid=(GROUPS // 2,),
        out_shape=bf(GROUPS, GROUPS, D, D),
        in_specs=[
            pl.BlockSpec((GROUPS, TOKENS, D), lambda r: (0, 0, 0)),
            pl.BlockSpec((TOKENS, 2 * D), lambda r: (0, r)),
        ],
        out_specs=pl.BlockSpec((2, GROUPS, D, D), lambda r: (r, 0, 0, 0)),
        name="weight_parts",
        interpret=interpret,
    )(sout, grad)


def shards(
    t_query, t_key, t_value, s_query, s_key, student_value, student_wo, projection,
    doc_ids, span_order, interpret=False,
):
    run = functools.partial(call, interpret=interpret)
    rep = lax.axis_index("rep")
    order = span_order[0]
    docs = doc_ids[0]
    start = jnp.sum((docs[None, :] < docs[:, None]).astype(jnp.int32), axis=1)
    first = start[::ROWS]
    start = start[:, None]

    mine = jnp.concatenate(
        [
            lax.dynamic_slice_in_dim(student_wo, rep * D, D, 1),
            lax.dynamic_slice_in_dim(projection, rep * D, D, 1),
        ],
        axis=0,
    )
    columns = lax.all_gather(mine, "seq", axis=0)
    columns = lax.all_gather(columns.reshape(GROUPS * 3 * D, D), "rep", axis=0)
    weights = columns.reshape(-1, GROUPS, 3 * D, D)

    def swap(blocks):
        return lax.all_to_all(blocks, "seq", split_axis=0, concat_axis=0, tiled=True)

    s_pack, t_pack = run(
        pack_kernel,
        (bf(GROUPS, TOKENS, 3 * D), bf(GROUPS, TOKENS, 4 * D)),
        (s_query, s_key, student_value, t_query, t_key, t_value),
    )
    s_in = swap(s_pack)
    t_in = swap(t_pack)
    sout, probs = run(
        student_kernel,
        (bf(GROUPS, TOKENS, D), bf(BLOCKS, ROWS, SPAN)),
        (order, first, start, s_in),
        [scratch(LENGTH, D)] + [scratch(LENGTH + LIMIT, D)] * 2 + [scratch(LENGTH, D)],
        scalars=2,
    )
    s_tokens = swap(sout)
    tout = run(
        teacher_kernel,
        bf(GROUPS, TOKENS, 2 * D),
        (order, first, start, t_in),
        [scratch(LENGTH, 2 * D)] + [scratch(LENGTH + LIMIT, D)] * 2 + [scratch(LENGTH, 2 * D)],
        scalars=2,
    )
    t_tokens = swap(tout)
    grad, d_attn, squares = difference(s_tokens, t_tokens, weights, interpret=interpret)
    grads = swap(d_attn)
    seq_loss = (lax.psum(jnp.sum(squares), "seq") / (LENGTH * WIDTH)).reshape(1)
    parts = weight_parts(s_tokens, grad, interpret=interpret)
    parts = parts.reshape(-1, GROUPS * D, D)
    parts = reduce_rep(parts)
    back = run(
        backward_kernel,
        bf(GROUPS, TOKENS, 3 * D),
        (order, first, grads, sout, s_in, probs),
        [scratch(LENGTH, D)] * 3
        + [scratch(LENGTH + LIMIT, D)] * 2
        + [scratch(LENGTH, D)]
        + [scratch(LENGTH + LIMIT, D, jnp.float32)] * 2,
        scalars=2,
    )
    dq, dk, dv = run(
        merge_kernel,
        (bf(TOKENS, GROUPS * D), bf(TOKENS, 4 * D), bf(TOKENS, 4 * D)),
        (swap(back),),
    )
    d_wo = run(sum_kernel, fl(D, D), (swap(parts.reshape(GROUPS, D, D)),))
    return seq_loss, d_wo, dq[None], dk[None], dv[None]


def reduce_rep(parts):
    return lax.psum_scatter(parts, "rep", scatter_dimension=0, tiled=True)


def solution(mesh):
    tokens = P("rep", "seq", None)
    in_specs = (tokens,) * 6 + (P("seq", None),) * 2 + (P("rep", None),) * 2
    out_specs = (P("rep"), P("seq", "rep"), tokens, tokens, tokens)
    return jax.shard_map(shards, mesh=mesh, in_specs=in_specs, out_specs=out_specs, check_vma=False)
```

time: 976 us -> 512 us (0.52)
  waiting for transfers between devices: 633 us -> 201 us
  blocking collectives: 43.3 us -> 183 us
  matrix products: 117 us -> 0 us
  Pallas kernels: 0 us -> 76.6 us
  local copies, waits for them, and re-layouts: 50.2 us -> 5.01 us
  other arithmetic: 45.4 us -> 3.06 us
  starting transfers between devices: 53.8 us -> 24.1 us
    all_gather x5 -> x2, waiting for transfers between devices: 393 us -> 122 us  [the longest x1 84.4 us: shards(): columns = lax.all_gather(mine, 'seq', axis=0)]
    reduce_scatter x1, waiting for transfers between devices: 222 us -> 43.3 us  [reduce_rep(): return lax.psum_scatter(parts, 'rep', scatter_dimension=0, tiled=True)]
    all_to_all x0 -> x4, blocking collectives: none -> 141 us  [swap(): lax.all_to_all(blocks, 'seq', split_axis=0, concat_axis=0, tiled=True)]
    dot_general x34 -> x0, matrix products: 117 us -> none  [the longest x3 15.2 us: absorb(): jnp.einsum('kgts,skd->kgtd', weights.astype(jnp.bfloat16), val_block, pre...]
    pallas_call x0 -> x8, Pallas kernels: none -> 76.6 us  [the longest x6 36.4 us: call(): pl.pallas_call(kernel, out_shape=outs, in_specs=specs, out_specs=VM if si...]
    all_to_all x5 -> x3, starting transfers between devices: 53.1 us -> 24 us  [swap(): lax.all_to_all(blocks, 'seq', split_axis=0, concat_axis=0, tiled=True)]
    all_to_all x5 -> x3, waiting for transfers between devices: 16.1 us -> 36.4 us  [swap(): lax.all_to_all(blocks, 'seq', split_axis=0, concat_axis=0, tiled=True)]
    reduce_sum x14 -> x2, other arithmetic: 19.4 us -> 2.42 us  [the longest x1 1.8 us: shards(): start = jnp.sum((docs[None, :] < docs[:, None]).astype(jnp.int32), axis=1)]
  transfers between devices with their start and end apart: 12 -> 6, of which waited for: 9 -> 5; matrix products, arithmetic and copies ran while one was open for 14% -> 1% of each run, Pallas kernels for 0% -> 7%
where the time goes in v1:
time: 512 us; the launch traced here: 508 us
  waiting for transfers between devices  201 us (39%)
  blocking collectives  183 us (36%)
  Pallas kernels  76.6 us (15%)
  starting transfers between devices  24.1 us (5%)
  between operations  15.6 us (3%)
    all_to_all x4, blocking collectives, swap(): lax.all_to_all(blocks, 'seq', split_axis=0, concat_axis=0, tiled=True)  141 us
    all_gather x1, waiting for transfers between devices, shards(): columns = lax.all_gather(mine, 'seq', axis=0)  84.4 us
    reduce_scatter x1, waiting for transfers between devices, reduce_rep(): return lax.psum_scatter(parts, 'rep', scatter_dimension=0, tiled=True)  43.3 us
    psum x1, blocking collectives, shards(): seq_loss = (lax.psum(jnp.sum(squares), 'seq') / (LENGTH * WIDTH)).reshape(1)  41.1 us
    all_gather x1, waiting for transfers between devices, shards(): columns = lax.all_gather(columns.reshape(GROUPS * 3 * D, D), 'rep', axis=0)  37.2 us
    all_to_all x3, waiting for transfers between devices, swap(): lax.all_to_all(blocks, 'seq', split_axis=0, concat_axis=0, tiled=True)  36.4 us
    pallas_call x6, Pallas kernels, call(): pl.pallas_call(kernel, out_shape=outs, in_specs=specs, out_specs=VM if si...  36.4 us
    pallas_call x1, Pallas kernels, difference(): pl.pallas_call(difference_kernel, grid=(GROUPS // 2,), out_shape=(bf(TOKE...  32.3 us
  transfers between devices with their start and end apart: 6, of which 5 were waited for; matrix products, arithmetic and copies ran while one was open for 1% of the time, Pallas kernels for 7%

profile of v1, /device:TPU:4, one launch (start us, length us, event | category | flops | bytes accessed | tf_op | source)
XLA Modules:
  0.0 508.2 jit_solution(2525699711553330609)
XLA Ops:
  9.2 84.4 %all-gather.5.cloned.1.call-done = bf16[6144,128]{1,0:T(8,128)(2,1)} async-done(((bf16[384,128]{1,0:T(8,128)(2,1)}), bf16[6144,128]{1,0:T(8,128)(2,1)}) %all-gather.5.cloned.1.call-update) | async-done | bytes 1572880 | tf_op jit(solution)/shard_map/all_gather | solution.py:316
  93.5 3.9 pack_kernel.1
  97.4 41.5 %all_to_all.35.in_ref = bf16[16,128,384]{2,1,0:T(8,128)(2,1)} all-to-all(bf16[16,128,384]{2,1,0:T(8,128)(2,1)} %get-tuple-element.15), channel_id=1, replica_groups=mesh['seq'=16,'rep'=16] {'seq'}, dimensions={0} | all-to-all | bytes 3145728 | tf_op jit(solution)/shard_map/all_to_all | solution.py:321
  138.9 7.1 %all-to-all-start.2 = ((bf16[16,128,512]{2,1,0:T(8,128)(2,1)}), bf16[16,128,512]{2,1,0:T(8,128)(2,1)S(1)}, u32[]{:S(2)}, u32[]{:S(2)}) async-start(bf16[16,128,512]{2,1,0:T(8,128)(2,1)} %get-tuple-element.17), calls=%async_computation.2 | async-start | bytes 4194304 | tf_op jit(solution)/shard_map/all_to_all | solution.py:321
  146.0 1.8 convert_reduce_fusion
  148.4 1.4 copy.17.start_ref
  149.8 8.9 %student_kernel.1 = (bf16[16,128,128]{2,1,0:T(8,128)(2,1)}, bf16[8,256,768]{2,1,0:T(8,128)(2,1)}) custom-call(s32[32]{0:T(128)} %bitcast.14, s32[8]{0:T(128)} %slice.3.first_ref, s32[2048,1]{1,0:T(8,128)} %copy.17.start_ref, bf16[16,128,384]{2,1,0:T(8,128)(2,1)} %all_to_all.35.in_ref), custom_call_target="tpu_custom_call" | custom-call | tf_op jit(solution)/shard_map/student_kernel/pallas_call | solution.py:250
  158.7 32.8 %all-to-all-done.2.in_ref = bf16[16,128,512]{2,1,0:T(8,128)(2,1)S(1)} async-done(((bf16[16,128,512]{2,1,0:T(8,128)(2,1)}), bf16[16,128,512]{2,1,0:T(8,128)(2,1)S(1)}, u32[]{:S(2)}, u32[]{:S(2)}) %all-to-all-start.2) | async-done | bytes 2097184 | tf_op jit(solution)/shard_map/all_to_all | solution.py:321
  191.5 7.6 %all-to-all-start.1 = ((bf16[16,128,128]{2,1,0:T(8,128)(2,1)}), bf16[16,128,128]{2,1,0:T(8,128)(2,1)}, u32[]{:S(2)}, u32[]{:S(2)}) async-start(bf16[16,128,128]{2,1,0:T(8,128)(2,1)} %get-tuple-element.16.out_ref), calls=%async_computation.1 | async-start | bytes 1048576 | tf_op jit(solution)/shard_map/all_to_all | solution.py:321
  199.2 10.1 %teacher_kernel.1 = bf16[16,128,256]{2,1,0:T(8,128)(2,1)} custom-call(s32[32]{0:T(128)} %bitcast.15, s32[8]{0:T(128)} %slice.3.first_ref, s32[2048,1]{1,0:T(8,128)} %copy.17.start_ref, bf16[16,128,512]{2,1,0:T(8,128)(2,1)} %copy-done.1), custom_call_target="tpu_custom_call" | custom-call | tf_op jit(solution)/shard_map/teacher_kernel/pallas_call | solution.py:250
  209.2 3.6 all-to-all-done.1.sout_ref
  212.8 32.0 %all_to_all.36.tout_ref = bf16[16,128,256]{2,1,0:T(8,128)(2,1)} all-to-all(bf16[16,128,256]{2,1,0:T(8,128)(2,1)} %teacher_kernel.1), channel_id=1, replica_groups=mesh['seq'=16,'rep'=16] {'seq'}, dimensions={0} | all-to-all | bytes 2097152 | tf_op jit(solution)/shard_map/all_to_all | solution.py:321
  244.8 37.2 %all-gather.7.cloned.1.call-done = bf16[98304,128]{1,0:T(8,128)(2,1)} async-done(((bf16[6144,128]{1,0:T(8,128)(2,1)}), bf16[98304,128]{1,0:T(8,128)(2,1)}) %all-gather.7.cloned.1.call-update) | async-done | bytes 25165840 | tf_op jit(solution)/shard_map/all_gather | solution.py:317
  282.0 32.3 %difference.1 = (bf16[128,2048]{1,0:T(8,128)(2,1)}, bf16[16,128,128]{2,1,0:T(8,128)(2,1)}, f32[1,2048]{1,0:T(1,128)}) custom-call(bf16[16,128,128]{2,1,0:T(8,128)(2,1)} %all-to-all-done.1.sout_ref, bf16[16,128,256]{2,1,0:T(8,128)(2,1)} %all_to_all.36.tout_ref, bf16[16,16,384,128]{3,2,1,0:T(8,128)(2,1)} %bitcast.11), custom_call_target="tpu_custom_call" | custom-call | tf_op jit(solution)/shard_map/difference/pallas_call | solution.py:262
  314.4 7.9 %weight_parts.1 = bf16[16,16,128,128]{3,2,1,0:T(8,128)(2,1)} custom-call(bf16[16,128,128]{2,1,0:T(8,128)(2,1)} %all-to-all-done.1.sout_ref, bf16[128,2048]{1,0:T(8,128)(2,1)} %get-tuple-element.19.grad_ref), custom_call_target="tpu_custom_call" | custom-call | tf_op jit(solution)/shard_map/weight_parts/pallas_call | solution.py:283
  322.2 1.0 copy-done.3
  323.3 23.4 %all_to_all.37.grad_ref = bf16[16,128,128]{2,1,0:T(8,128)(2,1)} all-to-all(bf16[16,128,128]{2,1,0:T(8,128)(2,1)S(1)} %copy-done.3), channel_id=1, replica_groups=mesh['seq'=16,'rep'=16] {'seq'}, dimensions={0} | all-to-all | bytes 1048576 | tf_op jit(solution)/shard_map/all_to_all | solution.py:321
  346.7 9.3 %backward_kernel.1 = bf16[16,128,384]{2,1,0:T(8,128)(2,1)} custom-call(s32[32]{0:T(128)} %bitcast.16, s32[8]{0:T(128)} %slice.3.first_ref, bf16[16,128,128]{2,1,0:T(8,128)(2,1)} %all_to_all.37.grad_ref, bf16[16,128,128]{2,1,0:T(8,128)(2,1)} %get-tuple-element.16.out_ref, bf16[16,128,384]{2,1,0:T(8,128)(2,1)} %all_to_all.35.in_ref, ...), custom_call_target="tpu_custom_call" | custom-call | tf_op jit(solution)/shard_map/backward_kernel/pallas_call | solution.py:250
  356.0 44.6 %all_to_all.38.back_ref = bf16[16,128,384]{2,1,0:T(8,128)(2,1)} all-to-all(bf16[16,128,384]{2,1,0:T(8,128)(2,1)} %backward_kernel.1), channel_id=1, replica_groups=mesh['seq'=16,'rep'=16] {'seq'}, dimensions={0} | all-to-all | bytes 3145728 | tf_op jit(solution)/shard_map/all_to_all | solution.py:321
  400.6 43.3 %reduce-scatter.2.cloned.1.call-done = bf16[1,2048,128]{2,1,0:T(8,128)(2,1)} async-done(((bf16[16,2048,128]{2,1,0:T(8,128)(2,1)}), bf16[1,2048,128]{2,1,0:T(8,128)(2,1)}) %reduce-scatter.2.cloned.1.call-update) | async-done | bytes 524304 | tf_op jit(solution)/shard_map/reduce_scatter | solution.py:372
  443.9 9.3 %all-to-all-start.4 = ((bf16[16,128,128]{2,1,0:T(8,128)(2,1)}), bf16[16,128,128]{2,1,0:T(8,128)(2,1)S(1)}, u32[]{:S(2)}, u32[]{:S(2)}) async-start(bf16[16,128,128]{2,1,0:T(8,128)(2,1)} %bitcast.12), calls=%async_computation.5 | async-start | bytes 1048576 | tf_op jit(solution)/shard_map/all_to_all | solution.py:321
  453.8 41.1 %psum.7 = f32[]{:T(128)} all-reduce(f32[]{:T(128)} %reduce_sum.19), channel_id=1, replica_groups=mesh['seq'=16,'rep'=16] {'seq'}, use_global_device_ids=true, to_apply=%region_2.0 | all-reduce | flops 1 | bytes 8 | tf_op jit(solution)/shard_map/psum | solution.py:348
  495.6 2.4 merge_kernel.1
  498.8 1.7 sum_kernel.1
  (23 shorter events, 4.1 us)
Async XLA Ops:
  7.2 1.2 copy-start
  7.2 86.3 %all-gather.5.cloned.1.call-start = ((), (), s32[]{:S(2)}) async-start(), calls=%async_computation.9 | async-start | bytes 1671168 | tf_op jit(solution)/shard_map/all_gather | solution.py:316
  9.1 272.9 %all-gather.7.cloned.1.call-start = ((), (), s32[]{:S(2)}) async-start(), calls=%async_computation.10 | async-start | bytes 26738688 | tf_op jit(solution)/shard_map/all_gather | solution.py:317
  97.4 48.6 %copy-start.5 = (s32[1,2048]{1,0:T(1,128)S(1)}, s32[1,2048]{1,0:T(1,128)}, u32[]{:S(2)}) copy-start(s32[1,2048]{1,0:T(1,128)} %param.18) | copy-start | bytes 24580
  138.9 52.6 %all-to-all-start.2 = ((bf16[16,128,512]{2,1,0:T(8,128)(2,1)}), bf16[16,128,512]{2,1,0:T(8,128)(2,1)S(1)}, u32[]{:S(2)}, u32[]{:S(2)}) async-start(bf16[16,128,512]{2,1,0:T(8,128)(2,1)} %get-tuple-element.17), calls=%async_computation.2 | async-start | bytes 4194304 | tf_op jit(solution)/shard_map/all_to_all | solution.py:321
  191.5 7.6 %copy-start.1 = (bf16[16,128,512]{2,1,0:T(8,128)(2,1)}, bf16[16,128,512]{2,1,0:T(8,128)(2,1)S(1)}, u32[]{:S(2)}) copy-start(bf16[16,128,512]{2,1,0:T(8,128)(2,1)S(1)} %all-to-all-done.2.in_ref) | copy-start | bytes 6291460
  191.5 21.3 %all-to-all-start.1 = ((bf16[16,128,128]{2,1,0:T(8,128)(2,1)}), bf16[16,128,128]{2,1,0:T(8,128)(2,1)}, u32[]{:S(2)}, u32[]{:S(2)}) async-start(bf16[16,128,128]{2,1,0:T(8,128)(2,1)} %get-tuple-element.16.out_ref), calls=%async_computation.1 | async-start | bytes 1048576 | tf_op jit(solution)/shard_map/all_to_all | solution.py:321
  199.1 244.8 %reduce-scatter.2.cloned.1.call-start = ((), (), s32[]{:S(2)}) async-start(), calls=%async_computation.8 | async-start | bytes 8912896 | tf_op jit(solution)/shard_map/reduce_scatter | solution.py:372
  322.2 1.0 copy-start.3
  356.0 97.2 %copy-start.4 = (f32[1,2048]{1,0:T(1,128)S(1)}, f32[1,2048]{1,0:T(1,128)}, u32[]{:S(2)}) copy-start(f32[1,2048]{1,0:T(1,128)} %get-tuple-element.18) | copy-start | bytes 24580
  443.9 54.1 %all-to-all-start.4 = ((bf16[16,128,128]{2,1,0:T(8,128)(2,1)}), bf16[16,128,128]{2,1,0:T(8,128)(2,1)S(1)}, u32[]{:S(2)}, u32[]{:S(2)}) async-start(bf16[16,128,128]{2,1,0:T(8,128)(2,1)} %bitcast.12), calls=%async_computation.5 | async-start | bytes 1048576 | tf_op jit(solution)/shard_map/all_to_all | solution.py:321
  498.0 0.8 copy-start.2
Sparse Core Ops, SparseCore 0:
  11.2 82.3 all-gather.4
  95.4 186.5 all-gather.6
  322.4 121.4 reduce-scatter.1

commit v2 on v1

v2 whole, which is shorter than its diff:
```python
import functools
import math

import jax
import jax.numpy as jnp
from jax import lax
from jax.experimental import pallas as pl
from jax.experimental.pallas import tpu as pltpu
from jax.sharding import PartitionSpec as P

D = 128
LENGTH = 2048
HALF = 64
SPANS = LENGTH // HALF
GROUPS = 16
RING = 8
PAIR = GROUPS // RING
TOKENS = LENGTH // GROUPS
WIDTH = 2048
BOTH = PAIR * TOKENS
COLS = 4
CHUNK = WIDTH // (2 * COLS * D)
ROWS = 256
BLOCKS = LENGTH // ROWS
STEP = 128
LIMIT = 512
SPAN = LIMIT + ROWS
STEPS = LIMIT // STEP + 1
SCALE = 1.0 / math.sqrt(D)
LOG2E = math.log2(math.e)
FAR = -1e30


def nt(a, b):
    return lax.dot_general(a, b, (((1,), (1,)), ((), ())), preferred_element_type=jnp.float32)


def nn(a, b):
    return lax.dot_general(a, b, (((1,), (0,)), ((), ())), preferred_element_type=jnp.float32)


def tn(a, b):
    return lax.dot_general(a, b, (((0,), (0,)), ((), ())), preferred_element_type=jnp.float32)


def key_steps(first_ref, block):
    return jnp.clip((block * ROWS - first_ref[block] + STEP - 1) // STEP, 0, STEPS - 1)


def each_window(first_ref, body):
    def one(block, carry):
        needed = key_steps(first_ref, block)
        for extra in range(STEPS):
            width = ROWS + extra * STEP

            @pl.when(needed == extra)
            def _():
                body(block, width)

        return carry

    lax.fori_loop(0, BLOCKS, one, 0)


def stored_slots():
    for group in range(GROUPS):
        for half in range(2):
            yield 2 * group + half, (group, half * HALF)


def ring_slots():
    for group in range(GROUPS):
        for half in range(2):
            yield 2 * group + half, (group % RING, (group // RING) * TOKENS + half * HALF)


def spread(order_ref, src_ref, first, dst, offset, slots):
    cols = slice(first, first + dst.shape[1])
    if offset:
        dst[:offset, :] = jnp.zeros((offset, dst.shape[1]), dst.dtype)
    for slot, (block, row) in slots():
        place = pl.ds(pl.multiple_of(order_ref[slot] * HALF + offset, HALF), HALF)
        dst[place, :] = src_ref[block, row : row + HALF, cols]


def window(start_ref, block, width):
    row = pl.multiple_of(block * ROWS, ROWS)
    keys = pl.ds(pl.multiple_of(row + SPAN - width, STEP), width)
    lane = lax.broadcasted_iota(jnp.int32, (ROWS, width), 1)
    line = lax.broadcasted_iota(jnp.int32, (ROWS, width), 0)
    begin = start_ref[pl.ds(row, ROWS), :] - (row + ROWS - width)
    allowed = (lane >= begin) & (lane - line <= width - ROWS)
    return pl.ds(row, ROWS), keys, jnp.where(allowed, 0.0, FAR)


def weights_of(queries, key_rows, bias):
    scores = nt(queries, key_rows) * (SCALE * LOG2E) + bias
    weights = jnp.exp2(scores - jnp.max(scores, axis=1, keepdims=True))
    return weights, jnp.sum(weights, axis=1, keepdims=True)


def put_back(order_ref, src, out_ref, cols, slots, offset=0, scale=None):
    for slot, (block, row) in slots():
        place = pl.ds(pl.multiple_of(order_ref[slot] * HALF + offset, HALF), HALF)
        value = src[place, :]
        if scale is not None:
            value = (value * scale).astype(out_ref.dtype)
        out_ref[block, row : row + HALF, cols] = value


def teacher_kernel(order_ref, first_ref, start_ref, in_ref, out_ref, tq, tk, tv, to):
    spread(order_ref, in_ref, 3 * D, tq, 0, stored_slots)
    spread(order_ref, in_ref, 5 * D, tk, LIMIT, stored_slots)
    spread(order_ref, in_ref, 6 * D, tv, LIMIT, stored_slots)

    def body(block, width):
        rows, keys, bias = window(start_ref, block, width)
        key_rows = tk[keys, :]
        val_rows = tv[keys, :]
        for head in range(2):
            cols = slice(head * D, (head + 1) * D)
            weights, totals = weights_of(tq[rows, cols], key_rows, bias)
            to[rows, cols] = (nn(weights.astype(jnp.bfloat16), val_rows) / -totals).astype(jnp.bfloat16)

    each_window(first_ref, body)
    put_back(order_ref, to, out_ref, slice(0, 2 * D), ring_slots)


def student_kernel(order_ref, first_ref, start_ref, in_ref, out_ref, probs_ref, sq, sk, sv, so):
    spread(order_ref, in_ref, 0, sq, 0, stored_slots)
    spread(order_ref, in_ref, D, sk, LIMIT, stored_slots)
    spread(order_ref, in_ref, 2 * D, sv, LIMIT, stored_slots)

    def body(block, width):
        rows, keys, bias = window(start_ref, block, width)
        weights, totals = weights_of(sq[rows, :], sk[keys, :], bias)
        probs = (weights * (1.0 / totals)).astype(jnp.bfloat16)
        probs_ref[block, :, SPAN - width :] = probs
        so[rows, :] = nn(probs, sv[keys, :]).astype(jnp.bfloat16)

    each_window(first_ref, body)
    put_back(order_ref, so, out_ref, slice(0, D), ring_slots)


def backward_kernel(
    order_ref, first_ref, grad_ref, out_ref, in_ref, probs_ref, back_ref, loss_ref,
    go, so, sq, sk, sv, dq, dk, dv,
):
    spread(order_ref, grad_ref, 0, go, 0, ring_slots)
    spread(order_ref, out_ref, 0, so, 0, ring_slots)
    spread(order_ref, in_ref, 0, sq, 0, stored_slots)
    spread(order_ref, in_ref, D, sk, LIMIT, stored_slots)
    spread(order_ref, in_ref, 2 * D, sv, LIMIT, stored_slots)
    squares = grad_ref[:, BOTH : BOTH + 8, :].astype(jnp.float32)
    loss_ref[...] = jnp.broadcast_to(jnp.sum(squares) / (LENGTH * WIDTH), (1, D))
    dk[...] = jnp.zeros_like(dk)
    dv[...] = jnp.zeros_like(dv)

    def body(block, width):
        row = pl.multiple_of(block * ROWS, ROWS)
        rows = pl.ds(row, ROWS)
        keys = pl.ds(pl.multiple_of(row + SPAN - width, STEP), width)
        probs = probs_ref[block, :, SPAN - width :]
        grads = go[rows, :]
        delta = jnp.sum(
            grads.astype(jnp.float32) * so[rows, :].astype(jnp.float32), axis=1, keepdims=True
        )
        d_probs = nt(grads, sv[keys, :])
        d_scores = (probs.astype(jnp.float32) * (d_probs - delta)).astype(jnp.bfloat16)
        dq[rows, :] = (nn(d_scores, sk[keys, :]) * SCALE).astype(jnp.bfloat16)
        dk[keys, :] += tn(d_scores, sq[rows, :])
        dv[keys, :] += tn(probs, grads)

    each_window(first_ref, body)
    put_back(order_ref, dq, back_ref, slice(0, D), stored_slots)
    put_back(order_ref, dk, back_ref, slice(D, 2 * D), stored_slots, LIMIT, SCALE)
    put_back(order_ref, dv, back_ref, slice(2 * D, 3 * D), stored_slots, LIMIT, 1.0)


def side_by_side(w_ref, group, rows):
    return jnp.concatenate([w_ref[col, group, :rows, :] for col in range(COLS)], axis=1)


def terms_kernel(sout_ref, tout_ref, w_ref, part_ref):
    total = None
    for group in range(RING):
        both = jnp.concatenate([sout_ref[group], tout_ref[group]], axis=1)
        term = nn(both, side_by_side(w_ref, group, 3 * D))
        term = term.astype(jnp.bfloat16).astype(jnp.float32)
        total = term if total is None else total + term
    part_ref[...] = total.astype(jnp.bfloat16)


def gradient_step(mine_ref, other_ref, w_ref, grad_ref):
    diff = mine_ref[...].astype(jnp.float32) + other_ref[...].astype(jnp.float32)
    grad = diff.astype(jnp.bfloat16)
    grad_ref[...] = grad
    square = jnp.sum(diff * diff, axis=0, keepdims=True)
    square = sum(square[:, col * D : (col + 1) * D] for col in range(COLS))
    wo = jnp.concatenate([side_by_side(w_ref, group, D) for group in range(RING)], axis=0)
    return nt(wo, grad), square


def first_kernel(mine_ref, other_ref, w_ref, grad_ref, attn_ref, square_ref):
    part, square = gradient_step(mine_ref, other_ref, w_ref, grad_ref)

    @pl.when(pl.program_id(0) == 0)
    def _():
        attn_ref[...] = part
        square_ref[...] = square

    @pl.when(pl.program_id(0) > 0)
    def _():
        attn_ref[...] += part
        square_ref[...] += square


def second_kernel(mine_ref, other_ref, w_ref, attn_in, square_in, grad_ref, attn_ref, attn, squares):
    part, square = gradient_step(mine_ref, other_ref, w_ref, grad_ref)
    step = pl.program_id(0)

    @pl.when(step == 0)
    def _():
        attn[...] = attn_in[...] + part
        squares[...] = square_in[...] + square

    @pl.when(step > 0)
    def _():
        attn[...] += part
        squares[...] += square

    @pl.when(step == pl.num_programs(0) - 1)
    def _():
        for group in range(RING):
            block = attn[group * D : (group + 1) * D, :]
            attn_ref[group, :BOTH, :] = block.T.astype(jnp.bfloat16)
        total = squares[...]
        high = total.astype(jnp.bfloat16).astype(jnp.float32)
        line = lax.broadcasted_iota(jnp.int32, (8, D), 0)
        rows = jnp.where(line == 0, high, jnp.where(line == 1, total - high, 0.0))
        for group in range(RING):
            attn_ref[group, BOTH:, :] = rows.astype(jnp.bfloat16)


def weight_kernel(sout_ref, first_ref, second_ref, part_ref, turned):
    step = pl.program_id(0)

    @pl.when(step == 0)
    def _():
        for group in range(RING):
            turned[group] = sout_ref[group].T

    grad = jnp.where(step < CHUNK, first_ref[...], second_ref[...])
    for group in range(RING):
        part = nn(turned[group], grad).astype(jnp.bfloat16)
        for col in range(COLS):
            part_ref[col, group] = part[:, col * D : (col + 1) * D]


def merge_kernel(back_ref, dq_ref, dk_ref, dv_ref):
    share = GROUPS // 4
    for group in range(GROUPS):
        dq_ref[:, group * D : (group + 1) * D] = back_ref[group, :, :D]
    for head in range(4):
        cols = slice(head * D, (head + 1) * D)
        for ref, first in ((dk_ref, D), (dv_ref, 2 * D)):
            summed = back_ref[head * share, :, first : first + D].astype(jnp.float32)
            for other in range(1, share):
                summed += back_ref[head * share + other, :, first : first + D].astype(jnp.float32)
            ref[:, cols] = summed.astype(jnp.bfloat16)


def sum_kernel(parts_ref, out_ref):
    total = parts_ref[0].astype(jnp.float32)
    for group in range(1, RING):
        total += parts_ref[group].astype(jnp.float32)
    out_ref[...] = total


def pack_kernel(sq_ref, sk_ref, sv_ref, tq_ref, tk_ref, tv_ref, out_ref):
    share = GROUPS // 4
    for group in range(GROUPS):
        key = slice((group // share) * D, (group // share + 1) * D)
        out_ref[group, :, :D] = sq_ref[0, :, group * D : (group + 1) * D]
        out_ref[group, :, D : 2 * D] = sk_ref[0, :, key]
        out_ref[group, :, 2 * D : 3 * D] = sv_ref[0, :, key]
        out_ref[group, :, 3 * D : 5 * D] = tq_ref[0, :, 2 * group * D : 2 * (group + 1) * D]
        out_ref[group, :, 5 * D : 6 * D] = tk_ref[0, :, key]
        out_ref[group, :, 6 * D :] = tv_ref[0, :, key]


VM = pl.BlockSpec(memory_space=pltpu.VMEM)
SM = pl.BlockSpec(memory_space=pltpu.SMEM)


def bf(*shape):
    return jax.ShapeDtypeStruct(shape, jnp.bfloat16)


def fl(*shape):
    return jax.ShapeDtypeStruct(shape, jnp.float32)


def scratch(rows, cols, dtype=jnp.bfloat16):
    return pltpu.VMEM((rows, cols), dtype)


def call(kernel, outs, ins, scratches=(), scalars=0, interpret=False):
    specs = [SM] * scalars + [VM] * (len(ins) - scalars)
    single = not isinstance(outs, tuple)
    return pl.pallas_call(
        kernel,
        out_shape=outs,
        in_specs=specs,
        out_specs=VM if single else (VM,) * len(outs),
        scratch_shapes=list(scratches),
        name=kernel.__name__,
        interpret=interpret,
    )(*ins)


def whole(*shape):
    return pl.BlockSpec(shape, lambda r: (0,) * len(shape))


def by_columns(rows):
    return pl.BlockSpec((rows, COLS * D), lambda r: (0, r))


def weight_block(rows, half):
    return pl.BlockSpec((COLS, RING, rows, D), lambda r: (r + half * CHUNK, 0, 0, 0))


def terms(sout, tout, weights, half, interpret=False):
    return pl.pallas_call(
        terms_kernel,
        grid=(CHUNK,),
        out_shape=bf(BOTH, WIDTH // 2),
        in_specs=[whole(RING, BOTH, D), whole(RING, BOTH, 2 * D), weight_block(3 * D, half)],
        out_specs=by_columns(BOTH),
        name="terms",
        interpret=interpret,
    )(sout, tout, weights)


def gradients_first(mine, other, weights, interpret=False):
    return pl.pallas_call(
        first_kernel,
        grid=(CHUNK,),
        out_shape=(bf(BOTH, WIDTH // 2), fl(RING * D, BOTH), fl(1, D)),
        in_specs=[by_columns(BOTH), by_columns(BOTH), weight_block(D, 0)],
        out_specs=(by_columns(BOTH), whole(RING * D, BOTH), whole(1, D)),
        name="gradients_first",
        interpret=interpret,
    )(mine, other, weights)


def gradients_second(mine, other, weights, attn, square, interpret=False):
    return pl.pallas_call(
        second_kernel,
        grid=(CHUNK,),
        out_shape=(bf(BOTH, WIDTH // 2), bf(RING, BOTH + 8, D)),
        in_specs=[
            by_columns(BOTH), by_columns(BOTH), weight_block(D, 1),
            whole(RING * D, BOTH), whole(1, D),
        ],
        out_specs=(by_columns(BOTH), whole(RING, BOTH + 8, D)),
        scratch_shapes=[scratch(RING * D, BOTH, jnp.float32), scratch(1, D, jnp.float32)],
        name="gradients_second",
        interpret=interpret,
    )(mine, other, weights, attn, square)


def weight_parts(sout, grad_first, grad_second, interpret=False):
    return pl.pallas_call(
        weight_kernel,
        grid=(2 * CHUNK,),
        out_shape=bf(WIDTH // D, RING, D, D),
        in_specs=[
            whole(RING, BOTH, D),
            pl.BlockSpec((BOTH, COLS * D), lambda r: (0, jnp.minimum(r, CHUNK - 1))),
            pl.BlockSpec((BOTH, COLS * D), lambda r: (0, jnp.maximum(r - CHUNK, 0))),
        ],
        out_specs=pl.BlockSpec((COLS, RING, D, D), lambda r: (r, 0, 0, 0)),
        scratch_shapes=[pltpu.VMEM((RING, D, BOTH), jnp.bfloat16)],
        name="weight_parts",
        interpret=interpret,
    )(sout, grad_first, grad_second)


def tie(value, *after):
    return lax.optimization_barrier((value,) + after)[0]


RINGS = [[ring * RING + place for place in range(RING)] for ring in range(PAIR)]
ACROSS = [(place, (place + RING) % GROUPS) for place in range(GROUPS)]


def gather_columns(student_wo, projection, swap):
    rep = lax.axis_index("rep")
    mine = jnp.concatenate(
        [
            lax.dynamic_slice_in_dim(student_wo, rep * D, D, 1),
            lax.dynamic_slice_in_dim(projection, rep * D, D, 1),
        ],
        axis=0,
    )
    pieces = swap(jnp.broadcast_to(mine, (RING,) + mine.shape))
    columns = lax.all_gather(pieces.reshape(RING * 3 * D, D), "rep", axis=0)
    return pieces, columns.reshape(-1, RING, 3 * D, D)


def shards(
    t_query, t_key, t_value, s_query, s_key, student_value, student_wo, projection,
    doc_ids, span_order, interpret=False,
):
    run = functools.partial(call, interpret=interpret)
    order = span_order[0]
    docs = doc_ids[0]
    start = jnp.sum((docs[None, :] < docs[:, None]).astype(jnp.int32), axis=1)
    first = start[::ROWS]
    start = start[:, None]

    def swap(blocks):
        return lax.all_to_all(blocks, "seq", split_axis=0, concat_axis=0, tiled=True)

    def swap_ring(blocks):
        return lax.all_to_all(
            blocks, "seq", split_axis=0, concat_axis=0, tiled=True, axis_index_groups=RINGS
        )

    pieces, weights = gather_columns(student_wo, projection, swap_ring)
    packed = run(
        pack_kernel,
        bf(GROUPS, TOKENS, 7 * D),
        (s_query, s_key, student_value, t_query, t_key, t_value),
    )
    heads_in = swap(tie(packed, pieces))
    sout, probs = run(
        student_kernel,
        (bf(RING, BOTH, D), bf(BLOCKS, ROWS, SPAN)),
        (order, first, start, heads_in),
        [scratch(LENGTH, D)] + [scratch(LENGTH + LIMIT, D)] * 2 + [scratch(LENGTH, D)],
        scalars=2,
    )
    s_tokens = swap_ring(sout)
    tout = run(
        teacher_kernel,
        bf(RING, BOTH, 2 * D),
        (order, first, start, heads_in),
        [scratch(LENGTH, 2 * D)] + [scratch(LENGTH + LIMIT, D)] * 2 + [scratch(LENGTH, 2 * D)],
        scalars=2,
    )
    t_tokens = swap_ring(tout)
    mine = [terms(s_tokens, t_tokens, weights, half, interpret=interpret) for half in range(2)]
    other = [lax.ppermute(part, "seq", ACROSS) for part in mine]
    grad_a, attn, square = gradients_first(mine[0], other[0], weights, interpret=interpret)
    grad_b, d_attn = gradients_second(
        mine[1], other[1], weights, attn, square, interpret=interpret
    )
    grads = swap_ring(d_attn)
    parts = weight_parts(s_tokens, grad_a, grad_b, interpret=interpret)
    parts = reduce_rep(parts.reshape(-1, RING * D, D))
    back, loss = run(
        backward_kernel,
        (bf(GROUPS, TOKENS, 3 * D), fl(1, D)),
        (order, first, grads, sout, heads_in, probs),
        [scratch(LENGTH, D)] * 3
        + [scratch(LENGTH + LIMIT, D)] * 2
        + [scratch(LENGTH, D)]
        + [scratch(LENGTH + LIMIT, D, jnp.float32)] * 2,
        scalars=2,
    )
    dq, dk, dv = run(
        merge_kernel,
        (bf(TOKENS, GROUPS * D), bf(TOKENS, 4 * D), bf(TOKENS, 4 * D)),
        (swap(back),),
    )
    d_wo = run(sum_kernel, fl(D, D), (swap_ring(parts.reshape(RING, D, D)),))
    return loss[0, :1], d_wo, dq[None], dk[None], dv[None]


def reduce_rep(parts):
    return lax.psum_scatter(parts, "rep", scatter_dimension=0, tiled=True)


def solution(mesh):
    tokens = P("rep", "seq", None)
    in_specs = (tokens,) * 6 + (P("seq", None),) * 2 + (P("rep", None),) * 2
    out_specs = (P("rep"), P("seq", "rep"), tokens, tokens, tokens)
    return jax.shard_map(shards, mesh=mesh, in_specs=in_specs, out_specs=out_specs, check_vma=False)
```

time: 512 us -> 351 us (0.69)
  waiting for transfers between devices: 201 us -> 115 us
  blocking collectives: 183 us -> 126 us
  Pallas kernels: 76.6 us -> 62.3 us
    all_gather x2 -> x1, waiting for transfers between devices: 122 us -> 0.01 us  [gather_columns(): columns = lax.all_gather(pieces.reshape(RING * 3 * D, D), 'rep', axis=0)]
    all_to_all x4 -> x1, blocking collectives: 141 us -> 41.2 us  [swap(): lax.all_to_all(blocks, 'seq', split_axis=0, concat_axis=0, tiled=True)]
    all_to_all x0 -> x3, blocking collectives: none -> 85.3 us  [swap_ring(): lax.all_to_all(blocks, 'seq', split_axis=0, concat_axis=0, tiled=True, ax...]
    all_to_all x3 -> x1, waiting for transfers between devices: 36.4 us -> 78.3 us  [swap(): lax.all_to_all(blocks, 'seq', split_axis=0, concat_axis=0, tiled=True)]
    psum x1 -> x0, blocking collectives: 41.1 us -> none  [shards(): seq_loss = (lax.psum(jnp.sum(squares), 'seq') / (LENGTH * WIDTH)).reshape(1)]
    reduce_scatter x1, waiting for transfers between devices: 43.3 us -> 8.74 us  [reduce_rep(): return lax.psum_scatter(parts, 'rep', scatter_dimension=0, tiled=True)]
    all_to_all x3 -> x1, starting transfers between devices: 24 us -> 4.95 us  [swap(): lax.all_to_all(blocks, 'seq', split_axis=0, concat_axis=0, tiled=True)]
    all_to_all x0 -> x2, starting transfers between devices: none -> 15.9 us  [swap_ring(): lax.all_to_all(blocks, 'seq', split_axis=0, concat_axis=0, tiled=True, ax...]
  transfers between devices with their start and end apart: 6 -> 7, of which waited for: 5 -> 6; matrix products, arithmetic and copies ran while one was open for 1% -> 1% of each run, Pallas kernels for 7% -> 13%
where the time goes in v2:
time: 351 us; the launch traced here: 350 us
  blocking collectives  126 us (36%)
  waiting for transfers between devices  115 us (33%)
  Pallas kernels  62.3 us (18%)
  starting transfers between devices  24.5 us (7%)
  between operations  14.1 us (4%)
  local copies, waits for them, and re-layouts  5.62 us (2%)
    all_to_all x3, blocking collectives, swap_ring(): lax.all_to_all(blocks, 'seq', split_axis=0, concat_axis=0, tiled=True, ax...  85.3 us
    all_to_all x1, waiting for transfers between devices, swap(): lax.all_to_all(blocks, 'seq', split_axis=0, concat_axis=0, tiled=True)  78.3 us
    all_to_all x1, blocking collectives, swap(): lax.all_to_all(blocks, 'seq', split_axis=0, concat_axis=0, tiled=True)  41.2 us
    pallas_call x6, Pallas kernels, call(): pl.pallas_call(kernel, out_shape=outs, in_specs=specs, out_specs=VM if si...  38 us
    all_to_all x2, starting transfers between devices, swap_ring(): lax.all_to_all(blocks, 'seq', split_axis=0, concat_axis=0, tiled=True, ax...  15.9 us
    all_to_all x2, waiting for transfers between devices, swap_ring(): lax.all_to_all(blocks, 'seq', split_axis=0, concat_axis=0, tiled=True, ax...  15.2 us
    ppermute x2, waiting for transfers between devices, shards(): other = [lax.ppermute(part, 'seq', ACROSS) for part in mine]  13 us
    pallas_call x2, Pallas kernels, terms(): pl.pallas_call(terms_kernel, grid=(CHUNK,), out_shape=bf(BOTH, WIDTH // 2...  11.2 us
  transfers between devices with their start and end apart: 7, of which 6 were waited for; matrix products, arithmetic and copies ran while one was open for 1% of the time, Pallas kernels for 13%

profile of v2, /device:TPU:4, one launch (start us, length us, event | category | flops | bytes accessed | tf_op | source)
XLA Modules:
  0.0 350.1 jit_solution(7659376078121761004)
XLA Ops:
  8.6 31.5 %all_to_all.35 = bf16[8,384,128]{2,1,0:T(8,128)(2,1)} all-to-all(bf16[8,384,128]{2,1,0:T(8,128)(2,1)S(1)} %broadcast_in_dim.16), channel_id=1, replica_groups={{0,16,32,48,64,80,96,112},{128,144,160,176,192,208,224,240},{1,17,33,49..., dimensions={0} | all-to-all | bytes 1572864 | tf_op jit(solution)/shard_map/all_to_all | solution.py:428
  40.1 3.8 %pack_kernel.1 = bf16[16,128,896]{2,1,0:T(8,128)(2,1)} custom-call(bf16[1,128,2048]{2,1,0:T(8,128)(2,1)} %sq_ref.1, bf16[1,128,512]{2,1,0:T(8,128)(2,1)} %sk_ref.1, bf16[1,128,512]{2,1,0:T(8,128)(2,1)} %sv_ref.1, bf16[1,128,4096]{2,1,0:T(8,128)(2,1)} %tq_ref.1, bf16[1,128,512]{2,1,0:T(8,128)(2,1)} %tk_ref.1, bf16[1,128,512]{2,1,0:T(8,128)(2,1)} %tv_ref.1), custom_call_target="tpu_custom_call" | custom-call | tf_op jit(solution)/shard_map/pack_kernel/pallas_call | solution.py:311
  43.8 5.0 %all-to-all-start.1 = ((bf16[16,128,896]{2,1,0:T(8,128)(2,1)}), bf16[16,128,896]{2,1,0:T(8,128)(2,1)}, u32[]{:S(2)}, u32[]{:S(2)}) async-start(bf16[16,128,896]{2,1,0:T(8,128)(2,1)} %pack_kernel.1), calls=%async_computation.1 | async-start | bytes 7340032 | tf_op jit(solution)/shard_map/all_to_all | solution.py:425
  52.6 78.3 %all-to-all-done.1.in_ref = bf16[16,128,896]{2,1,0:T(8,128)(2,1)} async-done(((bf16[16,128,896]{2,1,0:T(8,128)(2,1)}), bf16[16,128,896]{2,1,0:T(8,128)(2,1)}, u32[]{:S(2)}, u32[]{:S(2)}) %all-to-all-start.1) | async-done | bytes 3670048 | tf_op jit(solution)/shard_map/all_to_all | solution.py:425
  130.9 9.5 %student_kernel.1 = (bf16[8,256,128]{2,1,0:T(8,128)(2,1)}, bf16[8,256,768]{2,1,0:T(8,128)(2,1)}) custom-call(s32[32]{0:T(128)} %bitcast.20, s32[8]{0:T(128)} %slice.6.first_ref, s32[2048,1]{1,0:T(8,128)} %copy.19.start_ref, bf16[16,128,896]{2,1,0:T(8,128)(2,1)} %all-to-all-done.1.in_ref), custom_call_target="tpu_custom_call" | custom-call | tf_op jit(solution)/shard_map/student_kernel/pallas_call | solution.py:311
  140.4 7.9 %all-to-all-start.2 = ((bf16[8,256,128]{2,1,0:T(8,128)(2,1)}), bf16[8,256,128]{2,1,0:T(8,128)(2,1)S(1)}, u32[]{:S(2)}, u32[]{:S(2)}) async-start(bf16[8,256,128]{2,1,0:T(8,128)(2,1)} %get-tuple-element.19.out_ref), calls=%async_computation.2 | async-start | bytes 1048576 | tf_op jit(solution)/shard_map/all_to_all | solution.py:428
  148.4 10.6 %teacher_kernel.1 = bf16[8,256,256]{2,1,0:T(8,128)(2,1)} custom-call(s32[32]{0:T(128)} %bitcast.21, s32[8]{0:T(128)} %slice.6.first_ref, s32[2048,1]{1,0:T(8,128)} %copy.19.start_ref, bf16[16,128,896]{2,1,0:T(8,128)(2,1)} %all-to-all-done.1.in_ref), custom_call_target="tpu_custom_call" | custom-call | tf_op jit(solution)/shard_map/teacher_kernel/pallas_call | solution.py:311
  159.0 7.1 %all-to-all-done.2.sout_ref = bf16[8,256,128]{2,1,0:T(8,128)(2,1)S(1)} async-done(((bf16[8,256,128]{2,1,0:T(8,128)(2,1)}), bf16[8,256,128]{2,1,0:T(8,128)(2,1)S(1)}, u32[]{:S(2)}, u32[]{:S(2)}) %all-to-all-start.2) | async-done | bytes 524320 | tf_op jit(solution)/shard_map/all_to_all | solution.py:428
  166.1 33.4 %all_to_all.36.tout_ref = bf16[8,256,256]{2,1,0:T(8,128)(2,1)} all-to-all(bf16[8,256,256]{2,1,0:T(8,128)(2,1)} %teacher_kernel.1), channel_id=1, replica_groups={{0,16,32,48,64,80,96,112},{128,144,160,176,192,208,224,240},{1,17,33,49..., dimensions={0} | all-to-all | bytes 2097152 | tf_op jit(solution)/shard_map/all_to_all | solution.py:428
  199.5 5.6 %terms.3.mine_ref = bf16[256,1024]{1,0:T(8,128)(2,1)} custom-call(bf16[8,256,128]{2,1,0:T(8,128)(2,1)} %copy-done.1, bf16[8,256,256]{2,1,0:T(8,128)(2,1)} %all_to_all.36.tout_ref, bf16[16,8,384,128]{3,2,1,0:T(8,128)(2,1)} %bitcast.12), custom_call_target="tpu_custom_call" | custom-call | tf_op jit(solution)/shard_map/terms/pallas_call | solution.py:335
  205.1 5.6 %terms.2.mine_ref = bf16[256,1024]{1,0:T(8,128)(2,1)} custom-call(bf16[8,256,128]{2,1,0:T(8,128)(2,1)} %copy-done.1, bf16[8,256,256]{2,1,0:T(8,128)(2,1)} %all_to_all.36.tout_ref, bf16[16,8,384,128]{3,2,1,0:T(8,128)(2,1)} %bitcast.13), custom_call_target="tpu_custom_call" | custom-call | tf_op jit(solution)/shard_map/terms/pallas_call | solution.py:335
  210.8 3.5 %collective-permute-start = (bf16[256,1024]{1,0:T(8,128)(2,1)}, bf16[256,1024]{1,0:T(8,128)(2,1)S(1)}, u32[]{:S(2)}, u32[]{:S(2)}) collective-permute-start(bf16[256,1024]{1,0:T(8,128)(2,1)} %terms.2.mine_ref), channel_id=1, source_target_pairs={{0,128},{16,144},{32,160},{48,176},{64,192},{80,208},{96,224},{112... | collective-permute-start | bytes 1572872 | tf_op jit(solution)/shard_map/ppermute | solution.py:456
  214.3 7.4 %collective-permute-done.1.other_ref = bf16[256,1024]{1,0:T(8,128)(2,1)S(1)} collective-permute-done((bf16[256,1024]{1,0:T(8,128)(2,1)}, bf16[256,1024]{1,0:T(8,128)(2,1)S(1)}, u32[]{:S(2)}, u32[]{:S(2)}) %collective-permute-start.1) | collective-permute-done | bytes 524320 | tf_op jit(solution)/shard_map/ppermute | solution.py:456
  222.4 3.7 %gradients_first.1 = (bf16[256,1024]{1,0:T(8,128)(2,1)}, f32[1024,256]{1,0:T(8,128)}, f32[1,128]{1,0:T(1,128)}) custom-call(bf16[256,1024]{1,0:T(8,128)(2,1)} %terms.3.mine_ref, bf16[256,1024]{1,0:T(8,128)(2,1)} %copy-done.5, bf16[16,8,384,128]{3,2,1,0:T(8,128)(2,1)} %bitcast.14), custom_call_target="tpu_custom_call" | custom-call | tf_op jit(solution)/shard_map/gradients_first/pallas_call | solution.py:347
  226.1 5.6 %collective-permute-done.other_ref = bf16[256,1024]{1,0:T(8,128)(2,1)S(1)} collective-permute-done((bf16[256,1024]{1,0:T(8,128)(2,1)}, bf16[256,1024]{1,0:T(8,128)(2,1)S(1)}, u32[]{:S(2)}, u32[]{:S(2)}) %collective-permute-start) | collective-permute-done | bytes 524320 | tf_op jit(solution)/shard_map/ppermute | solution.py:456
  232.6 4.1 %gradients_second.1 = (bf16[256,1024]{1,0:T(8,128)(2,1)}, bf16[8,264,128]{2,1,0:T(8,128)(2,1)}) custom-call(bf16[256,1024]{1,0:T(8,128)(2,1)} %terms.2.mine_ref, bf16[256,1024]{1,0:T(8,128)(2,1)} %copy-done.4, bf16[16,8,384,128]{3,2,1,0:T(8,128)(2,1)} %bitcast.15, f32[1024,256]{1,0:T(8,128)} %get-tuple-element.20.attn_in, f32[1,128]{1,0:T(1,128)} %get-tuple-element.21.square_in), custom_call_target="tpu_custom_call" | custom-call | tf_op jit(solution)/shard_map/gradients_second/pallas_call | solution.py:359
  236.6 5.3 %weight_parts.1 = bf16[16,8,128,128]{3,2,1,0:T(8,128)(2,1)} custom-call(bf16[8,256,128]{2,1,0:T(8,128)(2,1)} %copy-done.1, bf16[256,1024]{1,0:T(8,128)(2,1)} %get-tuple-element.25.first_ref, bf16[256,1024]{1,0:T(8,128)(2,1)} %get-tuple-element.26.second_ref), custom_call_target="tpu_custom_call" | custom-call | tf_op jit(solution)/shard_map/weight_parts/pallas_call | solution.py:375
  242.0 20.4 %all_to_all.37.grad_ref = bf16[8,264,128]{2,1,0:T(8,128)(2,1)} all-to-all(bf16[8,264,128]{2,1,0:T(8,128)(2,1)S(1)} %copy-done.3), channel_id=1, replica_groups={{0,16,32,48,64,80,96,112},{128,144,160,176,192,208,224,240},{1,17,33,49..., dimensions={0} | all-to-all | bytes 1081344 | tf_op jit(solution)/shard_map/all_to_all | solution.py:428
  262.4 10.1 %backward_kernel.1 = (bf16[16,128,384]{2,1,0:T(8,128)(2,1)}, f32[1,128]{1,0:T(1,128)}) custom-call(s32[32]{0:T(128)} %bitcast.22, s32[8]{0:T(128)} %slice.6.first_ref, bf16[8,264,128]{2,1,0:T(8,128)(2,1)} %all_to_all.37.grad_ref, bf16[8,256,128]{2,1,0:T(8,128)(2,1)} %get-tuple-element.19.out_ref, bf16[16,128,896]{2,1,0:T(8,128)(2,1)} %all-to-all-done.1.in_ref, ...), custom_call_target="tpu_custom_call" | custom-call | tf_op jit(solution)/shard_map/backward_kernel/pallas_call | solution.py:311
  272.5 41.2 %all_to_all.38.back_ref = bf16[16,128,384]{2,1,0:T(8,128)(2,1)} all-to-all(bf16[16,128,384]{2,1,0:T(8,128)(2,1)} %get-tuple-element.27), channel_id=1, replica_groups=mesh['seq'=16,'rep'=16] {'seq'}, dimensions={0} | all-to-all | bytes 3145728 | tf_op jit(solution)/shard_map/all_to_all | solution.py:425
  313.7 8.7 %reduce-scatter.2.cloned.1.call-done = bf16[1,1024,128]{2,1,0:T(8,128)(2,1)} async-done(((bf16[16,1024,128]{2,1,0:T(8,128)(2,1)}), bf16[1,1024,128]{2,1,0:T(8,128)(2,1)}) %reduce-scatter.2.cloned.1.call-update) | async-done | bytes 262160 | tf_op jit(solution)/shard_map/reduce_scatter | solution.py:484
  322.4 8.0 %all-to-all-start.5 = ((bf16[8,128,128]{2,1,0:T(8,128)(2,1)}), bf16[8,128,128]{2,1,0:T(8,128)(2,1)S(1)}, u32[]{:S(2)}, u32[]{:S(2)}) async-start(bf16[8,128,128]{2,1,0:T(8,128)(2,1)} %bitcast.18), calls=%async_computation.6 | async-start | bytes 524288 | tf_op jit(solution)/shard_map/all_to_all | solution.py:428
  330.4 2.4 merge_kernel.1
  332.9 8.0 %all-to-all-done.5.parts_ref = bf16[8,128,128]{2,1,0:T(8,128)(2,1)S(1)} async-done(((bf16[8,128,128]{2,1,0:T(8,128)(2,1)}), bf16[8,128,128]{2,1,0:T(8,128)(2,1)S(1)}, u32[]{:S(2)}, u32[]{:S(2)}) %all-to-all-start.5) | async-done | bytes 262176 | tf_op jit(solution)/shard_map/all_to_all | solution.py:428
  (28 shorter events, 9.2 us)
Async XLA Ops:
  7.2 1.2 copy-start
  7.2 192.3 %all-gather.2.cloned.1.call-start = ((), (), s32[]{:S(2)}) async-start(), calls=%async_computation.8 | async-start | bytes 13369344 | tf_op jit(solution)/shard_map/all_gather | solution.py:409
  43.8 5.0 %copy-start.6 = (s32[1,2048]{1,0:T(1,128)S(1)}, s32[1,2048]{1,0:T(1,128)}, u32[]{:S(2)}) copy-start(s32[1,2048]{1,0:T(1,128)} %param.18) | copy-start | bytes 24580
  43.8 87.1 %all-to-all-start.1 = ((bf16[16,128,896]{2,1,0:T(8,128)(2,1)}), bf16[16,128,896]{2,1,0:T(8,128)(2,1)}, u32[]{:S(2)}, u32[]{:S(2)}) async-start(bf16[16,128,896]{2,1,0:T(8,128)(2,1)} %pack_kernel.1), calls=%async_computation.1 | async-start | bytes 7340032 | tf_op jit(solution)/shard_map/all_to_all | solution.py:425
  140.4 25.7 %all-to-all-start.2 = ((bf16[8,256,128]{2,1,0:T(8,128)(2,1)}), bf16[8,256,128]{2,1,0:T(8,128)(2,1)S(1)}, u32[]{:S(2)}, u32[]{:S(2)}) async-start(bf16[8,256,128]{2,1,0:T(8,128)(2,1)} %get-tuple-element.19.out_ref), calls=%async_computation.2 | async-start | bytes 1048576 | tf_op jit(solution)/shard_map/all_to_all | solution.py:428
  148.4 174.1 %reduce-scatter.2.cloned.1.call-start = ((), (), s32[]{:S(2)}) async-start(), calls=%async_computation.9 | async-start | bytes 4456448 | tf_op jit(solution)/shard_map/reduce_scatter | solution.py:484
  166.1 33.4 %copy-start.1 = (bf16[8,256,128]{2,1,0:T(8,128)(2,1)}, bf16[8,256,128]{2,1,0:T(8,128)(2,1)S(1)}, u32[]{:S(2)}) copy-start(bf16[8,256,128]{2,1,0:T(8,128)(2,1)S(1)} %all-to-all-done.2.sout_ref) | copy-start | bytes 1572868
  205.1 16.5 %collective-permute-start.1 = (bf16[256,1024]{1,0:T(8,128)(2,1)}, bf16[256,1024]{1,0:T(8,128)(2,1)S(1)}, u32[]{:S(2)}, u32[]{:S(2)}) collective-permute-start(bf16[256,1024]{1,0:T(8,128)(2,1)} %terms.3.mine_ref), channel_id=1, source_target_pairs={{0,128},{16,144},{32,160},{48,176},{64,192},{80,208},{96,224},{112... | collective-permute-start | bytes 1572872 | tf_op jit(solution)/shard_map/ppermute | solution.py:456
  210.8 21.0 %collective-permute-start = (bf16[256,1024]{1,0:T(8,128)(2,1)}, bf16[256,1024]{1,0:T(8,128)(2,1)S(1)}, u32[]{:S(2)}, u32[]{:S(2)}) collective-permute-start(bf16[256,1024]{1,0:T(8,128)(2,1)} %terms.2.mine_ref), channel_id=1, source_target_pairs={{0,128},{16,144},{32,160},{48,176},{64,192},{80,208},{96,224},{112... | collective-permute-start | bytes 1572872 | tf_op jit(solution)/shard_map/ppermute | solution.py:456
  221.6 0.8 copy-start.5
  231.8 0.8 copy-start.4
  236.6 5.3 %copy-start.3 = (bf16[8,264,128]{2,1,0:T(8,128)(2,1)S(1)}, bf16[8,264,128]{2,1,0:T(8,128)(2,1)}, u32[]{:S(2)}) copy-start(bf16[8,264,128]{2,1,0:T(8,128)(2,1)} %get-tuple-element.22) | copy-start | bytes 1622020
  322.4 18.5 %all-to-all-start.5 = ((bf16[8,128,128]{2,1,0:T(8,128)(2,1)}), bf16[8,128,128]{2,1,0:T(8,128)(2,1)S(1)}, u32[]{:S(2)}, u32[]{:S(2)}) async-start(bf16[8,128,128]{2,1,0:T(8,128)(2,1)} %bitcast.18), calls=%async_computation.6 | async-start | bytes 524288 | tf_op jit(solution)/shard_map/all_to_all | solution.py:428
  340.9 0.7 copy-start.2
Sparse Core Ops, SparseCore 0:
  40.2 109.5 all-gather.1
  242.1 80.2 reduce-scatter.1

commit v3 on v2

--- a/solution.py
+++ b/solution.py
@@ -8,10 +8,10 @@
 from jax.experimental.pallas import tpu as pltpu
 from jax.sharding import PartitionSpec as P
 
+
 D = 128
 LENGTH = 2048
 HALF = 64
-SPANS = LENGTH // HALF
 GROUPS = 16
 RING = 8
 PAIR = GROUPS // RING
@@ -19,6 +19,7 @@
 WIDTH = 2048
 BOTH = PAIR * TOKENS
 COLS = 4
+PADDED = 528
 CHUNK = WIDTH // (2 * COLS * D)
 ROWS = 256
 BLOCKS = LENGTH // ROWS
@@ -314,7 +315,6 @@
         in_specs=specs,
         out_specs=VM if single else (VM,) * len(outs),
         scratch_shapes=list(scratches),
-        name=kernel.__name__,
         interpret=interpret,
     )(*ins)
 
@@ -388,26 +388,29 @@
     )(sout, grad_first, grad_second)
 
 
-def tie(value, *after):
-    return lax.optimization_barrier((value,) + after)[0]
-
-
 RINGS = [[ring * RING + place for place in range(RING)] for ring in range(PAIR)]
 ACROSS = [(place, (place + RING) % GROUPS) for place in range(GROUPS)]
 
 
-def gather_columns(student_wo, projection, swap):
+def unpad_kernel(in_ref, out_ref):
+    for place in range(RING):
+        out_ref[place * 3 * D : (place + 1) * 3 * D, :] = in_ref[place, : 3 * D, :]
+
+
+def gather_columns(student_wo, projection, run):
     rep = lax.axis_index("rep")
     mine = jnp.concatenate(
         [
             lax.dynamic_slice_in_dim(student_wo, rep * D, D, 1),
             lax.dynamic_slice_in_dim(projection, rep * D, D, 1),
+            jnp.zeros((PADDED - 3 * D, D), jnp.bfloat16),
         ],
         axis=0,
     )
-    pieces = swap(jnp.broadcast_to(mine, (RING,) + mine.shape))
-    columns = lax.all_gather(pieces.reshape(RING * 3 * D, D), "rep", axis=0)
-    return pieces, columns.reshape(-1, RING, 3 * D, D)
+    pieces = lax.all_gather(mine, "seq", axis=0, axis_index_groups=RINGS)
+    pieces = run(unpad_kernel, bf(RING * 3 * D, D), (pieces,))
+    columns = lax.all_gather(pieces, "rep", axis=0)
+    return columns.reshape(-1, RING, 3 * D, D)
 
 
 def shards(
@@ -429,13 +432,13 @@
             blocks, "seq", split_axis=0, concat_axis=0, tiled=True, axis_index_groups=RINGS
         )
 
-    pieces, weights = gather_columns(student_wo, projection, swap_ring)
+    weights = gather_columns(student_wo, projection, run)
     packed = run(
         pack_kernel,
         bf(GROUPS, TOKENS, 7 * D),
         (s_query, s_key, student_value, t_query, t_key, t_value),
     )
-    heads_in = swap(tie(packed, pieces))
+    heads_in = swap(packed)
     sout, probs = run(
         student_kernel,
         (bf(RING, BOTH, D), bf(BLOCKS, ROWS, SPAN)),

time: 351 us -> 353 us (level)
  waiting for transfers between devices: 115 us -> 153 us
  blocking collectives: 126 us -> 90.1 us
    all_gather x1 -> x2, waiting for transfers between devices: 0.01 us -> 42.3 us  [the longest x1 42.3 us: gather_columns(): pieces = lax.all_gather(mine, 'seq', axis=0, axis_index_groups=RINGS)]
    all_to_all x3 -> x2, blocking collectives: 85.3 us -> 49.8 us  [swap_ring(): lax.all_to_all(blocks, 'seq', split_axis=0, concat_axis=0, tiled=True, ax...]
    reduce_scatter x1, waiting for transfers between devices: 8.74 us -> 13 us  [reduce_rep(): return lax.psum_scatter(parts, 'rep', scatter_dimension=0, tiled=True)]
    all_to_all x2, starting transfers between devices: 15.9 us -> 11.9 us  [swap_ring(): lax.all_to_all(blocks, 'seq', split_axis=0, concat_axis=0, tiled=True, ax...]
    all_to_all x1, waiting for transfers between devices: 78.3 us -> 74.4 us  [swap(): lax.all_to_all(blocks, 'seq', split_axis=0, concat_axis=0, tiled=True)]
    pallas_call x6 -> x7, Pallas kernels: 38 us -> 39.4 us  [call(): pl.pallas_call(kernel, out_shape=outs, in_specs=specs, out_specs=VM if si...]
  transfers between devices with their start and end apart: 7 -> 8, of which waited for: 6 -> 7; matrix products, arithmetic and copies ran while one was open for 1% -> 1% of each run, Pallas kernels for 13% -> 13%
where the time goes in v3:
time: 353 us; the launch traced here: 352 us
  waiting for transfers between devices  153 us (43%)
  blocking collectives  90.1 us (26%)
  Pallas kernels  63.7 us (18%)
  starting transfers between devices  23 us (7%)
  between operations  13.8 us (4%)
  local copies, waits for them, and re-layouts  5.46 us (2%)
    all_to_all x1, waiting for transfers between devices, swap(): lax.all_to_all(blocks, 'seq', split_axis=0, concat_axis=0, tiled=True)  74.4 us
    all_to_all x2, blocking collectives, swap_ring(): lax.all_to_all(blocks, 'seq', split_axis=0, concat_axis=0, tiled=True, ax...  49.8 us
    all_gather x1, waiting for transfers between devices, gather_columns(): pieces = lax.all_gather(mine, 'seq', axis=0, axis_index_groups=RINGS)  42.3 us
    all_to_all x1, blocking collectives, swap(): lax.all_to_all(blocks, 'seq', split_axis=0, concat_axis=0, tiled=True)  40.3 us
    pallas_call x7, Pallas kernels, call(): pl.pallas_call(kernel, out_shape=outs, in_specs=specs, out_specs=VM if si...  39.4 us
    all_to_all x2, waiting for transfers between devices, swap_ring(): lax.all_to_all(blocks, 'seq', split_axis=0, concat_axis=0, tiled=True, ax...  14 us
    reduce_scatter x1, waiting for transfers between devices, reduce_rep(): return lax.psum_scatter(parts, 'rep', scatter_dimension=0, tiled=True)  13 us
    all_to_all x2, starting transfers between devices, swap_ring(): lax.all_to_all(blocks, 'seq', split_axis=0, concat_axis=0, tiled=True, ax...  11.9 us
  transfers between devices with their start and end apart: 8, of which 7 were waited for; matrix products, arithmetic and copies ran while one was open for 1% of the time, Pallas kernels for 13%

profile of v3, /device:TPU:4, one launch (start us, length us, event | category | flops | bytes accessed | tf_op | source)
XLA Modules:
  0.0 352.0 jit_solution(13511494498442415714)
XLA Ops:
  9.3 42.3 %all-gather.5.cloned.1.call-done = bf16[4224,128]{1,0:T(8,128)(2,1)} async-done(((bf16[528,128]{1,0:T(8,128)(2,1)}), bf16[4224,128]{1,0:T(8,128)(2,1)}) %all-gather.5.cloned.1.call-update) | async-done | bytes 1081360 | tf_op jit(solution)/shard_map/all_gather | solution.py:410
  53.8 3.7 %shard_map.137 = bf16[16,128,896]{2,1,0:T(8,128)(2,1)} custom-call(bf16[1,128,2048]{2,1,0:T(8,128)(2,1)} %sq_ref.1, bf16[1,128,512]{2,1,0:T(8,128)(2,1)} %sk_ref.1, bf16[1,128,512]{2,1,0:T(8,128)(2,1)} %sv_ref.1, bf16[1,128,4096]{2,1,0:T(8,128)(2,1)} %tq_ref.1, bf16[1,128,512]{2,1,0:T(8,128)(2,1)} %tk_ref.1, bf16[1,128,512]{2,1,0:T(8,128)(2,1)} %tv_ref.1), custom_call_target="tpu_custom_call" | custom-call | tf_op jit(solution)/shard_map/pallas_call | solution.py:312
  57.6 7.5 %all-to-all-start = ((bf16[16,128,896]{2,1,0:T(8,128)(2,1)}), bf16[16,128,896]{2,1,0:T(8,128)(2,1)}, u32[]{:S(2)}, u32[]{:S(2)}) async-start(bf16[16,128,896]{2,1,0:T(8,128)(2,1)} %shard_map.137), calls=%async_computation | async-start | bytes 7340032 | tf_op jit(solution)/shard_map/all_to_all | solution.py:428
  68.8 74.4 %all-to-all-done.in_ref = bf16[16,128,896]{2,1,0:T(8,128)(2,1)} async-done(((bf16[16,128,896]{2,1,0:T(8,128)(2,1)}), bf16[16,128,896]{2,1,0:T(8,128)(2,1)}, u32[]{:S(2)}, u32[]{:S(2)}) %all-to-all-start) | async-done | bytes 3670048 | tf_op jit(solution)/shard_map/all_to_all | solution.py:428
  143.2 9.3 %shard_map.138 = (bf16[8,256,128]{2,1,0:T(8,128)(2,1)}, bf16[8,256,768]{2,1,0:T(8,128)(2,1)}) custom-call(s32[32]{0:T(128)} %bitcast.20, s32[8]{0:T(128)} %slice.6.first_ref, s32[2048,1]{1,0:T(8,128)} %copy.17.start_ref, bf16[16,128,896]{2,1,0:T(8,128)(2,1)} %all-to-all-done.in_ref), custom_call_target="tpu_custom_call" | custom-call | tf_op jit(solution)/shard_map/pallas_call | solution.py:312
  152.5 4.7 %all-to-all-start.1 = ((bf16[8,256,128]{2,1,0:T(8,128)(2,1)}), bf16[8,256,128]{2,1,0:T(8,128)(2,1)S(1)}, u32[]{:S(2)}, u32[]{:S(2)}) async-start(bf16[8,256,128]{2,1,0:T(8,128)(2,1)} %get-tuple-element.17.out_ref), calls=%async_computation.1 | async-start | bytes 1048576 | tf_op jit(solution)/shard_map/all_to_all | solution.py:431
  157.3 10.3 %shard_map.139 = bf16[8,256,256]{2,1,0:T(8,128)(2,1)} custom-call(s32[32]{0:T(128)} %bitcast.21, s32[8]{0:T(128)} %slice.6.first_ref, s32[2048,1]{1,0:T(8,128)} %copy.17.start_ref, bf16[16,128,896]{2,1,0:T(8,128)(2,1)} %all-to-all-done.in_ref), custom_call_target="tpu_custom_call" | custom-call | tf_op jit(solution)/shard_map/pallas_call | solution.py:312
  167.6 5.9 %all-to-all-done.1.sout_ref = bf16[8,256,128]{2,1,0:T(8,128)(2,1)S(1)} async-done(((bf16[8,256,128]{2,1,0:T(8,128)(2,1)}), bf16[8,256,128]{2,1,0:T(8,128)(2,1)S(1)}, u32[]{:S(2)}, u32[]{:S(2)}) %all-to-all-start.1) | async-done | bytes 524320 | tf_op jit(solution)/shard_map/all_to_all | solution.py:431
  173.5 31.1 %all_to_all.30.tout_ref = bf16[8,256,256]{2,1,0:T(8,128)(2,1)} all-to-all(bf16[8,256,256]{2,1,0:T(8,128)(2,1)} %shard_map.139), channel_id=1, replica_groups={{0,16,32,48,64,80,96,112},{128,144,160,176,192,208,224,240},{1,17,33,49..., dimensions={0} | all-to-all | bytes 2097152 | tf_op jit(solution)/shard_map/all_to_all | solution.py:431
  204.6 5.6 %terms.3.mine_ref = bf16[256,1024]{1,0:T(8,128)(2,1)} custom-call(bf16[8,256,128]{2,1,0:T(8,128)(2,1)} %copy-done.1, bf16[8,256,256]{2,1,0:T(8,128)(2,1)} %all_to_all.30.tout_ref, bf16[16,8,384,128]{3,2,1,0:T(8,128)(2,1)} %bitcast.12), custom_call_target="tpu_custom_call" | custom-call | tf_op jit(solution)/shard_map/terms/pallas_call | solution.py:335
  210.2 5.6 %terms.2.mine_ref = bf16[256,1024]{1,0:T(8,128)(2,1)} custom-call(bf16[8,256,128]{2,1,0:T(8,128)(2,1)} %copy-done.1, bf16[8,256,256]{2,1,0:T(8,128)(2,1)} %all_to_all.30.tout_ref, bf16[16,8,384,128]{3,2,1,0:T(8,128)(2,1)} %bitcast.13), custom_call_target="tpu_custom_call" | custom-call | tf_op jit(solution)/shard_map/terms/pallas_call | solution.py:335
  215.8 3.5 collective-permute-start
  219.4 7.4 %collective-permute-done.1.other_ref = bf16[256,1024]{1,0:T(8,128)(2,1)S(1)} collective-permute-done((bf16[256,1024]{1,0:T(8,128)(2,1)}, bf16[256,1024]{1,0:T(8,128)(2,1)S(1)}, u32[]{:S(2)}, u32[]{:S(2)}) %collective-permute-start.1) | collective-permute-done | bytes 524320 | tf_op jit(solution)/shard_map/ppermute | solution.py:459
  227.5 3.7 %gradients_first.1 = (bf16[256,1024]{1,0:T(8,128)(2,1)}, f32[1024,256]{1,0:T(8,128)}, f32[1,128]{1,0:T(1,128)}) custom-call(bf16[256,1024]{1,0:T(8,128)(2,1)} %terms.3.mine_ref, bf16[256,1024]{1,0:T(8,128)(2,1)} %copy-done.5, bf16[16,8,384,128]{3,2,1,0:T(8,128)(2,1)} %bitcast.14), custom_call_target="tpu_custom_call" | custom-call | tf_op jit(solution)/shard_map/gradients_first/pallas_call | solution.py:347
  231.2 2.2 collective-permute-done.other_ref
  234.2 4.1 %gradients_second.1 = (bf16[256,1024]{1,0:T(8,128)(2,1)}, bf16[8,264,128]{2,1,0:T(8,128)(2,1)}) custom-call(bf16[256,1024]{1,0:T(8,128)(2,1)} %terms.2.mine_ref, bf16[256,1024]{1,0:T(8,128)(2,1)} %copy-done.4, bf16[16,8,384,128]{3,2,1,0:T(8,128)(2,1)} %bitcast.15, f32[1024,256]{1,0:T(8,128)} %get-tuple-element.18.attn_in, f32[1,128]{1,0:T(1,128)} %get-tuple-element.19.square_in), custom_call_target="tpu_custom_call" | custom-call | tf_op jit(solution)/shard_map/gradients_second/pallas_call | solution.py:359
  238.3 5.3 %weight_parts.1 = bf16[16,8,128,128]{3,2,1,0:T(8,128)(2,1)} custom-call(bf16[8,256,128]{2,1,0:T(8,128)(2,1)} %copy-done.1, bf16[256,1024]{1,0:T(8,128)(2,1)} %get-tuple-element.23.first_ref, bf16[256,1024]{1,0:T(8,128)(2,1)} %get-tuple-element.24.second_ref), custom_call_target="tpu_custom_call" | custom-call | tf_op jit(solution)/shard_map/weight_parts/pallas_call | solution.py:375
  243.6 18.7 %all_to_all.31.grad_ref = bf16[8,264,128]{2,1,0:T(8,128)(2,1)} all-to-all(bf16[8,264,128]{2,1,0:T(8,128)(2,1)S(1)} %copy-done.3), channel_id=1, replica_groups={{0,16,32,48,64,80,96,112},{128,144,160,176,192,208,224,240},{1,17,33,49..., dimensions={0} | all-to-all | bytes 1081344 | tf_op jit(solution)/shard_map/all_to_all | solution.py:431
  262.3 9.8 %shard_map.141 = (bf16[16,128,384]{2,1,0:T(8,128)(2,1)}, f32[1,128]{1,0:T(1,128)}) custom-call(s32[32]{0:T(128)} %bitcast.22, s32[8]{0:T(128)} %slice.6.first_ref, bf16[8,264,128]{2,1,0:T(8,128)(2,1)} %all_to_all.31.grad_ref, bf16[8,256,128]{2,1,0:T(8,128)(2,1)} %get-tuple-element.17.out_ref, bf16[16,128,896]{2,1,0:T(8,128)(2,1)} %all-to-all-done.in_ref, ...), custom_call_target="tpu_custom_call" | custom-call | tf_op jit(solution)/shard_map/pallas_call | solution.py:312
  272.2 40.3 %all_to_all.32.back_ref = bf16[16,128,384]{2,1,0:T(8,128)(2,1)} all-to-all(bf16[16,128,384]{2,1,0:T(8,128)(2,1)} %get-tuple-element.25), channel_id=1, replica_groups=mesh['seq'=16,'rep'=16] {'seq'}, dimensions={0} | all-to-all | bytes 3145728 | tf_op jit(solution)/shard_map/all_to_all | solution.py:428
  312.5 13.0 %reduce-scatter.2.cloned.1.call-done = bf16[1,1024,128]{2,1,0:T(8,128)(2,1)} async-done(((bf16[16,1024,128]{2,1,0:T(8,128)(2,1)}), bf16[1,1024,128]{2,1,0:T(8,128)(2,1)}) %reduce-scatter.2.cloned.1.call-update) | async-done | bytes 262160 | tf_op jit(solution)/shard_map/reduce_scatter | solution.py:487
  325.5 7.2 %all-to-all-start.4 = ((bf16[8,128,128]{2,1,0:T(8,128)(2,1)}), bf16[8,128,128]{2,1,0:T(8,128)(2,1)S(1)}, u32[]{:S(2)}, u32[]{:S(2)}) async-start(bf16[8,128,128]{2,1,0:T(8,128)(2,1)} %bitcast.18), calls=%async_computation.5 | async-start | bytes 524288 | tf_op jit(solution)/shard_map/all_to_all | solution.py:431
  332.7 2.4 shard_map.143
  335.1 8.0 %all-to-all-done.4.parts_ref = bf16[8,128,128]{2,1,0:T(8,128)(2,1)S(1)} async-done(((bf16[8,128,128]{2,1,0:T(8,128)(2,1)}), bf16[8,128,128]{2,1,0:T(8,128)(2,1)S(1)}, u32[]{:S(2)}, u32[]{:S(2)}) %all-to-all-start.4) | async-done | bytes 262176 | tf_op jit(solution)/shard_map/all_to_all | solution.py:431
  (32 shorter events, 12.0 us)
Async XLA Ops:
  7.2 1.2 copy-start
  7.2 44.5 %all-gather.5.cloned.1.call-start = ((), (), s32[]{:S(2)}) async-start(), calls=%async_computation.8 | async-start | bytes 1216512 | tf_op jit(solution)/shard_map/all_gather | solution.py:410
  9.3 195.3 %all-gather.7.cloned.1.call-start = ((), (), s32[]{:S(2)}) async-start(), calls=%async_computation.9 | async-start | bytes 13369344 | tf_op jit(solution)/shard_map/all_gather | solution.py:412
  57.6 7.5 %copy-start.6 = (s32[1,2048]{1,0:T(1,128)S(1)}, s32[1,2048]{1,0:T(1,128)}, u32[]{:S(2)}) copy-start(s32[1,2048]{1,0:T(1,128)} %param.18) | copy-start | bytes 24580
  57.6 85.6 %all-to-all-start = ((bf16[16,128,896]{2,1,0:T(8,128)(2,1)}), bf16[16,128,896]{2,1,0:T(8,128)(2,1)}, u32[]{:S(2)}, u32[]{:S(2)}) async-start(bf16[16,128,896]{2,1,0:T(8,128)(2,1)} %shard_map.137), calls=%async_computation | async-start | bytes 7340032 | tf_op jit(solution)/shard_map/all_to_all | solution.py:428
  152.5 21.0 %all-to-all-start.1 = ((bf16[8,256,128]{2,1,0:T(8,128)(2,1)}), bf16[8,256,128]{2,1,0:T(8,128)(2,1)S(1)}, u32[]{:S(2)}, u32[]{:S(2)}) async-start(bf16[8,256,128]{2,1,0:T(8,128)(2,1)} %get-tuple-element.17.out_ref), calls=%async_computation.1 | async-start | bytes 1048576 | tf_op jit(solution)/shard_map/all_to_all | solution.py:431
  157.3 168.2 %reduce-scatter.2.cloned.1.call-start = ((), (), s32[]{:S(2)}) async-start(), calls=%async_computation.7 | async-start | bytes 4456448 | tf_op jit(solution)/shard_map/reduce_scatter | solution.py:487
  173.5 31.1 %copy-start.1 = (bf16[8,256,128]{2,1,0:T(8,128)(2,1)}, bf16[8,256,128]{2,1,0:T(8,128)(2,1)S(1)}, u32[]{:S(2)}) copy-start(bf16[8,256,128]{2,1,0:T(8,128)(2,1)S(1)} %all-to-all-done.1.sout_ref) | copy-start | bytes 1572868
  210.2 16.5 %collective-permute-start.1 = (bf16[256,1024]{1,0:T(8,128)(2,1)}, bf16[256,1024]{1,0:T(8,128)(2,1)S(1)}, u32[]{:S(2)}, u32[]{:S(2)}) collective-permute-start(bf16[256,1024]{1,0:T(8,128)(2,1)} %terms.3.mine_ref), channel_id=1, source_target_pairs={{0,128},{16,144},{32,160},{48,176},{64,192},{80,208},{96,224},{112... | collective-permute-start | bytes 1572872 | tf_op jit(solution)/shard_map/ppermute | solution.py:459
  215.8 17.6 %collective-permute-start = (bf16[256,1024]{1,0:T(8,128)(2,1)}, bf16[256,1024]{1,0:T(8,128)(2,1)S(1)}, u32[]{:S(2)}, u32[]{:S(2)}) collective-permute-start(bf16[256,1024]{1,0:T(8,128)(2,1)} %terms.2.mine_ref), channel_id=1, source_target_pairs={{0,128},{16,144},{32,160},{48,176},{64,192},{80,208},{96,224},{112... | collective-permute-start | bytes 1572872 | tf_op jit(solution)/shard_map/ppermute | solution.py:459
  226.7 0.8 copy-start.5
  233.4 0.8 copy-start.4
  238.3 5.3 %copy-start.3 = (bf16[8,264,128]{2,1,0:T(8,128)(2,1)S(1)}, bf16[8,264,128]{2,1,0:T(8,128)(2,1)}, u32[]{:S(2)}) copy-start(bf16[8,264,128]{2,1,0:T(8,128)(2,1)} %get-tuple-element.20) | copy-start | bytes 1622020
  325.5 17.6 %all-to-all-start.4 = ((bf16[8,128,128]{2,1,0:T(8,128)(2,1)}), bf16[8,128,128]{2,1,0:T(8,128)(2,1)S(1)}, u32[]{:S(2)}, u32[]{:S(2)}) async-start(bf16[8,128,128]{2,1,0:T(8,128)(2,1)} %bitcast.18), calls=%async_computation.5 | async-start | bytes 524288 | tf_op jit(solution)/shard_map/all_to_all | solution.py:431
  343.2 0.7 copy-start.2
Sparse Core Ops, SparseCore 0:
  10.3 41.2 all-gather.4
  54.0 108.3 all-gather.6
  243.7 81.7 reduce-scatter.1

commit v4 on v3

--- a/solution.py
+++ b/solution.py
@@ -20,6 +20,7 @@
 BOTH = PAIR * TOKENS
 COLS = 4
 PADDED = 528
+SIDES = WIDTH // (COLS * D)
 CHUNK = WIDTH // (2 * COLS * D)
 ROWS = 256
 BLOCKS = LENGTH // ROWS
@@ -243,7 +244,7 @@
             attn_ref[group, BOTH:, :] = rows.astype(jnp.bfloat16)
 
 
-def weight_kernel(sout_ref, first_ref, second_ref, part_ref, turned):
+def weight_kernel(place_ref, sout_ref, first_ref, second_ref, keep_ref, send_ref, turned):
     step = pl.program_id(0)
 
     @pl.when(step == 0)
@@ -252,10 +253,46 @@
             turned[group] = sout_ref[group].T
 
     grad = jnp.where(step < CHUNK, first_ref[...], second_ref[...])
+    swapped = place_ref[2] == 1
     for group in range(RING):
-        part = nn(turned[group], grad).astype(jnp.bfloat16)
-        for col in range(COLS):
-            part_ref[col, group] = part[:, col * D : (col + 1) * D]
+        part = nn(turned[group], grad)
+        for side in range(2):
+            low = part[:, 2 * side * D : (2 * side + 1) * D]
+            high = part[:, (2 * side + 1) * D : (2 * side + 2) * D]
+            across = jnp.bitwise_xor(place_ref[1], side)
+            keep_ref[0, across, group] = jnp.where(swapped, high, low).astype(jnp.bfloat16)
+            send_ref[0, across, group] = jnp.where(swapped, low, high).astype(jnp.bfloat16)
+
+
+def plus(*values):
+    total = values[0].astype(jnp.float32)
+    for value in values[1:]:
+        total += value.astype(jnp.float32)
+    return total.astype(jnp.bfloat16)
+
+
+def add_core_kernel(keep_ref, other_ref, *out_refs):
+    for turn, out_ref in enumerate(out_refs):
+        for side in range(2):
+            out_ref[side] = plus(keep_ref[turn, side], other_ref[turn, side])
+
+
+def add_rows_kernel(own_ref, a_ref, b_ref, c_ref, keep_ref, send_ref):
+    for side, out_ref in enumerate((keep_ref, send_ref)):
+        out_ref[...] = plus(own_ref[side], a_ref[side], b_ref[side], c_ref[side])
+
+
+def add_across_kernel(place_ref, own_ref, other_ref, *out_refs):
+    for turn, out_ref in enumerate(out_refs):
+        group = lax.rem(place_ref[3] + turn, RING)
+        out_ref[...] = plus(own_ref[group], other_ref[group])
+
+
+def total_kernel(*refs):
+    total = refs[0][...].astype(jnp.float32)
+    for ref in refs[1:-1]:
+        total += ref[...].astype(jnp.float32)
+    refs[-1][...] = total
 
 
 def merge_kernel(back_ref, dq_ref, dk_ref, dv_ref):
@@ -269,13 +306,6 @@
             for other in range(1, share):
                 summed += back_ref[head * share + other, :, first : first + D].astype(jnp.float32)
             ref[:, cols] = summed.astype(jnp.bfloat16)
-
-
-def sum_kernel(parts_ref, out_ref):
-    total = parts_ref[0].astype(jnp.float32)
-    for group in range(1, RING):
-        total += parts_ref[group].astype(jnp.float32)
-    out_ref[...] = total
 
 
 def pack_kernel(sq_ref, sk_ref, sv_ref, tq_ref, tk_ref, tv_ref, out_ref):
@@ -371,21 +401,49 @@
     )(mine, other, weights, attn, square)
 
 
-def weight_parts(sout, grad_first, grad_second, interpret=False):
+def weight_parts(place, sout, grad_first, grad_second, interpret=False):
+    turned = pl.BlockSpec(
+        (1, 2, RING, D, D), lambda r, at: (lax.rem(r - at[0] + SIDES, SIDES), 0, 0, 0, 0)
+    )
     return pl.pallas_call(
         weight_kernel,
-        grid=(2 * CHUNK,),
-        out_shape=bf(WIDTH // D, RING, D, D),
-        in_specs=[
-            whole(RING, BOTH, D),
-            pl.BlockSpec((BOTH, COLS * D), lambda r: (0, jnp.minimum(r, CHUNK - 1))),
-            pl.BlockSpec((BOTH, COLS * D), lambda r: (0, jnp.maximum(r - CHUNK, 0))),
-        ],
-        out_specs=pl.BlockSpec((COLS, RING, D, D), lambda r: (r, 0, 0, 0)),
-        scratch_shapes=[pltpu.VMEM((RING, D, BOTH), jnp.bfloat16)],
+        grid_spec=pltpu.PrefetchScalarGridSpec(
+            num_scalar_prefetch=1,
+            grid=(SIDES,),
+            in_specs=[
+                pl.BlockSpec((RING, BOTH, D), lambda r, at: (0, 0, 0)),
+                pl.BlockSpec((BOTH, COLS * D), lambda r, at: (0, jnp.minimum(r, CHUNK - 1))),
+                pl.BlockSpec((BOTH, COLS * D), lambda r, at: (0, jnp.maximum(r - CHUNK, 0))),
+            ],
+            out_specs=(turned, turned),
+            scratch_shapes=[pltpu.VMEM((RING, D, BOTH), jnp.bfloat16)],
+        ),
+        out_shape=(bf(SIDES, 2, RING, D, D),) * 2,
         name="weight_parts",
         interpret=interpret,
-    )(sout, grad_first, grad_second)
+    )(place, sout, grad_first, grad_second)
+
+
+def reduce_parts(place, keep, send, run):
+    reps = range(GROUPS)
+    other = lax.ppermute(send, "rep", [(rep, rep ^ 1) for rep in reps])
+    own, *rest = run(add_core_kernel, (bf(2, RING, D, D),) * SIDES, (keep, other))
+    moved = [
+        lax.ppermute(part, "rep", [(rep, (rep + turn * COLS) % GROUPS) for rep in reps])
+        for turn, part in enumerate(rest, 1)
+    ]
+    own, send = run(add_rows_kernel, (bf(RING, D, D),) * 2, (own, *moved))
+    other = lax.ppermute(send, "rep", [(rep, rep ^ 2) for rep in reps])
+    own, *rest = run(add_across_kernel, (bf(D, D),) * RING, (place, own, other), scalars=1)
+    moved = [
+        lax.ppermute(
+            part,
+            "seq",
+            [(at, at // RING * RING + (at + turn) % RING) for at in range(GROUPS)],
+        )
+        for turn, part in enumerate(rest, 1)
+    ]
+    return run(total_kernel, fl(D, D), (own, *moved))
 
 
 RINGS = [[ring * RING + place for place in range(RING)] for ring in range(PAIR)]
@@ -423,6 +481,8 @@
     start = jnp.sum((docs[None, :] < docs[:, None]).astype(jnp.int32), axis=1)
     first = start[::ROWS]
     start = start[:, None]
+    rep = lax.axis_index("rep")
+    place = jnp.stack([rep // 4, (rep // 2) % 2, rep % 2, lax.axis_index("seq") % RING])
 
     def swap(blocks):
         return lax.all_to_all(blocks, "seq", split_axis=0, concat_axis=0, tiled=True)
@@ -462,8 +522,8 @@
         mine[1], other[1], weights, attn, square, interpret=interpret
     )
     grads = swap_ring(d_attn)
-    parts = weight_parts(s_tokens, grad_a, grad_b, interpret=interpret)
-    parts = reduce_rep(parts.reshape(-1, RING * D, D))
+    keep, send = weight_parts(place, s_tokens, grad_a, grad_b, interpret=interpret)
+    d_wo = reduce_parts(place, keep, send, run)
     back, loss = run(
         backward_kernel,
         (bf(GROUPS, TOKENS, 3 * D), fl(1, D)),
@@ -474,17 +534,13 @@
         + [scratch(LENGTH + LIMIT, D, jnp.float32)] * 2,
         scalars=2,
     )
+    back = swap(back)
     dq, dk, dv = run(
         merge_kernel,
         (bf(TOKENS, GROUPS * D), bf(TOKENS, 4 * D), bf(TOKENS, 4 * D)),
-        (swap(back),),
-    )
-    d_wo = run(sum_kernel, fl(D, D), (swap_ring(parts.reshape(RING, D, D)),))
+        (back,),
+    )
     return loss[0, :1], d_wo, dq[None], dk[None], dv[None]
-
-
-def reduce_rep(parts):
-    return lax.psum_scatter(parts, "rep", scatter_dimension=0, tiled=True)
 
 
 def solution(mesh):

time: 353 us -> 346 us (0.980)
  blocking collectives: 90.1 us -> 31.1 us
  starting transfers between devices: 23 us -> 46.9 us
  waiting for transfers between devices: 153 us -> 169 us
  Pallas kernels: 63.7 us -> 72.2 us
    all_to_all x1 -> x0, blocking collectives: 40.3 us -> none  [swap(): lax.all_to_all(blocks, 'seq', split_axis=0, concat_axis=0, tiled=True)]
    ppermute x0 -> x12, waiting for transfers between devices: none -> 28.3 us  [the longest x3 19.1 us: reduce_parts(): lax.ppermute(part, 'rep', [(rep, (rep + turn * COLS) % GROUPS) for rep in...]
    ppermute x0 -> x12, starting transfers between devices: none -> 22.7 us  [the longest x7 16.3 us: reduce_parts(): lax.ppermute(part, 'seq', [(at, at // RING * RING + (at + turn) % RING) f...]
    all_to_all x2 -> x1, blocking collectives: 49.8 us -> 31.1 us  [swap_ring(): lax.all_to_all(blocks, 'seq', split_axis=0, concat_axis=0, tiled=True, ax...]
    reduce_scatter x1 -> x0, waiting for transfers between devices: 13 us -> none  [reduce_rep(): return lax.psum_scatter(parts, 'rep', scatter_dimension=0, tiled=True)]
    pallas_call x7 -> x10, Pallas kernels: 39.4 us -> 47.3 us  [call(): pl.pallas_call(kernel, out_shape=outs, in_specs=specs, out_specs=VM if si...]
    all_to_all x1 -> x2, starting transfers between devices: 7.47 us -> 12.3 us  [swap(): lax.all_to_all(blocks, 'seq', split_axis=0, concat_axis=0, tiled=True)]
    all_to_all x2, starting transfers between devices: 11.9 us -> 8.27 us  [swap_ring(): lax.all_to_all(blocks, 'seq', split_axis=0, concat_axis=0, tiled=True, ax...]
  transfers between devices with their start and end apart: 8 -> 20, of which waited for: 7 -> 11; matrix products, arithmetic and copies ran while one was open for 1% -> 1% of each run, Pallas kernels for 13% -> 17%
where the time goes in v4:
time: 346 us; the launch traced here: 345 us
  waiting for transfers between devices  169 us (49%)
  Pallas kernels  72.2 us (21%)
  starting transfers between devices  46.9 us (14%)
  blocking collectives  31.1 us (9%)
  between operations  14.2 us (4%)
  local copies, waits for them, and re-layouts  8.1 us (2%)
    all_to_all x2, waiting for transfers between devices, swap(): lax.all_to_all(blocks, 'seq', split_axis=0, concat_axis=0, tiled=True)  74.4 us
    pallas_call x10, Pallas kernels, call(): pl.pallas_call(kernel, out_shape=outs, in_specs=specs, out_specs=VM if si...  47.3 us
    all_gather x1, waiting for transfers between devices, gather_columns(): pieces = lax.all_gather(mine, 'seq', axis=0, axis_index_groups=RINGS)  42.3 us
    all_to_all x1, blocking collectives, swap_ring(): lax.all_to_all(blocks, 'seq', split_axis=0, concat_axis=0, tiled=True, ax...  31.1 us
    ppermute x3, waiting for transfers between devices, reduce_parts(): lax.ppermute(part, 'rep', [(rep, (rep + turn * COLS) % GROUPS) for rep in...  19.1 us
    ppermute x7, starting transfers between devices, reduce_parts(): lax.ppermute(part, 'seq', [(at, at // RING * RING + (at + turn) % RING) f...  16.3 us
    all_to_all x2, waiting for transfers between devices, swap_ring(): lax.all_to_all(blocks, 'seq', split_axis=0, concat_axis=0, tiled=True, ax...  14.6 us
    all_to_all x2, starting transfers between devices, swap(): lax.all_to_all(blocks, 'seq', split_axis=0, concat_axis=0, tiled=True)  12.3 us
  transfers between devices with their start and end apart: 20, of which 11 were waited for; matrix products, arithmetic and copies ran while one was open for 1% of the time, Pallas kernels for 17%

profile of v4, /device:TPU:4, one launch (start us, length us, event | category | flops | bytes accessed | tf_op | source)
XLA Modules:
  0.0 344.9 jit_solution(17557539187897946105)
XLA Ops:
  9.3 42.3 %all-gather.5.cloned.1.call-done = bf16[4224,128]{1,0:T(8,128)(2,1)} async-done(((bf16[528,128]{1,0:T(8,128)(2,1)}), bf16[4224,128]{1,0:T(8,128)(2,1)}) %all-gather.5.cloned.1.call-update) | async-done | bytes 1081360 | tf_op jit(solution)/shard_map/all_gather | solution.py:468
  53.9 3.7 %shard_map.137 = bf16[16,128,896]{2,1,0:T(8,128)(2,1)} custom-call(bf16[1,128,2048]{2,1,0:T(8,128)(2,1)} %sq_ref.1, bf16[1,128,512]{2,1,0:T(8,128)(2,1)} %sk_ref.1, bf16[1,128,512]{2,1,0:T(8,128)(2,1)} %sv_ref.1, bf16[1,128,4096]{2,1,0:T(8,128)(2,1)} %tq_ref.1, bf16[1,128,512]{2,1,0:T(8,128)(2,1)} %tk_ref.1, bf16[1,128,512]{2,1,0:T(8,128)(2,1)} %tv_ref.1), custom_call_target="tpu_custom_call" | custom-call | tf_op jit(solution)/shard_map/pallas_call | solution.py:342
  57.6 7.5 %all-to-all-start = ((bf16[16,128,896]{2,1,0:T(8,128)(2,1)}), bf16[16,128,896]{2,1,0:T(8,128)(2,1)}, u32[]{:S(2)}, u32[]{:S(2)}) async-start(bf16[16,128,896]{2,1,0:T(8,128)(2,1)} %shard_map.137), calls=%async_computation | async-start | bytes 7340032 | tf_op jit(solution)/shard_map/all_to_all | solution.py:488
  68.8 74.4 %all-to-all-done.in_ref = bf16[16,128,896]{2,1,0:T(8,128)(2,1)} async-done(((bf16[16,128,896]{2,1,0:T(8,128)(2,1)}), bf16[16,128,896]{2,1,0:T(8,128)(2,1)}, u32[]{:S(2)}, u32[]{:S(2)}) %all-to-all-start) | async-done | bytes 3670048 | tf_op jit(solution)/shard_map/all_to_all | solution.py:488
  143.2 9.3 %shard_map.138 = (bf16[8,256,128]{2,1,0:T(8,128)(2,1)}, bf16[8,256,768]{2,1,0:T(8,128)(2,1)}) custom-call(s32[32]{0:T(128)} %bitcast.20, s32[8]{0:T(128)} %slice.6.first_ref, s32[2048,1]{1,0:T(8,128)} %copy.17.start_ref, bf16[16,128,896]{2,1,0:T(8,128)(2,1)} %all-to-all-done.in_ref), custom_call_target="tpu_custom_call" | custom-call | tf_op jit(solution)/shard_map/pallas_call | solution.py:342
  152.5 4.7 %all-to-all-start.1 = ((bf16[8,256,128]{2,1,0:T(8,128)(2,1)}), bf16[8,256,128]{2,1,0:T(8,128)(2,1)S(1)}, u32[]{:S(2)}, u32[]{:S(2)}) async-start(bf16[8,256,128]{2,1,0:T(8,128)(2,1)} %get-tuple-element.33.out_ref), calls=%async_computation.1 | async-start | bytes 1048576 | tf_op jit(solution)/shard_map/all_to_all | solution.py:491
  157.3 10.3 %shard_map.139 = bf16[8,256,256]{2,1,0:T(8,128)(2,1)} custom-call(s32[32]{0:T(128)} %bitcast.21, s32[8]{0:T(128)} %slice.6.first_ref, s32[2048,1]{1,0:T(8,128)} %copy.17.start_ref, bf16[16,128,896]{2,1,0:T(8,128)(2,1)} %all-to-all-done.in_ref), custom_call_target="tpu_custom_call" | custom-call | tf_op jit(solution)/shard_map/pallas_call | solution.py:342
  167.6 6.0 %all-to-all-done.1.sout_ref = bf16[8,256,128]{2,1,0:T(8,128)(2,1)S(1)} async-done(((bf16[8,256,128]{2,1,0:T(8,128)(2,1)}), bf16[8,256,128]{2,1,0:T(8,128)(2,1)S(1)}, u32[]{:S(2)}, u32[]{:S(2)}) %all-to-all-start.1) | async-done | bytes 524320 | tf_op jit(solution)/shard_map/all_to_all | solution.py:491
  173.5 31.1 %all_to_all.25.tout_ref = bf16[8,256,256]{2,1,0:T(8,128)(2,1)} all-to-all(bf16[8,256,256]{2,1,0:T(8,128)(2,1)} %shard_map.139), channel_id=1, replica_groups={{0,16,32,48,64,80,96,112},{128,144,160,176,192,208,224,240},{1,17,33,49..., dimensions={0} | all-to-all | bytes 2097152 | tf_op jit(solution)/shard_map/all_to_all | solution.py:491
  204.6 5.6 %terms.3.mine_ref = bf16[256,1024]{1,0:T(8,128)(2,1)} custom-call(bf16[8,256,128]{2,1,0:T(8,128)(2,1)} %copy-done.1, bf16[8,256,256]{2,1,0:T(8,128)(2,1)} %all_to_all.25.tout_ref, bf16[16,8,384,128]{3,2,1,0:T(8,128)(2,1)} %bitcast.14), custom_call_target="tpu_custom_call" | custom-call | tf_op jit(solution)/shard_map/terms/pallas_call | solution.py:365
  210.2 5.6 %terms.2.mine_ref = bf16[256,1024]{1,0:T(8,128)(2,1)} custom-call(bf16[8,256,128]{2,1,0:T(8,128)(2,1)} %copy-done.1, bf16[8,256,256]{2,1,0:T(8,128)(2,1)} %all_to_all.25.tout_ref, bf16[16,8,384,128]{3,2,1,0:T(8,128)(2,1)} %bitcast.15), custom_call_target="tpu_custom_call" | custom-call | tf_op jit(solution)/shard_map/terms/pallas_call | solution.py:365
  219.4 7.4 %collective-permute-done.1.other_ref = bf16[256,1024]{1,0:T(8,128)(2,1)S(1)} collective-permute-done((bf16[256,1024]{1,0:T(8,128)(2,1)}, bf16[256,1024]{1,0:T(8,128)(2,1)S(1)}, u32[]{:S(2)}, u32[]{:S(2)}) %collective-permute-start.1) | collective-permute-done | bytes 524320 | tf_op jit(solution)/shard_map/ppermute | solution.py:519
  227.5 3.7 %gradients_first.1 = (bf16[256,1024]{1,0:T(8,128)(2,1)}, f32[1024,256]{1,0:T(8,128)}, f32[1,128]{1,0:T(1,128)}) custom-call(bf16[256,1024]{1,0:T(8,128)(2,1)} %terms.3.mine_ref, bf16[256,1024]{1,0:T(8,128)(2,1)} %copy-done.6, bf16[16,8,384,128]{3,2,1,0:T(8,128)(2,1)} %bitcast.16), custom_call_target="tpu_custom_call" | custom-call | tf_op jit(solution)/shard_map/gradients_first/pallas_call | solution.py:377
  234.2 4.1 %gradients_second.1 = (bf16[256,1024]{1,0:T(8,128)(2,1)}, bf16[8,264,128]{2,1,0:T(8,128)(2,1)}) custom-call(bf16[256,1024]{1,0:T(8,128)(2,1)} %terms.2.mine_ref, bf16[256,1024]{1,0:T(8,128)(2,1)} %copy-done.4, bf16[16,8,384,128]{3,2,1,0:T(8,128)(2,1)} %bitcast.17, f32[1024,256]{1,0:T(8,128)} %get-tuple-element.34.attn_in, f32[1,128]{1,0:T(1,128)} %get-tuple-element.35.square_in), custom_call_target="tpu_custom_call" | custom-call | tf_op jit(solution)/shard_map/gradients_second/pallas_call | solution.py:389
  238.3 3.5 %all-to-all-start.3 = ((bf16[8,264,128]{2,1,0:T(8,128)(2,1)}), bf16[8,264,128]{2,1,0:T(8,128)(2,1)S(1)}, u32[]{:S(2)}, u32[]{:S(2)}) async-start(bf16[8,264,128]{2,1,0:T(8,128)(2,1)} %get-tuple-element.36), calls=%async_computation.3 | async-start | bytes 1081344 | tf_op jit(solution)/shard_map/all_to_all | solution.py:491
  242.5 5.9 %weight_parts.1 = (bf16[4,2,8,128,128]{4,3,2,1,0:T(8,128)(2,1)}, bf16[4,2,8,128,128]{4,3,2,1,0:T(8,128)(2,1)}) custom-call(s32[4]{0:T(128)} %pad_add_fusion.place_ref, bf16[8,256,128]{2,1,0:T(8,128)(2,1)} %copy-done.1, bf16[256,1024]{1,0:T(8,128)(2,1)} %get-tuple-element.39.first_ref, bf16[256,1024]{1,0:T(8,128)(2,1)} %get-tuple-element.40.second_ref), custom_call_target="tpu_custom_call" | custom-call | tf_op jit(solution)/shard_map/weight_parts/pallas_call | solution.py:408
  248.5 8.6 %all-to-all-done.3.grad_ref = bf16[8,264,128]{2,1,0:T(8,128)(2,1)S(1)} async-done(((bf16[8,264,128]{2,1,0:T(8,128)(2,1)}), bf16[8,264,128]{2,1,0:T(8,128)(2,1)S(1)}, u32[]{:S(2)}, u32[]{:S(2)}) %all-to-all-start.3) | async-done | bytes 540704 | tf_op jit(solution)/shard_map/all_to_all | solution.py:491
  258.0 9.8 %shard_map.141 = (bf16[16,128,384]{2,1,0:T(8,128)(2,1)}, f32[1,128]{1,0:T(1,128)}) custom-call(s32[32]{0:T(128)} %bitcast.22, s32[8]{0:T(128)} %slice.6.first_ref, bf16[8,264,128]{2,1,0:T(8,128)(2,1)} %copy-done.3, bf16[8,256,128]{2,1,0:T(8,128)(2,1)} %get-tuple-element.33.out_ref, bf16[16,128,896]{2,1,0:T(8,128)(2,1)} %all-to-all-done.in_ref, ...), custom_call_target="tpu_custom_call" | custom-call | tf_op jit(solution)/shard_map/pallas_call | solution.py:342
  267.8 4.8 %all-to-all-start.4 = ((bf16[16,128,384]{2,1,0:T(8,128)(2,1)}), bf16[16,128,384]{2,1,0:T(8,128)(2,1)S(1)}, u32[]{:S(2)}, u32[]{:S(2)}) async-start(bf16[16,128,384]{2,1,0:T(8,128)(2,1)} %get-tuple-element.57), calls=%async_computation.4 | async-start | bytes 3145728 | tf_op jit(solution)/shard_map/all_to_all | solution.py:488
  272.6 3.7 %shard_map.142 = (bf16[2,8,128,128]{3,2,1,0:T(8,128)(2,1)}, bf16[2,8,128,128]{3,2,1,0:T(8,128)(2,1)}, bf16[2,8,128,128]{3,2,1,0:T(8,128)(2,1)}, bf16[2,8,128,128]{3,2,1,0:T(8,128)(2,1)}) custom-call(bf16[4,2,8,128,128]{4,3,2,1,0:T(8,128)(2,1)} %get-tuple-element.41.keep_ref, bf16[4,2,8,128,128]{4,3,2,1,0:T(8,128)(2,1)} %collective-permute-done.2.other_ref), custom_call_target="tpu_custom_call" | custom-call | tf_op jit(solution)/shard_map/pallas_call | solution.py:342
  281.9 9.5 %collective-permute-done.3.a_ref = bf16[2,8,128,128]{3,2,1,0:T(8,128)(2,1)S(1)} collective-permute-done((bf16[2,8,128,128]{3,2,1,0:T(8,128)(2,1)}, bf16[2,8,128,128]{3,2,1,0:T(8,128)(2,1)S(1)}, u32[]{:S(2)}, u32[]{:S(2)}) %collective-permute-start.3) | collective-permute-done | bytes 524320 | tf_op jit(solution)/shard_map/ppermute | solution.py:432
  291.5 9.5 %collective-permute-done.4.b_ref = bf16[2,8,128,128]{3,2,1,0:T(8,128)(2,1)} collective-permute-done((bf16[2,8,128,128]{3,2,1,0:T(8,128)(2,1)}, bf16[2,8,128,128]{3,2,1,0:T(8,128)(2,1)}, u32[]{:S(2)}, u32[]{:S(2)}) %collective-permute-start.4) | collective-permute-done | bytes 524320 | tf_op jit(solution)/shard_map/ppermute | solution.py:432
  304.2 6.6 %collective-permute-done.6.other_ref = bf16[8,128,128]{2,1,0:T(8,128)(2,1)S(1)} collective-permute-done((bf16[8,128,128]{2,1,0:T(8,128)(2,1)}, bf16[8,128,128]{2,1,0:T(8,128)(2,1)S(1)}, u32[]{:S(2)}, u32[]{:S(2)}) %collective-permute-start.6) | collective-permute-done | bytes 262176 | tf_op jit(solution)/shard_map/ppermute | solution.py:436
  324.6 3.6 %collective-permute-start.12 = (bf16[128,128]{1,0:T(8,128)(2,1)}, bf16[128,128]{1,0:T(8,128)(2,1)S(1)}, u32[]{:S(2)}, u32[]{:S(2)}) collective-permute-start(bf16[128,128]{1,0:T(8,128)(2,1)} %get-tuple-element.55), channel_id=1, source_target_pairs={{0,96},{16,112},{32,0},{48,16},{64,32},{80,48},{96,64},{112,80},{1... | collective-permute-start | bytes 98312 | tf_op jit(solution)/shard_map/ppermute | solution.py:439
  (75 shorter events, 49.3 us)
Async XLA Ops:
  7.2 44.5 %all-gather.5.cloned.1.call-start = ((), (), s32[]{:S(2)}) async-start(), calls=%async_computation.5 | async-start | bytes 1216512 | tf_op jit(solution)/shard_map/all_gather | solution.py:468
  9.3 195.3 %all-gather.7.cloned.1.call-start = ((), (), s32[]{:S(2)}) async-start(), calls=%async_computation.6 | async-start | bytes 13369344 | tf_op jit(solution)/shard_map/all_gather | solution.py:470
  57.6 7.5 %copy-start.15 = (s32[1,2048]{1,0:T(1,128)S(1)}, s32[1,2048]{1,0:T(1,128)}, u32[]{:S(2)}) copy-start(s32[1,2048]{1,0:T(1,128)} %param.18) | copy-start | bytes 24580
  57.6 85.6 %all-to-all-start = ((bf16[16,128,896]{2,1,0:T(8,128)(2,1)}), bf16[16,128,896]{2,1,0:T(8,128)(2,1)}, u32[]{:S(2)}, u32[]{:S(2)}) async-start(bf16[16,128,896]{2,1,0:T(8,128)(2,1)} %shard_map.137), calls=%async_computation | async-start | bytes 7340032 | tf_op jit(solution)/shard_map/all_to_all | solution.py:488
  152.5 21.0 %all-to-all-start.1 = ((bf16[8,256,128]{2,1,0:T(8,128)(2,1)}), bf16[8,256,128]{2,1,0:T(8,128)(2,1)S(1)}, u32[]{:S(2)}, u32[]{:S(2)}) async-start(bf16[8,256,128]{2,1,0:T(8,128)(2,1)} %get-tuple-element.33.out_ref), calls=%async_computation.1 | async-start | bytes 1048576 | tf_op jit(solution)/shard_map/all_to_all | solution.py:491
  173.5 31.1 %copy-start.1 = (bf16[8,256,128]{2,1,0:T(8,128)(2,1)}, bf16[8,256,128]{2,1,0:T(8,128)(2,1)S(1)}, u32[]{:S(2)}) copy-start(bf16[8,256,128]{2,1,0:T(8,128)(2,1)S(1)} %all-to-all-done.1.sout_ref) | copy-start | bytes 1572868
  210.2 16.5 %collective-permute-start.1 = (bf16[256,1024]{1,0:T(8,128)(2,1)}, bf16[256,1024]{1,0:T(8,128)(2,1)S(1)}, u32[]{:S(2)}, u32[]{:S(2)}) collective-permute-start(bf16[256,1024]{1,0:T(8,128)(2,1)} %terms.3.mine_ref), channel_id=1, source_target_pairs={{0,128},{16,144},{32,160},{48,176},{64,192},{80,208},{96,224},{112... | collective-permute-start | bytes 1572872 | tf_op jit(solution)/shard_map/ppermute | solution.py:519
  215.9 17.6 %collective-permute-start = (bf16[256,1024]{1,0:T(8,128)(2,1)}, bf16[256,1024]{1,0:T(8,128)(2,1)S(1)}, u32[]{:S(2)}, u32[]{:S(2)}) collective-permute-start(bf16[256,1024]{1,0:T(8,128)(2,1)} %terms.2.mine_ref), channel_id=1, source_target_pairs={{0,128},{16,144},{32,160},{48,176},{64,192},{80,208},{96,224},{112... | collective-permute-start | bytes 1572872 | tf_op jit(solution)/shard_map/ppermute | solution.py:519
  238.3 18.8 %all-to-all-start.3 = ((bf16[8,264,128]{2,1,0:T(8,128)(2,1)}), bf16[8,264,128]{2,1,0:T(8,128)(2,1)S(1)}, u32[]{:S(2)}, u32[]{:S(2)}) async-start(bf16[8,264,128]{2,1,0:T(8,128)(2,1)} %get-tuple-element.36), calls=%async_computation.3 | async-start | bytes 1081344 | tf_op jit(solution)/shard_map/all_to_all | solution.py:491
  248.5 24.1 %collective-permute-start.2 = (bf16[4,2,8,128,128]{4,3,2,1,0:T(8,128)(2,1)}, bf16[4,2,8,128,128]{4,3,2,1,0:T(8,128)(2,1)}, u32[]{:S(2)}, u32[]{:S(2)}) collective-permute-start(bf16[4,2,8,128,128]{4,3,2,1,0:T(8,128)(2,1)} %get-tuple-element.42), channel_id=1, source_target_pairs={{0,1},{1,0},{2,3},{3,2},{4,5},{5,4},{6,7},{7,6},{8,9},{9,8},{10,11... | collective-permute-start | bytes 6291464 | tf_op jit(solution)/shard_map/ppermute | solution.py:429
  267.8 66.6 %all-to-all-start.4 = ((bf16[16,128,384]{2,1,0:T(8,128)(2,1)}), bf16[16,128,384]{2,1,0:T(8,128)(2,1)S(1)}, u32[]{:S(2)}, u32[]{:S(2)}) async-start(bf16[16,128,384]{2,1,0:T(8,128)(2,1)} %get-tuple-element.57), calls=%async_computation.4 | async-start | bytes 3145728 | tf_op jit(solution)/shard_map/all_to_all | solution.py:488
  276.3 15.2 %collective-permute-start.3 = (bf16[2,8,128,128]{3,2,1,0:T(8,128)(2,1)}, bf16[2,8,128,128]{3,2,1,0:T(8,128)(2,1)S(1)}, u32[]{:S(2)}, u32[]{:S(2)}) collective-permute-start(bf16[2,8,128,128]{3,2,1,0:T(8,128)(2,1)} %get-tuple-element.44), channel_id=1, source_target_pairs={{0,4},{1,5},{2,6},{3,7},{4,8},{5,9},{6,10},{7,11},{8,12},{9,13},{1... | collective-permute-start | bytes 1572872 | tf_op jit(solution)/shard_map/ppermute | solution.py:432
  278.0 23.0 %collective-permute-start.4 = (bf16[2,8,128,128]{3,2,1,0:T(8,128)(2,1)}, bf16[2,8,128,128]{3,2,1,0:T(8,128)(2,1)}, u32[]{:S(2)}, u32[]{:S(2)}) collective-permute-start(bf16[2,8,128,128]{3,2,1,0:T(8,128)(2,1)} %get-tuple-element.45), channel_id=1, source_target_pairs={{0,8},{1,9},{2,10},{3,11},{4,12},{5,13},{6,14},{7,15},{8,0},{9,1},... | collective-permute-start | bytes 1572872 | tf_op jit(solution)/shard_map/ppermute | solution.py:432
  280.8 20.2 %collective-permute-start.5 = (bf16[2,8,128,128]{3,2,1,0:T(8,128)(2,1)}, bf16[2,8,128,128]{3,2,1,0:T(8,128)(2,1)}, u32[]{:S(2)}, u32[]{:S(2)}) collective-permute-start(bf16[2,8,128,128]{3,2,1,0:T(8,128)(2,1)} %get-tuple-element.46), channel_id=1, source_target_pairs={{0,12},{1,13},{2,14},{3,15},{4,0},{5,1},{6,2},{7,3},{8,4},{9,5},{1... | collective-permute-start | bytes 1572872 | tf_op jit(solution)/shard_map/ppermute | solution.py:432
  291.5 9.5 %copy-start.5 = (bf16[2,8,128,128]{3,2,1,0:T(8,128)(2,1)}, bf16[2,8,128,128]{3,2,1,0:T(8,128)(2,1)S(1)}, u32[]{:S(2)}) copy-start(bf16[2,8,128,128]{3,2,1,0:T(8,128)(2,1)S(1)} %collective-permute-done.3.a_ref) | copy-start | bytes 1572868
  303.5 7.3 %collective-permute-start.6 = (bf16[8,128,128]{2,1,0:T(8,128)(2,1)}, bf16[8,128,128]{2,1,0:T(8,128)(2,1)S(1)}, u32[]{:S(2)}, u32[]{:S(2)}) collective-permute-start(bf16[8,128,128]{2,1,0:T(8,128)(2,1)} %get-tuple-element.48), channel_id=1, source_target_pairs={{0,2},{1,3},{2,0},{3,1},{4,6},{5,7},{6,4},{7,5},{8,10},{9,11},{10,... | collective-permute-start | bytes 786440 | tf_op jit(solution)/shard_map/ppermute | solution.py:436
  313.3 11.3 %collective-permute-start.7 = (bf16[128,128]{1,0:T(8,128)(2,1)}, bf16[128,128]{1,0:T(8,128)(2,1)S(1)}, u32[]{:S(2)}, u32[]{:S(2)}) collective-permute-start(bf16[128,128]{1,0:T(8,128)(2,1)} %get-tuple-element.50), channel_id=1, source_target_pairs={{0,16},{16,32},{32,48},{48,64},{64,80},{80,96},{96,112},{112,0},{1... | collective-permute-start | bytes 98312 | tf_op jit(solution)/shard_map/ppermute | solution.py:439
  315.1 13.1 %collective-permute-start.8 = (bf16[128,128]{1,0:T(8,128)(2,1)}, bf16[128,128]{1,0:T(8,128)(2,1)S(1)}, u32[]{:S(2)}, u32[]{:S(2)}) collective-permute-start(bf16[128,128]{1,0:T(8,128)(2,1)} %get-tuple-element.51), channel_id=1, source_target_pairs={{0,32},{16,48},{32,64},{48,80},{64,96},{80,112},{96,0},{112,16},{1... | collective-permute-start | bytes 98312 | tf_op jit(solution)/shard_map/ppermute | solution.py:439
  316.8 12.8 %collective-permute-start.9 = (bf16[128,128]{1,0:T(8,128)(2,1)}, bf16[128,128]{1,0:T(8,128)(2,1)S(1)}, u32[]{:S(2)}, u32[]{:S(2)}) collective-permute-start(bf16[128,128]{1,0:T(8,128)(2,1)} %get-tuple-element.52), channel_id=1, source_target_pairs={{0,48},{16,64},{32,80},{48,96},{64,112},{80,0},{96,16},{112,32},{1... | collective-permute-start | bytes 98312 | tf_op jit(solution)/shard_map/ppermute | solution.py:439
  319.5 10.1 %collective-permute-start.10 = (bf16[128,128]{1,0:T(8,128)(2,1)}, bf16[128,128]{1,0:T(8,128)(2,1)S(1)}, u32[]{:S(2)}, u32[]{:S(2)}) collective-permute-start(bf16[128,128]{1,0:T(8,128)(2,1)} %get-tuple-element.53), channel_id=1, source_target_pairs={{0,64},{16,80},{32,96},{48,112},{64,0},{80,16},{96,32},{112,48},{1... | collective-permute-start | bytes 98312 | tf_op jit(solution)/shard_map/ppermute | solution.py:439
  321.9 7.7 %collective-permute-start.11 = (bf16[128,128]{1,0:T(8,128)(2,1)}, bf16[128,128]{1,0:T(8,128)(2,1)S(1)}, u32[]{:S(2)}, u32[]{:S(2)}) collective-permute-start(bf16[128,128]{1,0:T(8,128)(2,1)} %get-tuple-element.54), channel_id=1, source_target_pairs={{0,80},{16,96},{32,112},{48,0},{64,16},{80,32},{96,48},{112,64},{1... | collective-permute-start | bytes 98312 | tf_op jit(solution)/shard_map/ppermute | solution.py:439
  324.6 7.7 %copy-start.8 = (bf16[128,128]{1,0:T(8,128)(2,1)}, bf16[128,128]{1,0:T(8,128)(2,1)S(1)}, u32[]{:S(2)}) copy-start(bf16[128,128]{1,0:T(8,128)(2,1)S(1)} %collective-permute-done.7.refs_1_) | copy-start | bytes 98308
  324.6 5.5 %collective-permute-start.12 = (bf16[128,128]{1,0:T(8,128)(2,1)}, bf16[128,128]{1,0:T(8,128)(2,1)S(1)}, u32[]{:S(2)}, u32[]{:S(2)}) collective-permute-start(bf16[128,128]{1,0:T(8,128)(2,1)} %get-tuple-element.55), channel_id=1, source_target_pairs={{0,96},{16,112},{32,0},{48,16},{64,32},{80,48},{96,64},{112,80},{1... | collective-permute-start | bytes 98312 | tf_op jit(solution)/shard_map/ppermute | solution.py:439
  328.1 4.1 %collective-permute-start.13 = (bf16[128,128]{1,0:T(8,128)(2,1)}, bf16[128,128]{1,0:T(8,128)(2,1)S(1)}, u32[]{:S(2)}, u32[]{:S(2)}) collective-permute-start(bf16[128,128]{1,0:T(8,128)(2,1)} %get-tuple-element.56), channel_id=1, source_target_pairs={{0,112},{16,0},{32,16},{48,32},{64,48},{80,64},{96,80},{112,96},{1... | collective-permute-start | bytes 98312 | tf_op jit(solution)/shard_map/ppermute | solution.py:439
  (12 other events, 20.6 us)
Sparse Core Ops, SparseCore 0:
  10.3 41.2 all-gather.4
  54.0 108.3 all-gather.6

commit v5 on v4

--- a/solution.py
+++ b/solution.py
@@ -111,9 +111,9 @@
 
 
 def teacher_kernel(order_ref, first_ref, start_ref, in_ref, out_ref, tq, tk, tv, to):
-    spread(order_ref, in_ref, 3 * D, tq, 0, stored_slots)
-    spread(order_ref, in_ref, 5 * D, tk, LIMIT, stored_slots)
-    spread(order_ref, in_ref, 6 * D, tv, LIMIT, stored_slots)
+    spread(order_ref, in_ref, 0, tq, 0, stored_slots)
+    spread(order_ref, in_ref, 2 * D, tk, LIMIT, stored_slots)
+    spread(order_ref, in_ref, 3 * D, tv, LIMIT, stored_slots)
 
     def body(block, width):
         rows, keys, bias = window(start_ref, block, width)
@@ -272,14 +272,24 @@
 
 
 def add_core_kernel(keep_ref, other_ref, *out_refs):
-    for turn, out_ref in enumerate(out_refs):
-        for side in range(2):
-            out_ref[side] = plus(keep_ref[turn, side], other_ref[turn, side])
+    def one(group, carry):
+        for turn, out_ref in enumerate(out_refs):
+            for side in range(2):
+                out_ref[side, group] = plus(
+                    keep_ref[turn, side, group], other_ref[turn, side, group]
+                )
+        return carry
+
+    lax.fori_loop(0, RING, one, 0)
 
 
 def add_rows_kernel(own_ref, a_ref, b_ref, c_ref, keep_ref, send_ref):
-    for side, out_ref in enumerate((keep_ref, send_ref)):
-        out_ref[...] = plus(own_ref[side], a_ref[side], b_ref[side], c_ref[side])
+    def one(group, carry):
+        for side, out_ref in enumerate((keep_ref, send_ref)):
+            out_ref[group] = plus(*(ref[side, group] for ref in (own_ref, a_ref, b_ref, c_ref)))
+        return carry
+
+    lax.fori_loop(0, RING, one, 0)
 
 
 def add_across_kernel(place_ref, own_ref, other_ref, *out_refs):
@@ -308,16 +318,16 @@
             ref[:, cols] = summed.astype(jnp.bfloat16)
 
 
-def pack_kernel(sq_ref, sk_ref, sv_ref, tq_ref, tk_ref, tv_ref, out_ref):
+def pack_kernel(sq_ref, sk_ref, sv_ref, tq_ref, tk_ref, tv_ref, s_ref, t_ref):
     share = GROUPS // 4
     for group in range(GROUPS):
         key = slice((group // share) * D, (group // share + 1) * D)
-        out_ref[group, :, :D] = sq_ref[0, :, group * D : (group + 1) * D]
-        out_ref[group, :, D : 2 * D] = sk_ref[0, :, key]
-        out_ref[group, :, 2 * D : 3 * D] = sv_ref[0, :, key]
-        out_ref[group, :, 3 * D : 5 * D] = tq_ref[0, :, 2 * group * D : 2 * (group + 1) * D]
-        out_ref[group, :, 5 * D : 6 * D] = tk_ref[0, :, key]
-        out_ref[group, :, 6 * D :] = tv_ref[0, :, key]
+        s_ref[group, :, :D] = sq_ref[0, :, group * D : (group + 1) * D]
+        s_ref[group, :, D : 2 * D] = sk_ref[0, :, key]
+        s_ref[group, :, 2 * D :] = sv_ref[0, :, key]
+        t_ref[group, :, : 2 * D] = tq_ref[0, :, 2 * group * D : 2 * (group + 1) * D]
+        t_ref[group, :, 2 * D : 3 * D] = tk_ref[0, :, key]
+        t_ref[group, :, 3 * D :] = tv_ref[0, :, key]
 
 
 VM = pl.BlockSpec(memory_space=pltpu.VMEM)
@@ -428,10 +438,11 @@
     reps = range(GROUPS)
     other = lax.ppermute(send, "rep", [(rep, rep ^ 1) for rep in reps])
     own, *rest = run(add_core_kernel, (bf(2, RING, D, D),) * SIDES, (keep, other))
-    moved = [
-        lax.ppermute(part, "rep", [(rep, (rep + turn * COLS) % GROUPS) for rep in reps])
-        for turn, part in enumerate(rest, 1)
-    ]
+    moved = []
+    for turn, part in enumerate(rest, 1):
+        moved.append(
+            lax.ppermute(part, "rep", [(rep, (rep + turn * COLS) % GROUPS) for rep in reps])
+        )
     own, send = run(add_rows_kernel, (bf(RING, D, D),) * 2, (own, *moved))
     other = lax.ppermute(send, "rep", [(rep, rep ^ 2) for rep in reps])
     own, *rest = run(add_across_kernel, (bf(D, D),) * RING, (place, own, other), scalars=1)
@@ -446,6 +457,10 @@
     return run(total_kernel, fl(D, D), (own, *moved))
 
 
+def tie(value, *after):
+    return lax.optimization_barrier((value,) + after)[0]
+
+
 RINGS = [[ring * RING + place for place in range(RING)] for ring in range(PAIR)]
 ACROSS = [(place, (place + RING) % GROUPS) for place in range(GROUPS)]
 
@@ -493,24 +508,25 @@
         )
 
     weights = gather_columns(student_wo, projection, run)
-    packed = run(
+    s_pack, t_pack = run(
         pack_kernel,
-        bf(GROUPS, TOKENS, 7 * D),
+        (bf(GROUPS, TOKENS, 3 * D), bf(GROUPS, TOKENS, 4 * D)),
         (s_query, s_key, student_value, t_query, t_key, t_value),
     )
-    heads_in = swap(packed)
+    s_in = swap(s_pack)
+    t_in = swap(tie(t_pack, s_in))
     sout, probs = run(
         student_kernel,
         (bf(RING, BOTH, D), bf(BLOCKS, ROWS, SPAN)),
-        (order, first, start, heads_in),
+        (order, first, start, s_in),
         [scratch(LENGTH, D)] + [scratch(LENGTH + LIMIT, D)] * 2 + [scratch(LENGTH, D)],
         scalars=2,
     )
-    s_tokens = swap_ring(sout)
+    s_tokens = swap_ring(tie(sout, t_in))
     tout = run(
         teacher_kernel,
         bf(RING, BOTH, 2 * D),
-        (order, first, start, heads_in),
+        (order, first, start, t_in),
         [scratch(LENGTH, 2 * D)] + [scratch(LENGTH + LIMIT, D)] * 2 + [scratch(LENGTH, 2 * D)],
         scalars=2,
     )
@@ -527,7 +543,7 @@
     back, loss = run(
         backward_kernel,
         (bf(GROUPS, TOKENS, 3 * D), fl(1, D)),
-        (order, first, grads, sout, heads_in, probs),
+        (order, first, grads, sout, s_in, probs),
         [scratch(LENGTH, D)] * 3
         + [scratch(LENGTH + LIMIT, D)] * 2
         + [scratch(LENGTH, D)]

time: 346 us -> 340 us (0.983)
  waiting for transfers between devices: 169 us -> 124 us
  blocking collectives: 31.1 us -> 69.8 us
    all_to_all x2, waiting for transfers between devices: 74.4 us -> 32 us  [swap(): lax.all_to_all(blocks, 'seq', split_axis=0, concat_axis=0, tiled=True)]
    all_to_all x0 -> x1, blocking collectives: none -> 40 us  [swap(): lax.all_to_all(blocks, 'seq', split_axis=0, concat_axis=0, tiled=True)]
where the time goes in v5:
time: 340 us; the launch traced here: 338 us
  waiting for transfers between devices  124 us (36%)
  Pallas kernels  71 us (21%)
  blocking collectives  69.8 us (21%)
  starting transfers between devices  46.5 us (14%)
  between operations  14.2 us (4%)
  local copies, waits for them, and re-layouts  9.43 us (3%)
    pallas_call x10, Pallas kernels, call(): pl.pallas_call(kernel, out_shape=outs, in_specs=specs, out_specs=VM if si...  46 us
    all_gather x1, waiting for transfers between devices, gather_columns(): pieces = lax.all_gather(mine, 'seq', axis=0, axis_index_groups=RINGS)  42.3 us
    all_to_all x1, blocking collectives, swap(): lax.all_to_all(blocks, 'seq', split_axis=0, concat_axis=0, tiled=True)  40 us
    all_to_all x2, waiting for transfers between devices, swap(): lax.all_to_all(blocks, 'seq', split_axis=0, concat_axis=0, tiled=True)  32 us
    all_to_all x1, blocking collectives, swap_ring(): lax.all_to_all(blocks, 'seq', split_axis=0, concat_axis=0, tiled=True, ax...  29.8 us
    ppermute x3, waiting for transfers between devices, reduce_parts(): lax.ppermute(part, 'rep', [(rep, (rep + turn * COLS) % GROUPS) for rep in...  19 us
    ppermute x7, starting transfers between devices, reduce_parts(): lax.ppermute(part, 'seq', [(at, at // RING * RING + (at + turn) % RING) f...  15.6 us
    all_to_all x2, waiting for transfers between devices, swap_ring(): lax.all_to_all(blocks, 'seq', split_axis=0, concat_axis=0, tiled=True, ax...  13 us
  transfers between devices with their start and end apart: 20, of which 11 were waited for; matrix products, arithmetic and copies ran while one was open for 1% of the time, Pallas kernels for 17%

profile of v5, /device:TPU:4, one launch (start us, length us, event | category | flops | bytes accessed | tf_op | source)
XLA Modules:
  0.0 338.3 jit_solution(13305986848509978784)
XLA Ops:
  9.3 42.3 %all-gather.5.cloned.1.call-done = bf16[4224,128]{1,0:T(8,128)(2,1)} async-done(((bf16[528,128]{1,0:T(8,128)(2,1)}), bf16[4224,128]{1,0:T(8,128)(2,1)}) %all-gather.5.cloned.1.call-update) | async-done | bytes 1081360 | tf_op jit(solution)/shard_map/all_gather | solution.py:483
  53.9 3.8 %shard_map.137 = (bf16[16,128,384]{2,1,0:T(8,128)(2,1)}, bf16[16,128,512]{2,1,0:T(8,128)(2,1)}) custom-call(bf16[1,128,2048]{2,1,0:T(8,128)(2,1)} %sq_ref.1, bf16[1,128,512]{2,1,0:T(8,128)(2,1)} %sk_ref.1, bf16[1,128,512]{2,1,0:T(8,128)(2,1)} %sv_ref.1, bf16[1,128,4096]{2,1,0:T(8,128)(2,1)} %tq_ref.1, bf16[1,128,512]{2,1,0:T(8,128)(2,1)} %tk_ref.1, ...), custom_call_target="tpu_custom_call" | custom-call | tf_op jit(solution)/shard_map/pallas_call | solution.py:352
  57.7 40.0 %all_to_all.30.in_ref = bf16[16,128,384]{2,1,0:T(8,128)(2,1)} all-to-all(bf16[16,128,384]{2,1,0:T(8,128)(2,1)} %get-tuple-element.37), channel_id=1, replica_groups=mesh['seq'=16,'rep'=16] {'seq'}, dimensions={0} | all-to-all | bytes 3145728 | tf_op jit(solution)/shard_map/all_to_all | solution.py:503
  97.7 7.3 %all-to-all-start.1 = ((bf16[16,128,512]{2,1,0:T(8,128)(2,1)}), bf16[16,128,512]{2,1,0:T(8,128)(2,1)S(1)}, u32[]{:S(2)}, u32[]{:S(2)}) async-start(bf16[16,128,512]{2,1,0:T(8,128)(2,1)} %get-tuple-element.40), calls=%async_computation.1 | async-start | bytes 4194304 | tf_op jit(solution)/shard_map/all_to_all | solution.py:503
  108.7 8.7 %shard_map.138 = (bf16[8,256,128]{2,1,0:T(8,128)(2,1)}, bf16[8,256,768]{2,1,0:T(8,128)(2,1)}) custom-call(s32[32]{0:T(128)} %bitcast.20, s32[8]{0:T(128)} %slice.6.first_ref, s32[2048,1]{1,0:T(8,128)} %copy.17.start_ref, bf16[16,128,384]{2,1,0:T(8,128)(2,1)} %all_to_all.30.in_ref), custom_call_target="tpu_custom_call" | custom-call | tf_op jit(solution)/shard_map/pallas_call | solution.py:352
  117.4 32.0 %all-to-all-done.1.in_ref = bf16[16,128,512]{2,1,0:T(8,128)(2,1)S(1)} async-done(((bf16[16,128,512]{2,1,0:T(8,128)(2,1)}), bf16[16,128,512]{2,1,0:T(8,128)(2,1)S(1)}, u32[]{:S(2)}, u32[]{:S(2)}) %all-to-all-start.1) | async-done | bytes 2097184 | tf_op jit(solution)/shard_map/all_to_all | solution.py:503
  150.8 4.2 %all-to-all-start.2 = ((bf16[8,256,128]{2,1,0:T(8,128)(2,1)}), bf16[8,256,128]{2,1,0:T(8,128)(2,1)S(1)}, u32[]{:S(2)}, u32[]{:S(2)}) async-start(bf16[8,256,128]{2,1,0:T(8,128)(2,1)} %get-tuple-element.41.out_ref), calls=%async_computation.2 | async-start | bytes 1048576 | tf_op jit(solution)/shard_map/all_to_all | solution.py:506
  155.0 9.8 %shard_map.139 = bf16[8,256,256]{2,1,0:T(8,128)(2,1)} custom-call(s32[32]{0:T(128)} %bitcast.21, s32[8]{0:T(128)} %slice.6.first_ref, s32[2048,1]{1,0:T(8,128)} %copy.17.start_ref, bf16[16,128,512]{2,1,0:T(8,128)(2,1)} %copy-done.2), custom_call_target="tpu_custom_call" | custom-call | tf_op jit(solution)/shard_map/pallas_call | solution.py:352
  164.8 5.5 %all-to-all-done.2.sout_ref = bf16[8,256,128]{2,1,0:T(8,128)(2,1)S(1)} async-done(((bf16[8,256,128]{2,1,0:T(8,128)(2,1)}), bf16[8,256,128]{2,1,0:T(8,128)(2,1)S(1)}, u32[]{:S(2)}, u32[]{:S(2)}) %all-to-all-start.2) | async-done | bytes 524320 | tf_op jit(solution)/shard_map/all_to_all | solution.py:506
  170.2 29.8 %all_to_all.31.tout_ref = bf16[8,256,256]{2,1,0:T(8,128)(2,1)} all-to-all(bf16[8,256,256]{2,1,0:T(8,128)(2,1)} %shard_map.139), channel_id=1, replica_groups={{0,16,32,48,64,80,96,112},{128,144,160,176,192,208,224,240},{1,17,33,49..., dimensions={0} | all-to-all | bytes 2097152 | tf_op jit(solution)/shard_map/all_to_all | solution.py:506
  200.0 5.7 %terms.3.mine_ref = bf16[256,1024]{1,0:T(8,128)(2,1)} custom-call(bf16[8,256,128]{2,1,0:T(8,128)(2,1)} %copy-done.1, bf16[8,256,256]{2,1,0:T(8,128)(2,1)} %all_to_all.31.tout_ref, bf16[16,8,384,128]{3,2,1,0:T(8,128)(2,1)} %bitcast.14), custom_call_target="tpu_custom_call" | custom-call | tf_op jit(solution)/shard_map/terms/pallas_call | solution.py:375
  205.7 5.6 %terms.2.mine_ref = bf16[256,1024]{1,0:T(8,128)(2,1)} custom-call(bf16[8,256,128]{2,1,0:T(8,128)(2,1)} %copy-done.1, bf16[8,256,256]{2,1,0:T(8,128)(2,1)} %all_to_all.31.tout_ref, bf16[16,8,384,128]{3,2,1,0:T(8,128)(2,1)} %bitcast.15), custom_call_target="tpu_custom_call" | custom-call | tf_op jit(solution)/shard_map/terms/pallas_call | solution.py:375
  214.8 7.1 %collective-permute-done.1.other_ref = bf16[256,1024]{1,0:T(8,128)(2,1)S(1)} collective-permute-done((bf16[256,1024]{1,0:T(8,128)(2,1)}, bf16[256,1024]{1,0:T(8,128)(2,1)S(1)}, u32[]{:S(2)}, u32[]{:S(2)}) %collective-permute-start.1) | collective-permute-done | bytes 524320 | tf_op jit(solution)/shard_map/ppermute | solution.py:535
  222.8 3.7 %gradients_first.1 = (bf16[256,1024]{1,0:T(8,128)(2,1)}, f32[1024,256]{1,0:T(8,128)}, f32[1,128]{1,0:T(1,128)}) custom-call(bf16[256,1024]{1,0:T(8,128)(2,1)} %terms.3.mine_ref, bf16[256,1024]{1,0:T(8,128)(2,1)} %copy-done.7, bf16[16,8,384,128]{3,2,1,0:T(8,128)(2,1)} %bitcast.16), custom_call_target="tpu_custom_call" | custom-call | tf_op jit(solution)/shard_map/gradients_first/pallas_call | solution.py:387
  228.4 4.1 %gradients_second.1 = (bf16[256,1024]{1,0:T(8,128)(2,1)}, bf16[8,264,128]{2,1,0:T(8,128)(2,1)}) custom-call(bf16[256,1024]{1,0:T(8,128)(2,1)} %terms.2.mine_ref, bf16[256,1024]{1,0:T(8,128)(2,1)} %copy-done.5, bf16[16,8,384,128]{3,2,1,0:T(8,128)(2,1)} %bitcast.17, f32[1024,256]{1,0:T(8,128)} %get-tuple-element.42.attn_in, f32[1,128]{1,0:T(1,128)} %get-tuple-element.43.square_in), custom_call_target="tpu_custom_call" | custom-call | tf_op jit(solution)/shard_map/gradients_second/pallas_call | solution.py:399
  232.5 3.5 %all-to-all-start.4 = ((bf16[8,264,128]{2,1,0:T(8,128)(2,1)}), bf16[8,264,128]{2,1,0:T(8,128)(2,1)S(1)}, u32[]{:S(2)}, u32[]{:S(2)}) async-start(bf16[8,264,128]{2,1,0:T(8,128)(2,1)} %get-tuple-element.44), calls=%async_computation.4 | async-start | bytes 1081344 | tf_op jit(solution)/shard_map/all_to_all | solution.py:506
  236.7 5.9 %weight_parts.1 = (bf16[4,2,8,128,128]{4,3,2,1,0:T(8,128)(2,1)}, bf16[4,2,8,128,128]{4,3,2,1,0:T(8,128)(2,1)}) custom-call(s32[4]{0:T(128)} %pad_add_fusion.place_ref, bf16[8,256,128]{2,1,0:T(8,128)(2,1)} %copy-done.1, bf16[256,1024]{1,0:T(8,128)(2,1)} %get-tuple-element.47.first_ref, bf16[256,1024]{1,0:T(8,128)(2,1)} %get-tuple-element.48.second_ref), custom_call_target="tpu_custom_call" | custom-call | tf_op jit(solution)/shard_map/weight_parts/pallas_call | solution.py:418
  242.6 7.5 %all-to-all-done.4.grad_ref = bf16[8,264,128]{2,1,0:T(8,128)(2,1)S(1)} async-done(((bf16[8,264,128]{2,1,0:T(8,128)(2,1)}), bf16[8,264,128]{2,1,0:T(8,128)(2,1)S(1)}, u32[]{:S(2)}, u32[]{:S(2)}) %all-to-all-start.4) | async-done | bytes 540704 | tf_op jit(solution)/shard_map/all_to_all | solution.py:506
  250.9 9.2 %shard_map.141 = (bf16[16,128,384]{2,1,0:T(8,128)(2,1)}, f32[1,128]{1,0:T(1,128)}) custom-call(s32[32]{0:T(128)} %bitcast.22, s32[8]{0:T(128)} %slice.6.first_ref, bf16[8,264,128]{2,1,0:T(8,128)(2,1)} %copy-done.4, bf16[8,256,128]{2,1,0:T(8,128)(2,1)} %get-tuple-element.41.out_ref, bf16[16,128,384]{2,1,0:T(8,128)(2,1)} %all_to_all.30.in_ref, ...), custom_call_target="tpu_custom_call" | custom-call | tf_op jit(solution)/shard_map/pallas_call | solution.py:352
  260.1 5.1 %all-to-all-start.5 = ((bf16[16,128,384]{2,1,0:T(8,128)(2,1)}), bf16[16,128,384]{2,1,0:T(8,128)(2,1)S(1)}, u32[]{:S(2)}, u32[]{:S(2)}) async-start(bf16[16,128,384]{2,1,0:T(8,128)(2,1)} %get-tuple-element.65), calls=%async_computation.5 | async-start | bytes 3145728 | tf_op jit(solution)/shard_map/all_to_all | solution.py:503
  265.3 4.0 %shard_map.142 = (bf16[2,8,128,128]{3,2,1,0:T(8,128)(2,1)}, bf16[2,8,128,128]{3,2,1,0:T(8,128)(2,1)}, bf16[2,8,128,128]{3,2,1,0:T(8,128)(2,1)}, bf16[2,8,128,128]{3,2,1,0:T(8,128)(2,1)}) custom-call(bf16[4,2,8,128,128]{4,3,2,1,0:T(8,128)(2,1)} %get-tuple-element.49.keep_ref, bf16[4,2,8,128,128]{4,3,2,1,0:T(8,128)(2,1)} %collective-permute-done.2.other_ref), custom_call_target="tpu_custom_call" | custom-call | tf_op jit(solution)/shard_map/pallas_call | solution.py:352
  275.6 8.7 %collective-permute-done.3.a_ref = bf16[2,8,128,128]{3,2,1,0:T(8,128)(2,1)S(1)} collective-permute-done((bf16[2,8,128,128]{3,2,1,0:T(8,128)(2,1)}, bf16[2,8,128,128]{3,2,1,0:T(8,128)(2,1)S(1)}, u32[]{:S(2)}, u32[]{:S(2)}) %collective-permute-start.3) | collective-permute-done | bytes 524320 | tf_op jit(solution)/shard_map/ppermute | solution.py:444
  284.3 10.3 %collective-permute-done.4.b_ref = bf16[2,8,128,128]{3,2,1,0:T(8,128)(2,1)} collective-permute-done((bf16[2,8,128,128]{3,2,1,0:T(8,128)(2,1)}, bf16[2,8,128,128]{3,2,1,0:T(8,128)(2,1)}, u32[]{:S(2)}, u32[]{:S(2)}) %collective-permute-start.4) | collective-permute-done | bytes 524320 | tf_op jit(solution)/shard_map/ppermute | solution.py:444
  298.1 6.9 %collective-permute-done.6.other_ref = bf16[8,128,128]{2,1,0:T(8,128)(2,1)S(1)} collective-permute-done((bf16[8,128,128]{2,1,0:T(8,128)(2,1)}, bf16[8,128,128]{2,1,0:T(8,128)(2,1)S(1)}, u32[]{:S(2)}, u32[]{:S(2)}) %collective-permute-start.6) | collective-permute-done | bytes 262176 | tf_op jit(solution)/shard_map/ppermute | solution.py:447
  (78 shorter events, 53.4 us)
Async XLA Ops:
  7.2 44.5 %all-gather.5.cloned.1.call-start = ((), (), s32[]{:S(2)}) async-start(), calls=%async_computation.6 | async-start | bytes 1216512 | tf_op jit(solution)/shard_map/all_gather | solution.py:483
  9.3 190.7 %all-gather.7.cloned.1.call-start = ((), (), s32[]{:S(2)}) async-start(), calls=%async_computation.7 | async-start | bytes 13369344 | tf_op jit(solution)/shard_map/all_gather | solution.py:485
  97.7 7.3 %copy-start.16 = (s32[1,2048]{1,0:T(1,128)S(1)}, s32[1,2048]{1,0:T(1,128)}, u32[]{:S(2)}) copy-start(s32[1,2048]{1,0:T(1,128)} %param.18) | copy-start | bytes 24580
  97.7 51.7 %all-to-all-start.1 = ((bf16[16,128,512]{2,1,0:T(8,128)(2,1)}), bf16[16,128,512]{2,1,0:T(8,128)(2,1)S(1)}, u32[]{:S(2)}, u32[]{:S(2)}) async-start(bf16[16,128,512]{2,1,0:T(8,128)(2,1)} %get-tuple-element.40), calls=%async_computation.1 | async-start | bytes 4194304 | tf_op jit(solution)/shard_map/all_to_all | solution.py:503
  150.8 19.4 %all-to-all-start.2 = ((bf16[8,256,128]{2,1,0:T(8,128)(2,1)}), bf16[8,256,128]{2,1,0:T(8,128)(2,1)S(1)}, u32[]{:S(2)}, u32[]{:S(2)}) async-start(bf16[8,256,128]{2,1,0:T(8,128)(2,1)} %get-tuple-element.41.out_ref), calls=%async_computation.2 | async-start | bytes 1048576 | tf_op jit(solution)/shard_map/all_to_all | solution.py:506
  170.2 29.8 %copy-start.1 = (bf16[8,256,128]{2,1,0:T(8,128)(2,1)}, bf16[8,256,128]{2,1,0:T(8,128)(2,1)S(1)}, u32[]{:S(2)}) copy-start(bf16[8,256,128]{2,1,0:T(8,128)(2,1)S(1)} %all-to-all-done.2.sout_ref) | copy-start | bytes 1572868
  205.7 16.3 %collective-permute-start.1 = (bf16[256,1024]{1,0:T(8,128)(2,1)}, bf16[256,1024]{1,0:T(8,128)(2,1)S(1)}, u32[]{:S(2)}, u32[]{:S(2)}) collective-permute-start(bf16[256,1024]{1,0:T(8,128)(2,1)} %terms.3.mine_ref), channel_id=1, source_target_pairs={{0,128},{16,144},{32,160},{48,176},{64,192},{80,208},{96,224},{112... | collective-permute-start | bytes 1572872 | tf_op jit(solution)/shard_map/ppermute | solution.py:535
  211.3 16.3 %collective-permute-start = (bf16[256,1024]{1,0:T(8,128)(2,1)}, bf16[256,1024]{1,0:T(8,128)(2,1)S(1)}, u32[]{:S(2)}, u32[]{:S(2)}) collective-permute-start(bf16[256,1024]{1,0:T(8,128)(2,1)} %terms.2.mine_ref), channel_id=1, source_target_pairs={{0,128},{16,144},{32,160},{48,176},{64,192},{80,208},{96,224},{112... | collective-permute-start | bytes 1572872 | tf_op jit(solution)/shard_map/ppermute | solution.py:535
  232.5 17.7 %all-to-all-start.4 = ((bf16[8,264,128]{2,1,0:T(8,128)(2,1)}), bf16[8,264,128]{2,1,0:T(8,128)(2,1)S(1)}, u32[]{:S(2)}, u32[]{:S(2)}) async-start(bf16[8,264,128]{2,1,0:T(8,128)(2,1)} %get-tuple-element.44), calls=%async_computation.4 | async-start | bytes 1081344 | tf_op jit(solution)/shard_map/all_to_all | solution.py:506
  242.6 22.7 %collective-permute-start.2 = (bf16[4,2,8,128,128]{4,3,2,1,0:T(8,128)(2,1)}, bf16[4,2,8,128,128]{4,3,2,1,0:T(8,128)(2,1)}, u32[]{:S(2)}, u32[]{:S(2)}) collective-permute-start(bf16[4,2,8,128,128]{4,3,2,1,0:T(8,128)(2,1)} %get-tuple-element.50), channel_id=1, source_target_pairs={{0,1},{1,0},{2,3},{3,2},{4,5},{5,4},{6,7},{7,6},{8,9},{9,8},{10,11... | collective-permute-start | bytes 6291464 | tf_op jit(solution)/shard_map/ppermute | solution.py:439
  260.1 67.7 %all-to-all-start.5 = ((bf16[16,128,384]{2,1,0:T(8,128)(2,1)}), bf16[16,128,384]{2,1,0:T(8,128)(2,1)S(1)}, u32[]{:S(2)}, u32[]{:S(2)}) async-start(bf16[16,128,384]{2,1,0:T(8,128)(2,1)} %get-tuple-element.65), calls=%async_computation.5 | async-start | bytes 3145728 | tf_op jit(solution)/shard_map/all_to_all | solution.py:503
  269.3 15.0 %collective-permute-start.3 = (bf16[2,8,128,128]{3,2,1,0:T(8,128)(2,1)}, bf16[2,8,128,128]{3,2,1,0:T(8,128)(2,1)S(1)}, u32[]{:S(2)}, u32[]{:S(2)}) collective-permute-start(bf16[2,8,128,128]{3,2,1,0:T(8,128)(2,1)} %get-tuple-element.52), channel_id=1, source_target_pairs={{0,4},{1,5},{2,6},{3,7},{4,8},{5,9},{6,10},{7,11},{8,12},{9,13},{1... | collective-permute-start | bytes 1572872 | tf_op jit(solution)/shard_map/ppermute | solution.py:444
  271.5 23.1 %collective-permute-start.4 = (bf16[2,8,128,128]{3,2,1,0:T(8,128)(2,1)}, bf16[2,8,128,128]{3,2,1,0:T(8,128)(2,1)}, u32[]{:S(2)}, u32[]{:S(2)}) collective-permute-start(bf16[2,8,128,128]{3,2,1,0:T(8,128)(2,1)} %get-tuple-element.53), channel_id=1, source_target_pairs={{0,8},{1,9},{2,10},{3,11},{4,12},{5,13},{6,14},{7,15},{8,0},{9,1},... | collective-permute-start | bytes 1572872 | tf_op jit(solution)/shard_map/ppermute | solution.py:444
  273.6 20.9 %collective-permute-start.5 = (bf16[2,8,128,128]{3,2,1,0:T(8,128)(2,1)}, bf16[2,8,128,128]{3,2,1,0:T(8,128)(2,1)}, u32[]{:S(2)}, u32[]{:S(2)}) collective-permute-start(bf16[2,8,128,128]{3,2,1,0:T(8,128)(2,1)} %get-tuple-element.54), channel_id=1, source_target_pairs={{0,12},{1,13},{2,14},{3,15},{4,0},{5,1},{6,2},{7,3},{8,4},{9,5},{1... | collective-permute-start | bytes 1572872 | tf_op jit(solution)/shard_map/ppermute | solution.py:444
  284.3 10.3 %copy-start.6 = (bf16[2,8,128,128]{3,2,1,0:T(8,128)(2,1)}, bf16[2,8,128,128]{3,2,1,0:T(8,128)(2,1)S(1)}, u32[]{:S(2)}) copy-start(bf16[2,8,128,128]{3,2,1,0:T(8,128)(2,1)S(1)} %collective-permute-done.3.a_ref) | copy-start | bytes 1572868
  297.1 7.9 %collective-permute-start.6 = (bf16[8,128,128]{2,1,0:T(8,128)(2,1)}, bf16[8,128,128]{2,1,0:T(8,128)(2,1)S(1)}, u32[]{:S(2)}, u32[]{:S(2)}) collective-permute-start(bf16[8,128,128]{2,1,0:T(8,128)(2,1)} %get-tuple-element.56), channel_id=1, source_target_pairs={{0,2},{1,3},{2,0},{3,1},{4,6},{5,7},{6,4},{7,5},{8,10},{9,11},{10,... | collective-permute-start | bytes 786440 | tf_op jit(solution)/shard_map/ppermute | solution.py:447
  307.5 11.3 %collective-permute-start.7 = (bf16[128,128]{1,0:T(8,128)(2,1)}, bf16[128,128]{1,0:T(8,128)(2,1)S(1)}, u32[]{:S(2)}, u32[]{:S(2)}) collective-permute-start(bf16[128,128]{1,0:T(8,128)(2,1)} %get-tuple-element.58), channel_id=1, source_target_pairs={{0,16},{16,32},{32,48},{48,64},{64,80},{80,96},{96,112},{112,0},{1... | collective-permute-start | bytes 98312 | tf_op jit(solution)/shard_map/ppermute | solution.py:450
  308.9 12.6 %collective-permute-start.8 = (bf16[128,128]{1,0:T(8,128)(2,1)}, bf16[128,128]{1,0:T(8,128)(2,1)S(1)}, u32[]{:S(2)}, u32[]{:S(2)}) collective-permute-start(bf16[128,128]{1,0:T(8,128)(2,1)} %get-tuple-element.59), channel_id=1, source_target_pairs={{0,32},{16,48},{32,64},{48,80},{64,96},{80,112},{96,0},{112,16},{1... | collective-permute-start | bytes 98312 | tf_op jit(solution)/shard_map/ppermute | solution.py:450
  310.3 12.8 %collective-permute-start.9 = (bf16[128,128]{1,0:T(8,128)(2,1)}, bf16[128,128]{1,0:T(8,128)(2,1)S(1)}, u32[]{:S(2)}, u32[]{:S(2)}) collective-permute-start(bf16[128,128]{1,0:T(8,128)(2,1)} %get-tuple-element.60), channel_id=1, source_target_pairs={{0,48},{16,64},{32,80},{48,96},{64,112},{80,0},{96,16},{112,32},{1... | collective-permute-start | bytes 98312 | tf_op jit(solution)/shard_map/ppermute | solution.py:450
  313.1 9.9 %collective-permute-start.10 = (bf16[128,128]{1,0:T(8,128)(2,1)}, bf16[128,128]{1,0:T(8,128)(2,1)S(1)}, u32[]{:S(2)}, u32[]{:S(2)}) collective-permute-start(bf16[128,128]{1,0:T(8,128)(2,1)} %get-tuple-element.61), channel_id=1, source_target_pairs={{0,64},{16,80},{32,96},{48,112},{64,0},{80,16},{96,32},{112,48},{1... | collective-permute-start | bytes 98312 | tf_op jit(solution)/shard_map/ppermute | solution.py:450
  315.3 7.7 %collective-permute-start.11 = (bf16[128,128]{1,0:T(8,128)(2,1)}, bf16[128,128]{1,0:T(8,128)(2,1)S(1)}, u32[]{:S(2)}, u32[]{:S(2)}) collective-permute-start(bf16[128,128]{1,0:T(8,128)(2,1)} %get-tuple-element.62), channel_id=1, source_target_pairs={{0,80},{16,96},{32,112},{48,0},{64,16},{80,32},{96,48},{112,64},{1... | collective-permute-start | bytes 98312 | tf_op jit(solution)/shard_map/ppermute | solution.py:450
  318.8 6.9 %copy-start.9 = (bf16[128,128]{1,0:T(8,128)(2,1)}, bf16[128,128]{1,0:T(8,128)(2,1)S(1)}, u32[]{:S(2)}) copy-start(bf16[128,128]{1,0:T(8,128)(2,1)S(1)} %collective-permute-done.7.refs_1_) | copy-start | bytes 98308
  318.8 5.6 %collective-permute-start.12 = (bf16[128,128]{1,0:T(8,128)(2,1)}, bf16[128,128]{1,0:T(8,128)(2,1)S(1)}, u32[]{:S(2)}, u32[]{:S(2)}) collective-permute-start(bf16[128,128]{1,0:T(8,128)(2,1)} %get-tuple-element.63), channel_id=1, source_target_pairs={{0,96},{16,112},{32,0},{48,16},{64,32},{80,48},{96,64},{112,80},{1... | collective-permute-start | bytes 98312 | tf_op jit(solution)/shard_map/ppermute | solution.py:450
  321.6 4.1 %collective-permute-start.13 = (bf16[128,128]{1,0:T(8,128)(2,1)}, bf16[128,128]{1,0:T(8,128)(2,1)S(1)}, u32[]{:S(2)}, u32[]{:S(2)}) collective-permute-start(bf16[128,128]{1,0:T(8,128)(2,1)} %get-tuple-element.64), channel_id=1, source_target_pairs={{0,112},{16,0},{32,16},{48,32},{64,48},{80,64},{96,80},{112,96},{1... | collective-permute-start | bytes 98312 | tf_op jit(solution)/shard_map/ppermute | solution.py:450
  (13 other events, 21.0 us)
Sparse Core Ops, SparseCore 0:
  10.3 41.2 all-gather.4
  54.0 110.0 all-gather.6

commit v6 on v5

--- a/solution.py
+++ b/solution.py
@@ -19,15 +19,14 @@
 WIDTH = 2048
 BOTH = PAIR * TOKENS
 COLS = 4
-PADDED = 528
 SIDES = WIDTH // (COLS * D)
 CHUNK = WIDTH // (2 * COLS * D)
+HALF_COLS = COLS * CHUNK
 ROWS = 256
 BLOCKS = LENGTH // ROWS
 STEP = 128
 LIMIT = 512
 SPAN = LIMIT + ROWS
-STEPS = LIMIT // STEP + 1
 SCALE = 1.0 / math.sqrt(D)
 LOG2E = math.log2(math.e)
 FAR = -1e30
@@ -45,19 +44,15 @@
     return lax.dot_general(a, b, (((0,), (0,)), ((), ())), preferred_element_type=jnp.float32)
 
 
-def key_steps(first_ref, block):
-    return jnp.clip((block * ROWS - first_ref[block] + STEP - 1) // STEP, 0, STEPS - 1)
-
-
-def each_window(first_ref, body):
+def each_window(first_ref, body, step):
     def one(block, carry):
-        needed = key_steps(first_ref, block)
-        for extra in range(STEPS):
-            width = ROWS + extra * STEP
+        needed = (block * ROWS - first_ref[block] + step - 1) // step
+        needed = jnp.clip(needed, 0, LIMIT // step)
+        for extra in range(LIMIT // step + 1):
 
             @pl.when(needed == extra)
             def _():
-                body(block, width)
+                body(block, ROWS + extra * step)
 
         return carry
 
@@ -124,7 +119,7 @@
             weights, totals = weights_of(tq[rows, cols], key_rows, bias)
             to[rows, cols] = (nn(weights.astype(jnp.bfloat16), val_rows) / -totals).astype(jnp.bfloat16)
 
-    each_window(first_ref, body)
+    each_window(first_ref, body, 2 * STEP)
     put_back(order_ref, to, out_ref, slice(0, 2 * D), ring_slots)
 
 
@@ -140,7 +135,7 @@
         probs_ref[block, :, SPAN - width :] = probs
         so[rows, :] = nn(probs, sv[keys, :]).astype(jnp.bfloat16)
 
-    each_window(first_ref, body)
+    each_window(first_ref, body, 2 * STEP)
     put_back(order_ref, so, out_ref, slice(0, D), ring_slots)
 
 
@@ -173,78 +168,70 @@
         dk[keys, :] += tn(d_scores, sq[rows, :])
         dv[keys, :] += tn(probs, grads)
 
-    each_window(first_ref, body)
+    each_window(first_ref, body, STEP)
     put_back(order_ref, dq, back_ref, slice(0, D), stored_slots)
     put_back(order_ref, dk, back_ref, slice(D, 2 * D), stored_slots, LIMIT, SCALE)
     put_back(order_ref, dv, back_ref, slice(2 * D, 3 * D), stored_slots, LIMIT, 1.0)
 
 
-def side_by_side(w_ref, group, rows):
-    return jnp.concatenate([w_ref[col, group, :rows, :] for col in range(COLS)], axis=1)
-
-
-def terms_kernel(sout_ref, tout_ref, w_ref, part_ref):
-    total = None
-    for group in range(RING):
-        both = jnp.concatenate([sout_ref[group], tout_ref[group]], axis=1)
-        term = nn(both, side_by_side(w_ref, group, 3 * D))
-        term = term.astype(jnp.bfloat16).astype(jnp.float32)
-        total = term if total is None else total + term
-    part_ref[...] = total.astype(jnp.bfloat16)
-
-
-def gradient_step(mine_ref, other_ref, w_ref, grad_ref):
-    diff = mine_ref[...].astype(jnp.float32) + other_ref[...].astype(jnp.float32)
-    grad = diff.astype(jnp.bfloat16)
-    grad_ref[...] = grad
-    square = jnp.sum(diff * diff, axis=0, keepdims=True)
-    square = sum(square[:, col * D : (col + 1) * D] for col in range(COLS))
-    wo = jnp.concatenate([side_by_side(w_ref, group, D) for group in range(RING)], axis=0)
-    return nt(wo, grad), square
-
-
-def first_kernel(mine_ref, other_ref, w_ref, grad_ref, attn_ref, square_ref):
-    part, square = gradient_step(mine_ref, other_ref, w_ref, grad_ref)
+def side_by_side(refs, rows):
+    return jnp.concatenate([ref[side, 0, :rows, :] for ref in refs for side in range(2)], axis=1)
+
+
+def terms_kernel(sout_ref, tout_ref, a_ref, b_ref, c_ref, d_ref, part_ref, total):
+    both = jnp.concatenate([sout_ref[0], tout_ref[0]], axis=1)
+    term = nn(both, side_by_side((a_ref, b_ref, c_ref, d_ref), 3 * D))
+    term = term.astype(jnp.bfloat16).astype(jnp.float32)
 
     @pl.when(pl.program_id(0) == 0)
     def _():
-        attn_ref[...] = part
-        square_ref[...] = square
+        total[...] = term
 
     @pl.when(pl.program_id(0) > 0)
     def _():
-        attn_ref[...] += part
-        square_ref[...] += square
-
-
-def second_kernel(mine_ref, other_ref, w_ref, attn_in, square_in, grad_ref, attn_ref, attn, squares):
-    part, square = gradient_step(mine_ref, other_ref, w_ref, grad_ref)
-    step = pl.program_id(0)
-
-    @pl.when(step == 0)
+        total[...] += term
+
+    @pl.when(pl.program_id(0) == RING - 1)
     def _():
-        attn[...] = attn_in[...] + part
-        squares[...] = square_in[...] + square
-
-    @pl.when(step > 0)
+        part_ref[...] = total[...].astype(jnp.bfloat16)
+
+
+def gradient_once(mine_ref, other_ref, grad_ref, square_ref):
+    diff = mine_ref[...].astype(jnp.float32) + other_ref[...].astype(jnp.float32)
+    grad_ref[...] = diff.astype(jnp.bfloat16)
+    square = jnp.sum(diff * diff, axis=0, keepdims=True)
+    square_ref[...] = sum(square[:, col * D : (col + 1) * D] for col in range(HALF_COLS))
+
+
+def first_kernel(
+    mine_ref, other_ref, a_ref, b_ref, c_ref, d_ref, grad_ref, attn_ref, square_ref
+):
+    @pl.when(pl.program_id(0) == 0)
     def _():
-        attn[...] += part
-        squares[...] += square
-
-    @pl.when(step == pl.num_programs(0) - 1)
+        gradient_once(mine_ref, other_ref, grad_ref, square_ref)
+
+    attn_ref[0] = nt(side_by_side((a_ref, b_ref, c_ref, d_ref), D), grad_ref[...])
+
+
+def second_kernel(
+    mine_ref, other_ref, a_ref, b_ref, c_ref, d_ref, attn_in, square_in, grad_ref, attn_ref,
+    squares,
+):
+    @pl.when(pl.program_id(0) == 0)
     def _():
-        for group in range(RING):
-            block = attn[group * D : (group + 1) * D, :]
-            attn_ref[group, :BOTH, :] = block.T.astype(jnp.bfloat16)
-        total = squares[...]
-        high = total.astype(jnp.bfloat16).astype(jnp.float32)
-        line = lax.broadcasted_iota(jnp.int32, (8, D), 0)
-        rows = jnp.where(line == 0, high, jnp.where(line == 1, total - high, 0.0))
-        for group in range(RING):
-            attn_ref[group, BOTH:, :] = rows.astype(jnp.bfloat16)
-
-
-def weight_kernel(place_ref, sout_ref, first_ref, second_ref, keep_ref, send_ref, turned):
+        gradient_once(mine_ref, other_ref, grad_ref, squares)
+        squares[...] += square_in[...]
+
+    part = nt(side_by_side((a_ref, b_ref, c_ref, d_ref), D), grad_ref[...]) + attn_in[0]
+    attn_ref[0, :BOTH, :] = part.T.astype(jnp.bfloat16)
+    total = squares[...]
+    high = total.astype(jnp.bfloat16).astype(jnp.float32)
+    line = lax.broadcasted_iota(jnp.int32, (8, D), 0)
+    rows = jnp.where(line == 0, high, jnp.where(line == 1, total - high, 0.0))
+    attn_ref[0, BOTH:, :] = rows.astype(jnp.bfloat16)
+
+
+def weight_kernel(sout_ref, first_ref, second_ref, keep_ref, send_ref, turned):
     step = pl.program_id(0)
 
     @pl.when(step == 0)
@@ -253,15 +240,33 @@
             turned[group] = sout_ref[group].T
 
     grad = jnp.where(step < CHUNK, first_ref[...], second_ref[...])
-    swapped = place_ref[2] == 1
-    for group in range(RING):
-        part = nn(turned[group], grad)
-        for side in range(2):
-            low = part[:, 2 * side * D : (2 * side + 1) * D]
-            high = part[:, (2 * side + 1) * D : (2 * side + 2) * D]
-            across = jnp.bitwise_xor(place_ref[1], side)
-            keep_ref[0, across, group] = jnp.where(swapped, high, low).astype(jnp.bfloat16)
-            send_ref[0, across, group] = jnp.where(swapped, low, high).astype(jnp.bfloat16)
+
+    def one(pair, carry):
+        for half in range(2):
+            group = 2 * pair + half
+            part = nn(turned[group], grad).astype(jnp.bfloat16)
+            for side in range(2):
+                keep_ref[0, side, group] = part[:, side * D : (side + 1) * D]
+                send_ref[0, side, group] = part[:, (2 + side) * D : (3 + side) * D]
+        return carry
+
+    lax.fori_loop(0, RING // 2, one, 0)
+
+
+def gather_kernel(place_ref, own_ref, *refs):
+    out_ref = refs[-1]
+    out_ref[place_ref[0]] = own_ref[...]
+    for turn, ref in enumerate(refs[:-1], 1):
+        out_ref[lax.rem(place_ref[0] - turn + RING, RING)] = ref[...]
+
+
+def join_kernel(own_ref, other_ref, out_ref):
+    def one(group, carry):
+        out_ref[0, group] = own_ref[group]
+        out_ref[1, group] = other_ref[group]
+        return carry
+
+    lax.fori_loop(0, RING, one, 0)
 
 
 def plus(*values):
@@ -294,7 +299,7 @@
 
 def add_across_kernel(place_ref, own_ref, other_ref, *out_refs):
     for turn, out_ref in enumerate(out_refs):
-        group = lax.rem(place_ref[3] + turn, RING)
+        group = lax.rem(place_ref[0] + turn, RING)
         out_ref[...] = plus(own_ref[group], other_ref[group])
 
 
@@ -320,14 +325,22 @@
 
 def pack_kernel(sq_ref, sk_ref, sv_ref, tq_ref, tk_ref, tv_ref, s_ref, t_ref):
     share = GROUPS // 4
-    for group in range(GROUPS):
-        key = slice((group // share) * D, (group // share + 1) * D)
-        s_ref[group, :, :D] = sq_ref[0, :, group * D : (group + 1) * D]
-        s_ref[group, :, D : 2 * D] = sk_ref[0, :, key]
-        s_ref[group, :, 2 * D :] = sv_ref[0, :, key]
-        t_ref[group, :, : 2 * D] = tq_ref[0, :, 2 * group * D : 2 * (group + 1) * D]
-        t_ref[group, :, 2 * D : 3 * D] = tk_ref[0, :, key]
-        t_ref[group, :, 3 * D :] = tv_ref[0, :, key]
+
+    def one(head, carry):
+        key = pl.ds(pl.multiple_of(head * D, D), D)
+        for member in range(share):
+            group = head * share + member
+            start = pl.multiple_of(group * D, D)
+            s_ref[group, :, :D] = sq_ref[0, :, pl.ds(start, D)]
+            s_ref[group, :, D : 2 * D] = sk_ref[0, :, key]
+            s_ref[group, :, 2 * D :] = sv_ref[0, :, key]
+            start = pl.multiple_of(2 * group * D, 2 * D)
+            t_ref[group, :, : 2 * D] = tq_ref[0, :, pl.ds(start, 2 * D)]
+            t_ref[group, :, 2 * D : 3 * D] = tk_ref[0, :, key]
+            t_ref[group, :, 3 * D :] = tv_ref[0, :, key]
+        return carry
+
+    lax.fori_loop(0, 4, one, 0)
 
 
 VM = pl.BlockSpec(memory_space=pltpu.VMEM)
@@ -363,75 +376,70 @@
     return pl.BlockSpec(shape, lambda r: (0,) * len(shape))
 
 
-def by_columns(rows):
-    return pl.BlockSpec((rows, COLS * D), lambda r: (0, r))
-
-
-def weight_block(rows, half):
-    return pl.BlockSpec((COLS, RING, rows, D), lambda r: (r + half * CHUNK, 0, 0, 0))
-
-
-def terms(sout, tout, weights, half, interpret=False):
+def by_group(*shape):
+    return pl.BlockSpec((1,) + shape, lambda g: (g,) + (0,) * len(shape))
+
+
+def weight_blocks(rows):
+    return [pl.BlockSpec((2, 1, rows, D), lambda g: (0, g, 0, 0))] * 4
+
+
+def terms(sout, tout, weights, interpret=False):
     return pl.pallas_call(
         terms_kernel,
-        grid=(CHUNK,),
+        grid=(RING,),
         out_shape=bf(BOTH, WIDTH // 2),
-        in_specs=[whole(RING, BOTH, D), whole(RING, BOTH, 2 * D), weight_block(3 * D, half)],
-        out_specs=by_columns(BOTH),
+        in_specs=[by_group(BOTH, D), by_group(BOTH, 2 * D)] + weight_blocks(3 * D),
+        out_specs=whole(BOTH, WIDTH // 2),
+        scratch_shapes=[scratch(BOTH, WIDTH // 2, jnp.float32)],
         name="terms",
         interpret=interpret,
-    )(sout, tout, weights)
+    )(sout, tout, *weights)
 
 
 def gradients_first(mine, other, weights, interpret=False):
+    half = whole(BOTH, WIDTH // 2)
     return pl.pallas_call(
         first_kernel,
-        grid=(CHUNK,),
-        out_shape=(bf(BOTH, WIDTH // 2), fl(RING * D, BOTH), fl(1, D)),
-        in_specs=[by_columns(BOTH), by_columns(BOTH), weight_block(D, 0)],
-        out_specs=(by_columns(BOTH), whole(RING * D, BOTH), whole(1, D)),
+        grid=(RING,),
+        out_shape=(bf(BOTH, WIDTH // 2), fl(RING, D, BOTH), fl(1, D)),
+        in_specs=[half, half] + weight_blocks(D),
+        out_specs=(half, by_group(D, BOTH), whole(1, D)),
         name="gradients_first",
         interpret=interpret,
-    )(mine, other, weights)
+    )(mine, other, *weights)
 
 
 def gradients_second(mine, other, weights, attn, square, interpret=False):
+    half = whole(BOTH, WIDTH // 2)
     return pl.pallas_call(
         second_kernel,
-        grid=(CHUNK,),
+        grid=(RING,),
         out_shape=(bf(BOTH, WIDTH // 2), bf(RING, BOTH + 8, D)),
-        in_specs=[
-            by_columns(BOTH), by_columns(BOTH), weight_block(D, 1),
-            whole(RING * D, BOTH), whole(1, D),
-        ],
-        out_specs=(by_columns(BOTH), whole(RING, BOTH + 8, D)),
-        scratch_shapes=[scratch(RING * D, BOTH, jnp.float32), scratch(1, D, jnp.float32)],
+        in_specs=[half, half] + weight_blocks(D) + [by_group(D, BOTH), whole(1, D)],
+        out_specs=(half, by_group(BOTH + 8, D)),
+        scratch_shapes=[scratch(1, D, jnp.float32)],
         name="gradients_second",
         interpret=interpret,
-    )(mine, other, weights, attn, square)
-
-
-def weight_parts(place, sout, grad_first, grad_second, interpret=False):
-    turned = pl.BlockSpec(
-        (1, 2, RING, D, D), lambda r, at: (lax.rem(r - at[0] + SIDES, SIDES), 0, 0, 0, 0)
-    )
+    )(mine, other, *weights, attn, square)
+
+
+def weight_parts(sout, grad_first, grad_second, interpret=False):
+    turned = pl.BlockSpec((1, 2, RING, D, D), lambda r: (r, 0, 0, 0, 0))
     return pl.pallas_call(
         weight_kernel,
-        grid_spec=pltpu.PrefetchScalarGridSpec(
-            num_scalar_prefetch=1,
-            grid=(SIDES,),
-            in_specs=[
-                pl.BlockSpec((RING, BOTH, D), lambda r, at: (0, 0, 0)),
-                pl.BlockSpec((BOTH, COLS * D), lambda r, at: (0, jnp.minimum(r, CHUNK - 1))),
-                pl.BlockSpec((BOTH, COLS * D), lambda r, at: (0, jnp.maximum(r - CHUNK, 0))),
-            ],
-            out_specs=(turned, turned),
-            scratch_shapes=[pltpu.VMEM((RING, D, BOTH), jnp.bfloat16)],
-        ),
+        grid=(SIDES,),
         out_shape=(bf(SIDES, 2, RING, D, D),) * 2,
+        in_specs=[
+            whole(RING, BOTH, D),
+            pl.BlockSpec((BOTH, COLS * D), lambda r: (0, jnp.minimum(r, CHUNK - 1))),
+            pl.BlockSpec((BOTH, COLS * D), lambda r: (0, jnp.maximum(r - CHUNK, 0))),
+        ],
+        out_specs=(turned, turned),
+        scratch_shapes=[pltpu.VMEM((RING, D, BOTH), jnp.bfloat16)],
         name="weight_parts",
         interpret=interpret,
-    )(place, sout, grad_first, grad_second)
+    )(sout, grad_first, grad_second)
 
 
 def reduce_parts(place, keep, send, run):
@@ -441,19 +449,12 @@
     moved = []
     for turn, part in enumerate(rest, 1):
         moved.append(
-            lax.ppermute(part, "rep", [(rep, (rep + turn * COLS) % GROUPS) for rep in reps])
+            lax.ppermute(part, "rep", [(rep, (rep - turn * COLS) % GROUPS) for rep in reps])
         )
     own, send = run(add_rows_kernel, (bf(RING, D, D),) * 2, (own, *moved))
     other = lax.ppermute(send, "rep", [(rep, rep ^ 2) for rep in reps])
     own, *rest = run(add_across_kernel, (bf(D, D),) * RING, (place, own, other), scalars=1)
-    moved = [
-        lax.ppermute(
-            part,
-            "seq",
-            [(at, at // RING * RING + (at + turn) % RING) for at in range(GROUPS)],
-        )
-        for turn, part in enumerate(rest, 1)
-    ]
+    moved = [lax.ppermute(part, "seq", ring_turn(turn)) for turn, part in enumerate(rest, 1)]
     return run(total_kernel, fl(D, D), (own, *moved))
 
 
@@ -465,25 +466,32 @@
 ACROSS = [(place, (place + RING) % GROUPS) for place in range(GROUPS)]
 
 
-def unpad_kernel(in_ref, out_ref):
-    for place in range(RING):
-        out_ref[place * 3 * D : (place + 1) * 3 * D, :] = in_ref[place, : 3 * D, :]
-
-
-def gather_columns(student_wo, projection, run):
+def gather_columns(student_wo, projection, place, run):
     rep = lax.axis_index("rep")
+    reps = range(GROUPS)
     mine = jnp.concatenate(
         [
             lax.dynamic_slice_in_dim(student_wo, rep * D, D, 1),
             lax.dynamic_slice_in_dim(projection, rep * D, D, 1),
-            jnp.zeros((PADDED - 3 * D, D), jnp.bfloat16),
         ],
         axis=0,
     )
-    pieces = lax.all_gather(mine, "seq", axis=0, axis_index_groups=RINGS)
-    pieces = run(unpad_kernel, bf(RING * 3 * D, D), (pieces,))
-    columns = lax.all_gather(pieces, "rep", axis=0)
-    return columns.reshape(-1, RING, 3 * D, D)
+    pieces = [lax.ppermute(mine, "seq", ring_turn(turn)) for turn in range(1, RING)]
+    own = run(gather_kernel, bf(RING, 3 * D, D), (place, mine, *pieces), scalars=1)
+    other = lax.ppermute(own, "rep", [(rep, rep ^ 2) for rep in reps])
+    rows = [run(join_kernel, bf(2, RING, 3 * D, D), (own, other))]
+    for turn in range(1, SIDES):
+        rows.append(
+            lax.ppermute(rows[0], "rep", [(rep, (rep + turn * COLS) % GROUPS) for rep in reps])
+        )
+    weights = []
+    for part in rows:
+        weights += [part, lax.ppermute(part, "rep", [(rep, rep ^ 1) for rep in reps])]
+    return weights[:4], weights[4:]
+
+
+def ring_turn(turn):
+    return [(at, at // RING * RING + (at + turn) % RING) for at in range(GROUPS)]
 
 
 def shards(
@@ -496,8 +504,7 @@
     start = jnp.sum((docs[None, :] < docs[:, None]).astype(jnp.int32), axis=1)
     first = start[::ROWS]
     start = start[:, None]
-    rep = lax.axis_index("rep")
-    place = jnp.stack([rep // 4, (rep // 2) % 2, rep % 2, lax.axis_index("seq") % RING])
+    place = (lax.axis_index("seq") % RING).reshape(1)
 
     def swap(blocks):
         return lax.all_to_all(blocks, "seq", split_axis=0, concat_axis=0, tiled=True)
@@ -507,7 +514,7 @@
             blocks, "seq", split_axis=0, concat_axis=0, tiled=True, axis_index_groups=RINGS
         )
 
-    weights = gather_columns(student_wo, projection, run)
+    weights = gather_columns(student_wo, projection, place, run)
     s_pack, t_pack = run(
         pack_kernel,
         (bf(GROUPS, TOKENS, 3 * D), bf(GROUPS, TOKENS, 4 * D)),
@@ -531,14 +538,14 @@
         scalars=2,
     )
     t_tokens = swap_ring(tout)
-    mine = [terms(s_tokens, t_tokens, weights, half, interpret=interpret) for half in range(2)]
+    mine = [terms(s_tokens, t_tokens, half, interpret=interpret) for half in weights]
     other = [lax.ppermute(part, "seq", ACROSS) for part in mine]
-    grad_a, attn, square = gradients_first(mine[0], other[0], weights, interpret=interpret)
+    grad_a, attn, square = gradients_first(mine[0], other[0], weights[0], interpret=interpret)
     grad_b, d_attn = gradients_second(
-        mine[1], other[1], weights, attn, square, interpret=interpret
+        mine[1], other[1], weights[1], attn, square, interpret=interpret
     )
     grads = swap_ring(d_attn)
-    keep, send = weight_parts(place, s_tokens, grad_a, grad_b, interpret=interpret)
+    keep, send = weight_parts(s_tokens, grad_a, grad_b, interpret=interpret)
     d_wo = reduce_parts(place, keep, send, run)
     back, loss = run(
         backward_kernel,

time: 340 us -> 375 us (1.10)
  starting transfers between devices: 46.5 us -> 82.2 us
  blocking collectives: 69.8 us -> 48.5 us
  waiting for transfers between devices: 124 us -> 142 us
  Pallas kernels: 71 us -> 87.7 us
  between operations: 14.2 us -> 0.85 us
    ppermute x10 -> x25, waiting for transfers between devices: 21.6 us -> 110 us  [the longest x7 47.5 us: gather_columns(): lax.ppermute(mine, 'seq', ring_turn(turn))]
    all_gather x2 -> x0, waiting for transfers between devices: 42.3 us -> none  [the longest x1 42.3 us: gather_columns(): pieces = lax.all_gather(mine, 'seq', axis=0, axis_index_groups=RINGS)]
    all_to_all x2, waiting for transfers between devices: 32 us -> 0.01 us  [swap(): lax.all_to_all(blocks, 'seq', split_axis=0, concat_axis=0, tiled=True)]
    all_to_all x1 -> x0, blocking collectives: 29.8 us -> none  [swap_ring(): lax.all_to_all(blocks, 'seq', split_axis=0, concat_axis=0, tiled=True, ax...]
    ppermute x10 -> x25, starting transfers between devices: 21.8 us -> 43.7 us  [the longest x7 16.8 us: gather_columns(): lax.ppermute(mine, 'seq', ring_turn(turn))]
    all_to_all x2 -> x3, starting transfers between devices: 7.73 us -> 21.6 us  [swap_ring(): lax.all_to_all(blocks, 'seq', split_axis=0, concat_axis=0, tiled=True, ax...]
    pallas_call x5, Pallas kernels: 24.9 us -> 38.9 us  [the longest x2 17.3 us: terms(): pl.pallas_call(terms_kernel, grid=(RING,), out_shape=bf(BOTH, WIDTH // 2)...]
    all_to_all x1, blocking collectives: 40 us -> 48.5 us  [swap(): lax.all_to_all(blocks, 'seq', split_axis=0, concat_axis=0, tiled=True)]
  transfers between devices with their start and end apart: 20 -> 34, of which waited for: 11 -> 17; matrix products, arithmetic and copies ran while one was open for 1% -> 1% of each run, Pallas kernels for 17% -> 20%
where the time goes in v6:
time: 375 us; the launch traced here: 374 us
  waiting for transfers between devices  142 us (38%)
  Pallas kernels  87.7 us (23%)
  starting transfers between devices  82.2 us (22%)
  blocking collectives  48.5 us (13%)
  local copies, waits for them, and re-layouts  10.1 us (3%)
    pallas_call x11, Pallas kernels, call(): pl.pallas_call(kernel, out_shape=outs, in_specs=specs, out_specs=VM if si...  48.9 us
    all_to_all x1, blocking collectives, swap(): lax.all_to_all(blocks, 'seq', split_axis=0, concat_axis=0, tiled=True)  48.5 us
    ppermute x7, waiting for transfers between devices, gather_columns(): lax.ppermute(mine, 'seq', ring_turn(turn))  47.5 us
    ppermute x3, waiting for transfers between devices, reduce_parts(): lax.ppermute(part, 'rep', [(rep, (rep - turn * COLS) % GROUPS) for rep in...  22.4 us
    ppermute x3, waiting for transfers between devices, gather_columns(): lax.ppermute(rows[0], 'rep', [(rep, (rep + turn * COLS) % GROUPS) for rep...  21.7 us
    all_to_all x3, starting transfers between devices, swap_ring(): lax.all_to_all(blocks, 'seq', split_axis=0, concat_axis=0, tiled=True, ax...  21.6 us
    all_to_all x3, waiting for transfers between devices, swap_ring(): lax.all_to_all(blocks, 'seq', split_axis=0, concat_axis=0, tiled=True, ax...  19.9 us
    pallas_call x2, Pallas kernels, terms(): pl.pallas_call(terms_kernel, grid=(RING,), out_shape=bf(BOTH, WIDTH // 2)...  17.3 us
  transfers between devices with their start and end apart: 34, of which 17 were waited for; matrix products, arithmetic and copies ran while one was open for 1% of the time, Pallas kernels for 20%

profile of v6, /device:TPU:4, one launch (start us, length us, event | category | flops | bytes accessed | tf_op | source)
XLA Modules:
  0.0 373.5 jit_solution(3777214460459997204)
XLA Ops:
  0.6 3.9 %shard_map.137 = (bf16[16,128,384]{2,1,0:T(8,128)(2,1)}, bf16[16,128,512]{2,1,0:T(8,128)(2,1)}) custom-call(bf16[1,128,2048]{2,1,0:T(8,128)(2,1)} %sq_ref.1, bf16[1,128,512]{2,1,0:T(8,128)(2,1)} %sk_ref.1, bf16[1,128,512]{2,1,0:T(8,128)(2,1)} %sv_ref.1, bf16[1,128,4096]{2,1,0:T(8,128)(2,1)} %tq_ref.1, bf16[1,128,512]{2,1,0:T(8,128)(2,1)} %tk_ref.1, ...), custom_call_target="tpu_custom_call" | custom-call | tf_op jit(solution)/shard_map/pallas_call | solution.py:365
  4.6 48.5 %all_to_all.30.in_ref = bf16[16,128,384]{2,1,0:T(8,128)(2,1)} all-to-all(bf16[16,128,384]{2,1,0:T(8,128)(2,1)} %get-tuple-element.37), channel_id=1, replica_groups=mesh['seq'=16,'rep'=16] {'seq'}, dimensions={0} | all-to-all | bytes 3145728 | tf_op jit(solution)/shard_map/all_to_all | solution.py:510
  53.1 7.3 %all-to-all-start.1 = ((bf16[16,128,512]{2,1,0:T(8,128)(2,1)}), bf16[16,128,512]{2,1,0:T(8,128)(2,1)S(1)}, u32[]{:S(2)}, u32[]{:S(2)}) async-start(bf16[16,128,512]{2,1,0:T(8,128)(2,1)} %get-tuple-element.40), calls=%async_computation.1 | async-start | bytes 4194304 | tf_op jit(solution)/shard_map/all_to_all | solution.py:510
  72.8 39.0 %collective-permute-done.refs_0_ = bf16[384,128]{1,0:T(8,128)(2,1)S(1)} collective-permute-done((bf16[384,128]{1,0:T(8,128)(2,1)S(1)}, bf16[384,128]{1,0:T(8,128)(2,1)S(1)}, u32[]{:S(2)}, u32[]{:S(2)}) %collective-permute-start) | collective-permute-done | bytes 98336 | tf_op jit(solution)/shard_map/ppermute | solution.py:479
  128.9 15.7 %collective-permute-done.7.other_ref = bf16[8,384,128]{2,1,0:T(8,128)(2,1)} collective-permute-done((bf16[8,384,128]{2,1,0:T(8,128)(2,1)}, bf16[8,384,128]{2,1,0:T(8,128)(2,1)}, u32[]{:S(2)}, u32[]{:S(2)}) %collective-permute-start.7) | collective-permute-done | bytes 786464 | tf_op jit(solution)/shard_map/ppermute | solution.py:481
  156.2 8.7 %shard_map.138 = (bf16[8,256,128]{2,1,0:T(8,128)(2,1)}, bf16[8,256,768]{2,1,0:T(8,128)(2,1)}) custom-call(s32[32]{0:T(128)} %bitcast.10, s32[8]{0:T(128)} %slice.6.first_ref, s32[2048,1]{1,0:T(8,128)} %copy.17.start_ref, bf16[16,128,384]{2,1,0:T(8,128)(2,1)} %all_to_all.30.in_ref), custom_call_target="tpu_custom_call" | custom-call | tf_op jit(solution)/shard_map/pallas_call | solution.py:365
  166.3 7.3 %all-to-all-start.2 = ((bf16[8,256,128]{2,1,0:T(8,128)(2,1)}), bf16[8,256,128]{2,1,0:T(8,128)(2,1)S(1)}, u32[]{:S(2)}, u32[]{:S(2)}) async-start(bf16[8,256,128]{2,1,0:T(8,128)(2,1)} %get-tuple-element.41.out_ref), calls=%async_computation.2 | async-start | bytes 1048576 | tf_op jit(solution)/shard_map/all_to_all | solution.py:513
  173.6 9.8 %shard_map.139 = bf16[8,256,256]{2,1,0:T(8,128)(2,1)} custom-call(s32[32]{0:T(128)} %bitcast.11, s32[8]{0:T(128)} %slice.6.first_ref, s32[2048,1]{1,0:T(8,128)} %copy.17.start_ref, bf16[16,128,512]{2,1,0:T(8,128)(2,1)} %copy-done.3), custom_call_target="tpu_custom_call" | custom-call | tf_op jit(solution)/shard_map/pallas_call | solution.py:365
  183.5 6.1 %all-to-all-done.2.sout_ref = bf16[8,256,128]{2,1,0:T(8,128)(2,1)S(1)} async-done(((bf16[8,256,128]{2,1,0:T(8,128)(2,1)}), bf16[8,256,128]{2,1,0:T(8,128)(2,1)S(1)}, u32[]{:S(2)}, u32[]{:S(2)}) %all-to-all-start.2) | async-done | bytes 524320 | tf_op jit(solution)/shard_map/all_to_all | solution.py:513
  189.6 4.2 %all-to-all-start.3 = ((bf16[8,256,256]{2,1,0:T(8,128)(2,1)}), bf16[8,256,256]{2,1,0:T(8,128)(2,1)}, u32[]{:S(2)}, u32[]{:S(2)}) async-start(bf16[8,256,256]{2,1,0:T(8,128)(2,1)} %shard_map.139), calls=%async_computation.3 | async-start | bytes 2097152 | tf_op jit(solution)/shard_map/all_to_all | solution.py:513
  194.6 21.7 %collective-permute-done.8.a_ref = bf16[2,8,384,128]{3,2,1,0:T(8,128)(2,1)} collective-permute-done((bf16[2,8,384,128]{3,2,1,0:T(8,128)(2,1)}, bf16[2,8,384,128]{3,2,1,0:T(8,128)(2,1)}, u32[]{:S(2)}, u32[]{:S(2)}) %collective-permute-start.8) | collective-permute-done | bytes 1572896 | tf_op jit(solution)/shard_map/ppermute | solution.py:485
  220.3 8.6 %terms.3.mine_ref = bf16[256,1024]{1,0:T(8,128)(2,1)} custom-call(bf16[8,256,128]{2,1,0:T(8,128)(2,1)} %copy-done.2, bf16[8,256,256]{2,1,0:T(8,128)(2,1)} %all-to-all-done.3.tout_ref, bf16[2,8,384,128]{3,2,1,0:T(8,128)(2,1)} %shard_map.141.a_ref, bf16[2,8,384,128]{3,2,1,0:T(8,128)(2,1)} %copy-done.4, bf16[2,8,384,128]{3,2,1,0:T(8,128)(2,1)} %collective-permute-done.14.c_ref, ...), custom_call_target="tpu_custom_call" | custom-call | tf_op jit(solution)/shard_map/terms/pallas_call | solution.py:388
  229.1 8.6 %terms.2.mine_ref = bf16[256,1024]{1,0:T(8,128)(2,1)} custom-call(bf16[8,256,128]{2,1,0:T(8,128)(2,1)} %copy-done.2, bf16[8,256,256]{2,1,0:T(8,128)(2,1)} %all-to-all-done.3.tout_ref, bf16[2,8,384,128]{3,2,1,0:T(8,128)(2,1)} %collective-permute-done.8.a_ref, bf16[2,8,384,128]{3,2,1,0:T(8,128)(2,1)} %collective-permute-done.9.b_ref, ...), custom_call_target="tpu_custom_call" | custom-call | tf_op jit(solution)/shard_map/terms/pallas_call | solution.py:388
  244.6 7.1 %gradients_first.1 = (bf16[256,1024]{1,0:T(8,128)(2,1)}, f32[8,128,256]{2,1,0:T(8,128)}, f32[1,128]{1,0:T(1,128)}) custom-call(bf16[256,1024]{1,0:T(8,128)(2,1)} %terms.3.mine_ref, bf16[256,1024]{1,0:T(8,128)(2,1)} %copy-done.7, bf16[2,8,384,128]{3,2,1,0:T(8,128)(2,1)} %shard_map.141.a_ref, bf16[2,8,384,128]{3,2,1,0:T(8,128)(2,1)} %copy-done.4, ...), custom_call_target="tpu_custom_call" | custom-call | tf_op jit(solution)/shard_map/gradients_first/pallas_call | solution.py:402
  254.2 7.8 %gradients_second.1 = (bf16[256,1024]{1,0:T(8,128)(2,1)}, bf16[8,264,128]{2,1,0:T(8,128)(2,1)}) custom-call(bf16[256,1024]{1,0:T(8,128)(2,1)} %terms.2.mine_ref, bf16[256,1024]{1,0:T(8,128)(2,1)} %copy-done.8, bf16[2,8,384,128]{3,2,1,0:T(8,128)(2,1)} %collective-permute-done.8.a_ref, bf16[2,8,384,128]{3,2,1,0:T(8,128)(2,1)} %collective-permute-done.9.b_ref, ...), custom_call_target="tpu_custom_call" | custom-call | tf_op jit(solution)/shard_map/gradients_second/pallas_call | solution.py:415
  262.0 10.1 %all-to-all-start.4 = ((bf16[8,264,128]{2,1,0:T(8,128)(2,1)}), bf16[8,264,128]{2,1,0:T(8,128)(2,1)S(1)}, u32[]{:S(2)}, u32[]{:S(2)}) async-start(bf16[8,264,128]{2,1,0:T(8,128)(2,1)} %get-tuple-element.44), calls=%async_computation.4 | async-start | bytes 1081344 | tf_op jit(solution)/shard_map/all_to_all | solution.py:513
  272.1 6.7 %weight_parts.1 = (bf16[4,2,8,128,128]{4,3,2,1,0:T(8,128)(2,1)}, bf16[4,2,8,128,128]{4,3,2,1,0:T(8,128)(2,1)}) custom-call(bf16[8,256,128]{2,1,0:T(8,128)(2,1)} %copy-done.2, bf16[256,1024]{1,0:T(8,128)(2,1)} %get-tuple-element.47.first_ref, bf16[256,1024]{1,0:T(8,128)(2,1)} %get-tuple-element.48.second_ref), custom_call_target="tpu_custom_call" | custom-call | tf_op jit(solution)/shard_map/weight_parts/pallas_call | solution.py:429
  278.7 11.0 %all-to-all-done.4.grad_ref = bf16[8,264,128]{2,1,0:T(8,128)(2,1)S(1)} async-done(((bf16[8,264,128]{2,1,0:T(8,128)(2,1)}), bf16[8,264,128]{2,1,0:T(8,128)(2,1)S(1)}, u32[]{:S(2)}, u32[]{:S(2)}) %all-to-all-start.4) | async-done | bytes 540704 | tf_op jit(solution)/shard_map/all_to_all | solution.py:513
  290.5 9.2 %shard_map.142 = (bf16[16,128,384]{2,1,0:T(8,128)(2,1)}, f32[1,128]{1,0:T(1,128)}) custom-call(s32[32]{0:T(128)} %bitcast.12, s32[8]{0:T(128)} %slice.6.first_ref, bf16[8,264,128]{2,1,0:T(8,128)(2,1)} %copy-done.6, bf16[8,256,128]{2,1,0:T(8,128)(2,1)} %get-tuple-element.41.out_ref, bf16[16,128,384]{2,1,0:T(8,128)(2,1)} %all_to_all.30.in_ref, ...), custom_call_target="tpu_custom_call" | custom-call | tf_op jit(solution)/shard_map/pallas_call | solution.py:365
  299.7 4.8 %all-to-all-start.5 = ((bf16[16,128,384]{2,1,0:T(8,128)(2,1)}), bf16[16,128,384]{2,1,0:T(8,128)(2,1)S(1)}, u32[]{:S(2)}, u32[]{:S(2)}) async-start(bf16[16,128,384]{2,1,0:T(8,128)(2,1)} %get-tuple-element.65), calls=%async_computation.5 | async-start | bytes 3145728 | tf_op jit(solution)/shard_map/all_to_all | solution.py:510
  304.6 4.0 %shard_map.143 = (bf16[2,8,128,128]{3,2,1,0:T(8,128)(2,1)}, bf16[2,8,128,128]{3,2,1,0:T(8,128)(2,1)}, bf16[2,8,128,128]{3,2,1,0:T(8,128)(2,1)}, bf16[2,8,128,128]{3,2,1,0:T(8,128)(2,1)}) custom-call(bf16[4,2,8,128,128]{4,3,2,1,0:T(8,128)(2,1)} %get-tuple-element.49.keep_ref, bf16[4,2,8,128,128]{4,3,2,1,0:T(8,128)(2,1)} %collective-permute-done.17.other_ref), custom_call_target="tpu_custom_call" | custom-call | tf_op jit(solution)/shard_map/pallas_call | solution.py:365
  312.7 10.9 %collective-permute-done.18.a_ref = bf16[2,8,128,128]{3,2,1,0:T(8,128)(2,1)S(1)} collective-permute-done((bf16[2,8,128,128]{3,2,1,0:T(8,128)(2,1)}, bf16[2,8,128,128]{3,2,1,0:T(8,128)(2,1)S(1)}, u32[]{:S(2)}, u32[]{:S(2)}) %collective-permute-start.18) | collective-permute-done | bytes 524320 | tf_op jit(solution)/shard_map/ppermute | solution.py:452
  326.7 8.4 %collective-permute-done.20.c_ref = bf16[2,8,128,128]{3,2,1,0:T(8,128)(2,1)} collective-permute-done((bf16[2,8,128,128]{3,2,1,0:T(8,128)(2,1)}, bf16[2,8,128,128]{3,2,1,0:T(8,128)(2,1)}, u32[]{:S(2)}, u32[]{:S(2)}) %collective-permute-start.20) | collective-permute-done | bytes 524320 | tf_op jit(solution)/shard_map/ppermute | solution.py:452
  338.8 8.1 %collective-permute-done.21.other_ref = bf16[8,128,128]{2,1,0:T(8,128)(2,1)S(1)} collective-permute-done((bf16[8,128,128]{2,1,0:T(8,128)(2,1)}, bf16[8,128,128]{2,1,0:T(8,128)(2,1)S(1)}, u32[]{:S(2)}, u32[]{:S(2)}) %collective-permute-start.21) | collective-permute-done | bytes 262176 | tf_op jit(solution)/shard_map/ppermute | solution.py:455
  (113 shorter events, 95.0 us)
Async XLA Ops:
  53.1 111.9 %all-to-all-start.1 = ((bf16[16,128,512]{2,1,0:T(8,128)(2,1)}), bf16[16,128,512]{2,1,0:T(8,128)(2,1)S(1)}, u32[]{:S(2)}, u32[]{:S(2)}) async-start(bf16[16,128,512]{2,1,0:T(8,128)(2,1)} %get-tuple-element.40), calls=%async_computation.1 | async-start | bytes 4194304 | tf_op jit(solution)/shard_map/all_to_all | solution.py:510
  61.2 50.6 %collective-permute-start = (bf16[384,128]{1,0:T(8,128)(2,1)S(1)}, bf16[384,128]{1,0:T(8,128)(2,1)S(1)}, u32[]{:S(2)}, u32[]{:S(2)}) collective-permute-start(bf16[384,128]{1,0:T(8,128)(2,1)S(1)} %pad_maximum_fusion.own_ref), channel_id=1, source_target_pairs={{0,16},{16,32},{32,48},{48,64},{64,80},{80,96},{96,112},{112,0},{1... | collective-permute-start | bytes 294920 | tf_op jit(solution)/shard_map/ppermute | solution.py:479
  62.7 55.0 %collective-permute-start.1 = (bf16[384,128]{1,0:T(8,128)(2,1)S(1)}, bf16[384,128]{1,0:T(8,128)(2,1)S(1)}, u32[]{:S(2)}, u32[]{:S(2)}) collective-permute-start(bf16[384,128]{1,0:T(8,128)(2,1)S(1)} %pad_maximum_fusion.own_ref), channel_id=1, source_target_pairs={{0,32},{16,48},{32,64},{48,80},{64,96},{80,112},{96,0},{112,16},{1... | collective-permute-start | bytes 294920 | tf_op jit(solution)/shard_map/ppermute | solution.py:479
  65.1 58.2 %collective-permute-start.2 = (bf16[384,128]{1,0:T(8,128)(2,1)S(1)}, bf16[384,128]{1,0:T(8,128)(2,1)S(1)}, u32[]{:S(2)}, u32[]{:S(2)}) collective-permute-start(bf16[384,128]{1,0:T(8,128)(2,1)S(1)} %pad_maximum_fusion.own_ref), channel_id=1, source_target_pairs={{0,48},{16,64},{32,80},{48,96},{64,112},{80,0},{96,16},{112,32},{1... | collective-permute-start | bytes 294920 | tf_op jit(solution)/shard_map/ppermute | solution.py:479
  67.7 57.7 %collective-permute-start.3 = (bf16[384,128]{1,0:T(8,128)(2,1)S(1)}, bf16[384,128]{1,0:T(8,128)(2,1)}, u32[]{:S(2)}, u32[]{:S(2)}) collective-permute-start(bf16[384,128]{1,0:T(8,128)(2,1)S(1)} %pad_maximum_fusion.own_ref), channel_id=1, source_target_pairs={{0,64},{16,80},{32,96},{48,112},{64,0},{80,16},{96,32},{112,48},{1... | collective-permute-start | bytes 294920 | tf_op jit(solution)/shard_map/ppermute | solution.py:479
  70.1 55.4 %collective-permute-start.4 = (bf16[384,128]{1,0:T(8,128)(2,1)S(1)}, bf16[384,128]{1,0:T(8,128)(2,1)}, u32[]{:S(2)}, u32[]{:S(2)}) collective-permute-start(bf16[384,128]{1,0:T(8,128)(2,1)S(1)} %pad_maximum_fusion.own_ref), channel_id=1, source_target_pairs={{0,80},{16,96},{32,112},{48,0},{64,16},{80,32},{96,48},{112,64},{1... | collective-permute-start | bytes 294920 | tf_op jit(solution)/shard_map/ppermute | solution.py:479
  111.8 13.7 %collective-permute-start.5 = (bf16[384,128]{1,0:T(8,128)(2,1)S(1)}, bf16[384,128]{1,0:T(8,128)(2,1)}, u32[]{:S(2)}, u32[]{:S(2)}) collective-permute-start(bf16[384,128]{1,0:T(8,128)(2,1)S(1)} %pad_maximum_fusion.own_ref), channel_id=1, source_target_pairs={{0,96},{16,112},{32,0},{48,16},{64,32},{80,48},{96,64},{112,80},{1... | collective-permute-start | bytes 294920 | tf_op jit(solution)/shard_map/ppermute | solution.py:479
  127.7 16.9 %collective-permute-start.7 = (bf16[8,384,128]{2,1,0:T(8,128)(2,1)}, bf16[8,384,128]{2,1,0:T(8,128)(2,1)}, u32[]{:S(2)}, u32[]{:S(2)}) collective-permute-start(bf16[8,384,128]{2,1,0:T(8,128)(2,1)} %shard_map.140.own_ref), channel_id=1, source_target_pairs={{0,2},{1,3},{2,0},{3,1},{4,6},{5,7},{6,4},{7,5},{8,10},{9,11},{10,... | collective-permute-start | bytes 2359304 | tf_op jit(solution)/shard_map/ppermute | solution.py:481
  147.3 46.7 %collective-permute-start.14 = (bf16[2,8,384,128]{3,2,1,0:T(8,128)(2,1)}, bf16[2,8,384,128]{3,2,1,0:T(8,128)(2,1)}, u32[]{:S(2)}, u32[]{:S(2)}) collective-permute-start(bf16[2,8,384,128]{3,2,1,0:T(8,128)(2,1)} %shard_map.141.a_ref), channel_id=1, source_target_pairs={{0,4},{1,5},{2,6},{3,7},{4,8},{5,9},{6,10},{7,11},{8,12},{9,13},{1... | collective-permute-start | bytes 4718600 | tf_op jit(solution)/shard_map/ppermute | solution.py:485
  148.8 45.6 %collective-permute-start.10 = (bf16[2,8,384,128]{3,2,1,0:T(8,128)(2,1)}, bf16[2,8,384,128]{3,2,1,0:T(8,128)(2,1)}, u32[]{:S(2)}, u32[]{:S(2)}) collective-permute-start(bf16[2,8,384,128]{3,2,1,0:T(8,128)(2,1)} %shard_map.141.a_ref), channel_id=1, source_target_pairs={{0,12},{1,13},{2,14},{3,15},{4,0},{5,1},{6,2},{7,3},{8,4},{9,5},{1... | collective-permute-start | bytes 4718600 | tf_op jit(solution)/shard_map/ppermute | solution.py:485
  150.5 65.8 %collective-permute-start.8 = (bf16[2,8,384,128]{3,2,1,0:T(8,128)(2,1)}, bf16[2,8,384,128]{3,2,1,0:T(8,128)(2,1)}, u32[]{:S(2)}, u32[]{:S(2)}) collective-permute-start(bf16[2,8,384,128]{3,2,1,0:T(8,128)(2,1)} %shard_map.141.a_ref), channel_id=1, source_target_pairs={{0,8},{1,9},{2,10},{3,11},{4,12},{5,13},{6,14},{7,15},{8,0},{9,1},... | collective-permute-start | bytes 4718600 | tf_op jit(solution)/shard_map/ppermute | solution.py:485
  166.3 23.3 %all-to-all-start.2 = ((bf16[8,256,128]{2,1,0:T(8,128)(2,1)}), bf16[8,256,128]{2,1,0:T(8,128)(2,1)S(1)}, u32[]{:S(2)}, u32[]{:S(2)}) async-start(bf16[8,256,128]{2,1,0:T(8,128)(2,1)} %get-tuple-element.41.out_ref), calls=%async_computation.2 | async-start | bytes 1048576 | tf_op jit(solution)/shard_map/all_to_all | solution.py:513
  189.6 30.7 %all-to-all-start.3 = ((bf16[8,256,256]{2,1,0:T(8,128)(2,1)}), bf16[8,256,256]{2,1,0:T(8,128)(2,1)}, u32[]{:S(2)}, u32[]{:S(2)}) async-start(bf16[8,256,256]{2,1,0:T(8,128)(2,1)} %shard_map.139), calls=%async_computation.3 | async-start | bytes 2097152 | tf_op jit(solution)/shard_map/all_to_all | solution.py:513
  193.8 22.4 %collective-permute-start.13 = (bf16[2,8,384,128]{3,2,1,0:T(8,128)(2,1)S(1)}, bf16[2,8,384,128]{3,2,1,0:T(8,128)(2,1)S(1)}, u32[]{:S(2)}, u32[]{:S(2)}) collective-permute-start(bf16[2,8,384,128]{3,2,1,0:T(8,128)(2,1)S(1)} %copy-done.1), channel_id=1, source_target_pairs={{0,1},{1,0},{2,3},{3,2},{4,5},{5,4},{6,7},{7,6},{8,9},{9,8},{10,11... | collective-permute-start | bytes 4718600 | tf_op jit(solution)/shard_map/ppermute | solution.py:489
  194.0 23.5 %collective-permute-start.15 = (bf16[2,8,384,128]{3,2,1,0:T(8,128)(2,1)}, bf16[2,8,384,128]{3,2,1,0:T(8,128)(2,1)}, u32[]{:S(2)}, u32[]{:S(2)}) collective-permute-start(bf16[2,8,384,128]{3,2,1,0:T(8,128)(2,1)} %collective-permute-done.14.c_ref), channel_id=1, source_target_pairs={{0,1},{1,0},{2,3},{3,2},{4,5},{5,4},{6,7},{7,6},{8,9},{9,8},{10,11... | collective-permute-start | bytes 4718600 | tf_op jit(solution)/shard_map/ppermute | solution.py:489
  194.5 34.7 %collective-permute-start.11 = (bf16[2,8,384,128]{3,2,1,0:T(8,128)(2,1)}, bf16[2,8,384,128]{3,2,1,0:T(8,128)(2,1)}, u32[]{:S(2)}, u32[]{:S(2)}) collective-permute-start(bf16[2,8,384,128]{3,2,1,0:T(8,128)(2,1)} %collective-permute-done.10.c_ref), channel_id=1, source_target_pairs={{0,1},{1,0},{2,3},{3,2},{4,5},{5,4},{6,7},{7,6},{8,9},{9,8},{10,11... | collective-permute-start | bytes 4718600 | tf_op jit(solution)/shard_map/ppermute | solution.py:489
  228.9 14.9 %collective-permute-start.16 = (bf16[256,1024]{1,0:T(8,128)(2,1)}, bf16[256,1024]{1,0:T(8,128)(2,1)S(1)}, u32[]{:S(2)}, u32[]{:S(2)}) collective-permute-start(bf16[256,1024]{1,0:T(8,128)(2,1)} %terms.3.mine_ref), channel_id=1, source_target_pairs={{0,128},{16,144},{32,160},{48,176},{64,192},{80,208},{96,224},{112... | collective-permute-start | bytes 1572872 | tf_op jit(solution)/shard_map/ppermute | solution.py:542
  237.7 15.6 %collective-permute-start.12 = (bf16[256,1024]{1,0:T(8,128)(2,1)}, bf16[256,1024]{1,0:T(8,128)(2,1)S(1)}, u32[]{:S(2)}, u32[]{:S(2)}) collective-permute-start(bf16[256,1024]{1,0:T(8,128)(2,1)} %terms.2.mine_ref), channel_id=1, source_target_pairs={{0,128},{16,144},{32,160},{48,176},{64,192},{80,208},{96,224},{112... | collective-permute-start | bytes 1572872 | tf_op jit(solution)/shard_map/ppermute | solution.py:542
  262.0 27.7 %all-to-all-start.4 = ((bf16[8,264,128]{2,1,0:T(8,128)(2,1)}), bf16[8,264,128]{2,1,0:T(8,128)(2,1)S(1)}, u32[]{:S(2)}, u32[]{:S(2)}) async-start(bf16[8,264,128]{2,1,0:T(8,128)(2,1)} %get-tuple-element.44), calls=%async_computation.4 | async-start | bytes 1081344 | tf_op jit(solution)/shard_map/all_to_all | solution.py:513
  278.7 25.8 %collective-permute-start.17 = (bf16[4,2,8,128,128]{4,3,2,1,0:T(8,128)(2,1)}, bf16[4,2,8,128,128]{4,3,2,1,0:T(8,128)(2,1)}, u32[]{:S(2)}, u32[]{:S(2)}) collective-permute-start(bf16[4,2,8,128,128]{4,3,2,1,0:T(8,128)(2,1)} %get-tuple-element.50), channel_id=1, source_target_pairs={{0,1},{1,0},{2,3},{3,2},{4,5},{5,4},{6,7},{7,6},{8,9},{9,8},{10,11... | collective-permute-start | bytes 6291464 | tf_op jit(solution)/shard_map/ppermute | solution.py:447
  299.7 70.2 %all-to-all-start.5 = ((bf16[16,128,384]{2,1,0:T(8,128)(2,1)}), bf16[16,128,384]{2,1,0:T(8,128)(2,1)S(1)}, u32[]{:S(2)}, u32[]{:S(2)}) async-start(bf16[16,128,384]{2,1,0:T(8,128)(2,1)} %get-tuple-element.65), calls=%async_computation.5 | async-start | bytes 3145728 | tf_op jit(solution)/shard_map/all_to_all | solution.py:510
  308.6 15.0 %collective-permute-start.18 = (bf16[2,8,128,128]{3,2,1,0:T(8,128)(2,1)}, bf16[2,8,128,128]{3,2,1,0:T(8,128)(2,1)S(1)}, u32[]{:S(2)}, u32[]{:S(2)}) collective-permute-start(bf16[2,8,128,128]{3,2,1,0:T(8,128)(2,1)} %get-tuple-element.52), channel_id=1, source_target_pairs={{0,12},{1,13},{2,14},{3,15},{4,0},{5,1},{6,2},{7,3},{8,4},{9,5},{1... | collective-permute-start | bytes 1572872 | tf_op jit(solution)/shard_map/ppermute | solution.py:452
  310.0 16.7 %collective-permute-start.19 = (bf16[2,8,128,128]{3,2,1,0:T(8,128)(2,1)}, bf16[2,8,128,128]{3,2,1,0:T(8,128)(2,1)}, u32[]{:S(2)}, u32[]{:S(2)}) collective-permute-start(bf16[2,8,128,128]{3,2,1,0:T(8,128)(2,1)} %get-tuple-element.53), channel_id=1, source_target_pairs={{0,8},{1,9},{2,10},{3,11},{4,12},{5,13},{6,14},{7,15},{8,0},{9,1},... | collective-permute-start | bytes 1572872 | tf_op jit(solution)/shard_map/ppermute | solution.py:452
  311.9 23.1 %collective-permute-start.20 = (bf16[2,8,128,128]{3,2,1,0:T(8,128)(2,1)}, bf16[2,8,128,128]{3,2,1,0:T(8,128)(2,1)}, u32[]{:S(2)}, u32[]{:S(2)}) collective-permute-start(bf16[2,8,128,128]{3,2,1,0:T(8,128)(2,1)} %get-tuple-element.54), channel_id=1, source_target_pairs={{0,4},{1,5},{2,6},{3,7},{4,8},{5,9},{6,10},{7,11},{8,12},{9,13},{1... | collective-permute-start | bytes 1572872 | tf_op jit(solution)/shard_map/ppermute | solution.py:452
  (33 other events, 348.8 us)

commit v7 on v6

--- a/solution.py
+++ b/solution.py
@@ -19,6 +19,7 @@
 WIDTH = 2048
 BOTH = PAIR * TOKENS
 COLS = 4
+BATCH = 4
 SIDES = WIDTH // (COLS * D)
 CHUNK = WIDTH // (2 * COLS * D)
 HALF_COLS = COLS * CHUNK
@@ -174,61 +175,76 @@
     put_back(order_ref, dv, back_ref, slice(2 * D, 3 * D), stored_slots, LIMIT, 1.0)
 
 
-def side_by_side(refs, rows):
-    return jnp.concatenate([ref[side, 0, :rows, :] for ref in refs for side in range(2)], axis=1)
+def side_by_side(refs, group, rows):
+    return jnp.concatenate(
+        [ref[side, group, :rows, :] for ref in refs for side in range(2)], axis=1
+    )
 
 
 def terms_kernel(sout_ref, tout_ref, a_ref, b_ref, c_ref, d_ref, part_ref, total):
-    both = jnp.concatenate([sout_ref[0], tout_ref[0]], axis=1)
-    term = nn(both, side_by_side((a_ref, b_ref, c_ref, d_ref), 3 * D))
-    term = term.astype(jnp.bfloat16).astype(jnp.float32)
-
     @pl.when(pl.program_id(0) == 0)
     def _():
-        total[...] = term
-
-    @pl.when(pl.program_id(0) > 0)
-    def _():
-        total[...] += term
-
-    @pl.when(pl.program_id(0) == RING - 1)
+        total[...] = jnp.zeros_like(total)
+
+    def one(group, carry):
+        both = jnp.concatenate([sout_ref[group], tout_ref[group]], axis=1)
+        term = nn(both, side_by_side((a_ref, b_ref, c_ref, d_ref), group, 3 * D))
+        total[...] += term.astype(jnp.bfloat16).astype(jnp.float32)
+        return carry
+
+    lax.fori_loop(0, BATCH, one, 0)
+
+    @pl.when(pl.program_id(0) == RING // BATCH - 1)
     def _():
         part_ref[...] = total[...].astype(jnp.bfloat16)
 
 
-def gradient_once(mine_ref, other_ref, grad_ref, square_ref):
+def gradient_once(mine_ref, other_ref, grad_ref, turned, square_ref):
     diff = mine_ref[...].astype(jnp.float32) + other_ref[...].astype(jnp.float32)
-    grad_ref[...] = diff.astype(jnp.bfloat16)
+    grad = diff.astype(jnp.bfloat16)
+    grad_ref[...] = grad
+    turned[...] = grad.T
     square = jnp.sum(diff * diff, axis=0, keepdims=True)
     square_ref[...] = sum(square[:, col * D : (col + 1) * D] for col in range(HALF_COLS))
 
 
 def first_kernel(
-    mine_ref, other_ref, a_ref, b_ref, c_ref, d_ref, grad_ref, attn_ref, square_ref
+    mine_ref, other_ref, a_ref, b_ref, c_ref, d_ref, grad_ref, attn_ref, square_ref, turned
 ):
     @pl.when(pl.program_id(0) == 0)
     def _():
-        gradient_once(mine_ref, other_ref, grad_ref, square_ref)
-
-    attn_ref[0] = nt(side_by_side((a_ref, b_ref, c_ref, d_ref), D), grad_ref[...])
+        gradient_once(mine_ref, other_ref, grad_ref, turned, square_ref)
+
+    def one(group, carry):
+        attn_ref[group] = nn(side_by_side((a_ref, b_ref, c_ref, d_ref), group, D), turned[...])
+        return carry
+
+    lax.fori_loop(0, BATCH, one, 0)
 
 
 def second_kernel(
     mine_ref, other_ref, a_ref, b_ref, c_ref, d_ref, attn_in, square_in, grad_ref, attn_ref,
-    squares,
+    turned, squares,
 ):
     @pl.when(pl.program_id(0) == 0)
     def _():
-        gradient_once(mine_ref, other_ref, grad_ref, squares)
+        gradient_once(mine_ref, other_ref, grad_ref, turned, squares)
         squares[...] += square_in[...]
 
-    part = nt(side_by_side((a_ref, b_ref, c_ref, d_ref), D), grad_ref[...]) + attn_in[0]
-    attn_ref[0, :BOTH, :] = part.T.astype(jnp.bfloat16)
     total = squares[...]
     high = total.astype(jnp.bfloat16).astype(jnp.float32)
     line = lax.broadcasted_iota(jnp.int32, (8, D), 0)
     rows = jnp.where(line == 0, high, jnp.where(line == 1, total - high, 0.0))
-    attn_ref[0, BOTH:, :] = rows.astype(jnp.bfloat16)
+    rows = rows.astype(jnp.bfloat16)
+
+    def one(group, carry):
+        part = nn(side_by_side((a_ref, b_ref, c_ref, d_ref), group, D), turned[...])
+        part += attn_in[group]
+        attn_ref[group, :BOTH, :] = part.T.astype(jnp.bfloat16)
+        attn_ref[group, BOTH:, :] = rows
+        return carry
+
+    lax.fori_loop(0, BATCH, one, 0)
 
 
 def weight_kernel(sout_ref, first_ref, second_ref, keep_ref, send_ref, turned):
@@ -377,17 +393,17 @@
 
 
 def by_group(*shape):
-    return pl.BlockSpec((1,) + shape, lambda g: (g,) + (0,) * len(shape))
+    return pl.BlockSpec((BATCH,) + shape, lambda g: (g,) + (0,) * len(shape))
 
 
 def weight_blocks(rows):
-    return [pl.BlockSpec((2, 1, rows, D), lambda g: (0, g, 0, 0))] * 4
+    return [pl.BlockSpec((2, BATCH, rows, D), lambda g: (0, g, 0, 0))] * 4
 
 
 def terms(sout, tout, weights, interpret=False):
     return pl.pallas_call(
         terms_kernel,
-        grid=(RING,),
+        grid=(RING // BATCH,),
         out_shape=bf(BOTH, WIDTH // 2),
         in_specs=[by_group(BOTH, D), by_group(BOTH, 2 * D)] + weight_blocks(3 * D),
         out_specs=whole(BOTH, WIDTH // 2),
@@ -401,10 +417,11 @@
     half = whole(BOTH, WIDTH // 2)
     return pl.pallas_call(
         first_kernel,
-        grid=(RING,),
+        grid=(RING // BATCH,),
         out_shape=(bf(BOTH, WIDTH // 2), fl(RING, D, BOTH), fl(1, D)),
         in_specs=[half, half] + weight_blocks(D),
         out_specs=(half, by_group(D, BOTH), whole(1, D)),
+        scratch_shapes=[scratch(WIDTH // 2, BOTH)],
         name="gradients_first",
         interpret=interpret,
     )(mine, other, *weights)
@@ -414,11 +431,11 @@
     half = whole(BOTH, WIDTH // 2)
     return pl.pallas_call(
         second_kernel,
-        grid=(RING,),
+        grid=(RING // BATCH,),
         out_shape=(bf(BOTH, WIDTH // 2), bf(RING, BOTH + 8, D)),
         in_specs=[half, half] + weight_blocks(D) + [by_group(D, BOTH), whole(1, D)],
         out_specs=(half, by_group(BOTH + 8, D)),
-        scratch_shapes=[scratch(1, D, jnp.float32)],
+        scratch_shapes=[scratch(WIDTH // 2, BOTH), scratch(1, D, jnp.float32)],
         name="gradients_second",
         interpret=interpret,
     )(mine, other, *weights, attn, square)

time: 375 us -> 370 us (0.987)
  Pallas kernels: 87.7 us -> 78.8 us
  waiting for transfers between devices: 142 us -> 147 us
    pallas_call x4, Pallas kernels: 32.2 us -> 23.3 us  [the longest x2 13.2 us: terms(): pl.pallas_call(terms_kernel, grid=(RING // BATCH,), out_shape=bf(BOTH, WI...]
    ppermute x2, waiting for transfers between devices: 4.4 us -> 8.87 us  [shards(): other = [lax.ppermute(part, 'seq', ACROSS) for part in mine]]
  transfers between devices with their start and end apart: 34 -> 34, of which waited for: 17 -> 17; matrix products, arithmetic and copies ran while one was open for 1% -> 1% of each run, Pallas kernels for 20% -> 18%
where the time goes in v7:
time: 370 us; the launch traced here: 369 us
  waiting for transfers between devices  147 us (40%)
  starting transfers between devices  82.2 us (22%)
  Pallas kernels  78.8 us (21%)
  blocking collectives  48.5 us (13%)
  local copies, waits for them, and re-layouts  10.1 us (3%)
    pallas_call x11, Pallas kernels, call(): pl.pallas_call(kernel, out_shape=outs, in_specs=specs, out_specs=VM if si...  48.9 us
    all_to_all x1, blocking collectives, swap(): lax.all_to_all(blocks, 'seq', split_axis=0, concat_axis=0, tiled=True)  48.5 us
    ppermute x7, waiting for transfers between devices, gather_columns(): lax.ppermute(mine, 'seq', ring_turn(turn))  47.5 us
    ppermute x3, waiting for transfers between devices, reduce_parts(): lax.ppermute(part, 'rep', [(rep, (rep - turn * COLS) % GROUPS) for rep in...  22.4 us
    ppermute x3, waiting for transfers between devices, gather_columns(): lax.ppermute(rows[0], 'rep', [(rep, (rep + turn * COLS) % GROUPS) for rep...  21.7 us
    all_to_all x3, starting transfers between devices, swap_ring(): lax.all_to_all(blocks, 'seq', split_axis=0, concat_axis=0, tiled=True, ax...  21.6 us
    all_to_all x3, waiting for transfers between devices, swap_ring(): lax.all_to_all(blocks, 'seq', split_axis=0, concat_axis=0, tiled=True, ax...  19.9 us
    ppermute x7, starting transfers between devices, gather_columns(): lax.ppermute(mine, 'seq', ring_turn(turn))  16.8 us
  transfers between devices with their start and end apart: 34, of which 17 were waited for; matrix products, arithmetic and copies ran while one was open for 1% of the time, Pallas kernels for 18%

profile of v7, /device:TPU:4, one launch (start us, length us, event | category | flops | bytes accessed | tf_op | source)
XLA Modules:
  0.0 369.0 jit_solution(1790215763721744764)
XLA Ops:
  4.6 48.5 %all_to_all.30.in_ref = bf16[16,128,384]{2,1,0:T(8,128)(2,1)} all-to-all(bf16[16,128,384]{2,1,0:T(8,128)(2,1)} %get-tuple-element.37), channel_id=1, replica_groups=mesh['seq'=16,'rep'=16] {'seq'}, dimensions={0} | all-to-all | bytes 3145728 | tf_op jit(solution)/shard_map/all_to_all | solution.py:527
  53.1 7.3 %all-to-all-start.1 = ((bf16[16,128,512]{2,1,0:T(8,128)(2,1)}), bf16[16,128,512]{2,1,0:T(8,128)(2,1)S(1)}, u32[]{:S(2)}, u32[]{:S(2)}) async-start(bf16[16,128,512]{2,1,0:T(8,128)(2,1)} %get-tuple-element.40), calls=%async_computation.1 | async-start | bytes 4194304 | tf_op jit(solution)/shard_map/all_to_all | solution.py:527
  72.8 39.0 %collective-permute-done.refs_0_ = bf16[384,128]{1,0:T(8,128)(2,1)S(1)} collective-permute-done((bf16[384,128]{1,0:T(8,128)(2,1)S(1)}, bf16[384,128]{1,0:T(8,128)(2,1)S(1)}, u32[]{:S(2)}, u32[]{:S(2)}) %collective-permute-start) | collective-permute-done | bytes 98336 | tf_op jit(solution)/shard_map/ppermute | solution.py:496
  128.9 15.7 %collective-permute-done.7.other_ref = bf16[8,384,128]{2,1,0:T(8,128)(2,1)} collective-permute-done((bf16[8,384,128]{2,1,0:T(8,128)(2,1)}, bf16[8,384,128]{2,1,0:T(8,128)(2,1)}, u32[]{:S(2)}, u32[]{:S(2)}) %collective-permute-start.7) | collective-permute-done | bytes 786464 | tf_op jit(solution)/shard_map/ppermute | solution.py:498
  156.2 8.7 %shard_map.138 = (bf16[8,256,128]{2,1,0:T(8,128)(2,1)}, bf16[8,256,768]{2,1,0:T(8,128)(2,1)}) custom-call(s32[32]{0:T(128)} %bitcast.10, s32[8]{0:T(128)} %slice.6.first_ref, s32[2048,1]{1,0:T(8,128)} %copy.17.start_ref, bf16[16,128,384]{2,1,0:T(8,128)(2,1)} %all_to_all.30.in_ref), custom_call_target="tpu_custom_call" | custom-call | tf_op jit(solution)/shard_map/pallas_call | solution.py:381
  166.3 7.3 %all-to-all-start.2 = ((bf16[8,256,128]{2,1,0:T(8,128)(2,1)}), bf16[8,256,128]{2,1,0:T(8,128)(2,1)S(1)}, u32[]{:S(2)}, u32[]{:S(2)}) async-start(bf16[8,256,128]{2,1,0:T(8,128)(2,1)} %get-tuple-element.41.out_ref), calls=%async_computation.2 | async-start | bytes 1048576 | tf_op jit(solution)/shard_map/all_to_all | solution.py:530
  173.6 9.8 %shard_map.139 = bf16[8,256,256]{2,1,0:T(8,128)(2,1)} custom-call(s32[32]{0:T(128)} %bitcast.11, s32[8]{0:T(128)} %slice.6.first_ref, s32[2048,1]{1,0:T(8,128)} %copy.17.start_ref, bf16[16,128,512]{2,1,0:T(8,128)(2,1)} %copy-done.3), custom_call_target="tpu_custom_call" | custom-call | tf_op jit(solution)/shard_map/pallas_call | solution.py:381
  183.5 6.1 %all-to-all-done.2.sout_ref = bf16[8,256,128]{2,1,0:T(8,128)(2,1)S(1)} async-done(((bf16[8,256,128]{2,1,0:T(8,128)(2,1)}), bf16[8,256,128]{2,1,0:T(8,128)(2,1)S(1)}, u32[]{:S(2)}, u32[]{:S(2)}) %all-to-all-start.2) | async-done | bytes 524320 | tf_op jit(solution)/shard_map/all_to_all | solution.py:530
  189.6 4.2 %all-to-all-start.3 = ((bf16[8,256,256]{2,1,0:T(8,128)(2,1)}), bf16[8,256,256]{2,1,0:T(8,128)(2,1)}, u32[]{:S(2)}, u32[]{:S(2)}) async-start(bf16[8,256,256]{2,1,0:T(8,128)(2,1)} %shard_map.139), calls=%async_computation.3 | async-start | bytes 2097152 | tf_op jit(solution)/shard_map/all_to_all | solution.py:530
  194.6 21.7 %collective-permute-done.8.a_ref = bf16[2,8,384,128]{3,2,1,0:T(8,128)(2,1)} collective-permute-done((bf16[2,8,384,128]{3,2,1,0:T(8,128)(2,1)}, bf16[2,8,384,128]{3,2,1,0:T(8,128)(2,1)}, u32[]{:S(2)}, u32[]{:S(2)}) %collective-permute-start.8) | collective-permute-done | bytes 1572896 | tf_op jit(solution)/shard_map/ppermute | solution.py:502
  220.3 6.6 %terms.3.mine_ref = bf16[256,1024]{1,0:T(8,128)(2,1)} custom-call(bf16[8,256,128]{2,1,0:T(8,128)(2,1)} %copy-done.2, bf16[8,256,256]{2,1,0:T(8,128)(2,1)} %all-to-all-done.3.tout_ref, bf16[2,8,384,128]{3,2,1,0:T(8,128)(2,1)} %shard_map.141.a_ref, bf16[2,8,384,128]{3,2,1,0:T(8,128)(2,1)} %copy-done.4, bf16[2,8,384,128]{3,2,1,0:T(8,128)(2,1)} %collective-permute-done.14.c_ref, ...), custom_call_target="tpu_custom_call" | custom-call | tf_op jit(solution)/shard_map/terms/pallas_call | solution.py:404
  227.1 6.6 %terms.2.mine_ref = bf16[256,1024]{1,0:T(8,128)(2,1)} custom-call(bf16[8,256,128]{2,1,0:T(8,128)(2,1)} %copy-done.2, bf16[8,256,256]{2,1,0:T(8,128)(2,1)} %all-to-all-done.3.tout_ref, bf16[2,8,384,128]{3,2,1,0:T(8,128)(2,1)} %collective-permute-done.8.a_ref, bf16[2,8,384,128]{3,2,1,0:T(8,128)(2,1)} %collective-permute-done.9.b_ref, ...), custom_call_target="tpu_custom_call" | custom-call | tf_op jit(solution)/shard_map/terms/pallas_call | solution.py:404
  237.0 6.4 %collective-permute-done.16.other_ref = bf16[256,1024]{1,0:T(8,128)(2,1)S(1)} collective-permute-done((bf16[256,1024]{1,0:T(8,128)(2,1)}, bf16[256,1024]{1,0:T(8,128)(2,1)S(1)}, u32[]{:S(2)}, u32[]{:S(2)}) %collective-permute-start.16) | collective-permute-done | bytes 524320 | tf_op jit(solution)/shard_map/ppermute | solution.py:559
  244.2 4.7 %gradients_first.1 = (bf16[256,1024]{1,0:T(8,128)(2,1)}, f32[8,128,256]{2,1,0:T(8,128)}, f32[1,128]{1,0:T(1,128)}) custom-call(bf16[256,1024]{1,0:T(8,128)(2,1)} %terms.3.mine_ref, bf16[256,1024]{1,0:T(8,128)(2,1)} %copy-done.7, bf16[2,8,384,128]{3,2,1,0:T(8,128)(2,1)} %shard_map.141.a_ref, bf16[2,8,384,128]{3,2,1,0:T(8,128)(2,1)} %copy-done.4, ...), custom_call_target="tpu_custom_call" | custom-call | tf_op jit(solution)/shard_map/gradients_first/pallas_call | solution.py:418
  252.1 5.4 %gradients_second.1 = (bf16[256,1024]{1,0:T(8,128)(2,1)}, bf16[8,264,128]{2,1,0:T(8,128)(2,1)}) custom-call(bf16[256,1024]{1,0:T(8,128)(2,1)} %terms.2.mine_ref, bf16[256,1024]{1,0:T(8,128)(2,1)} %copy-done.8, bf16[2,8,384,128]{3,2,1,0:T(8,128)(2,1)} %collective-permute-done.8.a_ref, bf16[2,8,384,128]{3,2,1,0:T(8,128)(2,1)} %collective-permute-done.9.b_ref, ...), custom_call_target="tpu_custom_call" | custom-call | tf_op jit(solution)/shard_map/gradients_second/pallas_call | solution.py:432
  257.5 10.1 %all-to-all-start.4 = ((bf16[8,264,128]{2,1,0:T(8,128)(2,1)}), bf16[8,264,128]{2,1,0:T(8,128)(2,1)S(1)}, u32[]{:S(2)}, u32[]{:S(2)}) async-start(bf16[8,264,128]{2,1,0:T(8,128)(2,1)} %get-tuple-element.44), calls=%async_computation.4 | async-start | bytes 1081344 | tf_op jit(solution)/shard_map/all_to_all | solution.py:530
  267.6 6.7 %weight_parts.1 = (bf16[4,2,8,128,128]{4,3,2,1,0:T(8,128)(2,1)}, bf16[4,2,8,128,128]{4,3,2,1,0:T(8,128)(2,1)}) custom-call(bf16[8,256,128]{2,1,0:T(8,128)(2,1)} %copy-done.2, bf16[256,1024]{1,0:T(8,128)(2,1)} %get-tuple-element.47.first_ref, bf16[256,1024]{1,0:T(8,128)(2,1)} %get-tuple-element.48.second_ref), custom_call_target="tpu_custom_call" | custom-call | tf_op jit(solution)/shard_map/weight_parts/pallas_call | solution.py:446
  274.3 11.0 %all-to-all-done.4.grad_ref = bf16[8,264,128]{2,1,0:T(8,128)(2,1)S(1)} async-done(((bf16[8,264,128]{2,1,0:T(8,128)(2,1)}), bf16[8,264,128]{2,1,0:T(8,128)(2,1)S(1)}, u32[]{:S(2)}, u32[]{:S(2)}) %all-to-all-start.4) | async-done | bytes 540704 | tf_op jit(solution)/shard_map/all_to_all | solution.py:530
  286.1 9.2 %shard_map.142 = (bf16[16,128,384]{2,1,0:T(8,128)(2,1)}, f32[1,128]{1,0:T(1,128)}) custom-call(s32[32]{0:T(128)} %bitcast.12, s32[8]{0:T(128)} %slice.6.first_ref, bf16[8,264,128]{2,1,0:T(8,128)(2,1)} %copy-done.6, bf16[8,256,128]{2,1,0:T(8,128)(2,1)} %get-tuple-element.41.out_ref, bf16[16,128,384]{2,1,0:T(8,128)(2,1)} %all_to_all.30.in_ref, ...), custom_call_target="tpu_custom_call" | custom-call | tf_op jit(solution)/shard_map/pallas_call | solution.py:381
  295.3 4.8 %all-to-all-start.5 = ((bf16[16,128,384]{2,1,0:T(8,128)(2,1)}), bf16[16,128,384]{2,1,0:T(8,128)(2,1)S(1)}, u32[]{:S(2)}, u32[]{:S(2)}) async-start(bf16[16,128,384]{2,1,0:T(8,128)(2,1)} %get-tuple-element.65), calls=%async_computation.5 | async-start | bytes 3145728 | tf_op jit(solution)/shard_map/all_to_all | solution.py:527
  300.1 4.0 %shard_map.143 = (bf16[2,8,128,128]{3,2,1,0:T(8,128)(2,1)}, bf16[2,8,128,128]{3,2,1,0:T(8,128)(2,1)}, bf16[2,8,128,128]{3,2,1,0:T(8,128)(2,1)}, bf16[2,8,128,128]{3,2,1,0:T(8,128)(2,1)}) custom-call(bf16[4,2,8,128,128]{4,3,2,1,0:T(8,128)(2,1)} %get-tuple-element.49.keep_ref, bf16[4,2,8,128,128]{4,3,2,1,0:T(8,128)(2,1)} %collective-permute-done.17.other_ref), custom_call_target="tpu_custom_call" | custom-call | tf_op jit(solution)/shard_map/pallas_call | solution.py:381
  308.2 10.9 %collective-permute-done.18.a_ref = bf16[2,8,128,128]{3,2,1,0:T(8,128)(2,1)S(1)} collective-permute-done((bf16[2,8,128,128]{3,2,1,0:T(8,128)(2,1)}, bf16[2,8,128,128]{3,2,1,0:T(8,128)(2,1)S(1)}, u32[]{:S(2)}, u32[]{:S(2)}) %collective-permute-start.18) | collective-permute-done | bytes 524320 | tf_op jit(solution)/shard_map/ppermute | solution.py:469
  322.2 8.4 %collective-permute-done.20.c_ref = bf16[2,8,128,128]{3,2,1,0:T(8,128)(2,1)} collective-permute-done((bf16[2,8,128,128]{3,2,1,0:T(8,128)(2,1)}, bf16[2,8,128,128]{3,2,1,0:T(8,128)(2,1)}, u32[]{:S(2)}, u32[]{:S(2)}) %collective-permute-start.20) | collective-permute-done | bytes 524320 | tf_op jit(solution)/shard_map/ppermute | solution.py:469
  334.3 8.1 %collective-permute-done.21.other_ref = bf16[8,128,128]{2,1,0:T(8,128)(2,1)S(1)} collective-permute-done((bf16[8,128,128]{2,1,0:T(8,128)(2,1)}, bf16[8,128,128]{2,1,0:T(8,128)(2,1)S(1)}, u32[]{:S(2)}, u32[]{:S(2)}) %collective-permute-start.21) | collective-permute-done | bytes 262176 | tf_op jit(solution)/shard_map/ppermute | solution.py:472
  (113 shorter events, 96.9 us)
Async XLA Ops:
  53.1 111.9 %all-to-all-start.1 = ((bf16[16,128,512]{2,1,0:T(8,128)(2,1)}), bf16[16,128,512]{2,1,0:T(8,128)(2,1)S(1)}, u32[]{:S(2)}, u32[]{:S(2)}) async-start(bf16[16,128,512]{2,1,0:T(8,128)(2,1)} %get-tuple-element.40), calls=%async_computation.1 | async-start | bytes 4194304 | tf_op jit(solution)/shard_map/all_to_all | solution.py:527
  61.2 50.6 %collective-permute-start = (bf16[384,128]{1,0:T(8,128)(2,1)S(1)}, bf16[384,128]{1,0:T(8,128)(2,1)S(1)}, u32[]{:S(2)}, u32[]{:S(2)}) collective-permute-start(bf16[384,128]{1,0:T(8,128)(2,1)S(1)} %pad_maximum_fusion.own_ref), channel_id=1, source_target_pairs={{0,16},{16,32},{32,48},{48,64},{64,80},{80,96},{96,112},{112,0},{1... | collective-permute-start | bytes 294920 | tf_op jit(solution)/shard_map/ppermute | solution.py:496
  62.7 55.0 %collective-permute-start.1 = (bf16[384,128]{1,0:T(8,128)(2,1)S(1)}, bf16[384,128]{1,0:T(8,128)(2,1)S(1)}, u32[]{:S(2)}, u32[]{:S(2)}) collective-permute-start(bf16[384,128]{1,0:T(8,128)(2,1)S(1)} %pad_maximum_fusion.own_ref), channel_id=1, source_target_pairs={{0,32},{16,48},{32,64},{48,80},{64,96},{80,112},{96,0},{112,16},{1... | collective-permute-start | bytes 294920 | tf_op jit(solution)/shard_map/ppermute | solution.py:496
  65.1 58.2 %collective-permute-start.2 = (bf16[384,128]{1,0:T(8,128)(2,1)S(1)}, bf16[384,128]{1,0:T(8,128)(2,1)S(1)}, u32[]{:S(2)}, u32[]{:S(2)}) collective-permute-start(bf16[384,128]{1,0:T(8,128)(2,1)S(1)} %pad_maximum_fusion.own_ref), channel_id=1, source_target_pairs={{0,48},{16,64},{32,80},{48,96},{64,112},{80,0},{96,16},{112,32},{1... | collective-permute-start | bytes 294920 | tf_op jit(solution)/shard_map/ppermute | solution.py:496
  67.7 57.7 %collective-permute-start.3 = (bf16[384,128]{1,0:T(8,128)(2,1)S(1)}, bf16[384,128]{1,0:T(8,128)(2,1)}, u32[]{:S(2)}, u32[]{:S(2)}) collective-permute-start(bf16[384,128]{1,0:T(8,128)(2,1)S(1)} %pad_maximum_fusion.own_ref), channel_id=1, source_target_pairs={{0,64},{16,80},{32,96},{48,112},{64,0},{80,16},{96,32},{112,48},{1... | collective-permute-start | bytes 294920 | tf_op jit(solution)/shard_map/ppermute | solution.py:496
  70.1 55.4 %collective-permute-start.4 = (bf16[384,128]{1,0:T(8,128)(2,1)S(1)}, bf16[384,128]{1,0:T(8,128)(2,1)}, u32[]{:S(2)}, u32[]{:S(2)}) collective-permute-start(bf16[384,128]{1,0:T(8,128)(2,1)S(1)} %pad_maximum_fusion.own_ref), channel_id=1, source_target_pairs={{0,80},{16,96},{32,112},{48,0},{64,16},{80,32},{96,48},{112,64},{1... | collective-permute-start | bytes 294920 | tf_op jit(solution)/shard_map/ppermute | solution.py:496
  111.8 13.7 %collective-permute-start.5 = (bf16[384,128]{1,0:T(8,128)(2,1)S(1)}, bf16[384,128]{1,0:T(8,128)(2,1)}, u32[]{:S(2)}, u32[]{:S(2)}) collective-permute-start(bf16[384,128]{1,0:T(8,128)(2,1)S(1)} %pad_maximum_fusion.own_ref), channel_id=1, source_target_pairs={{0,96},{16,112},{32,0},{48,16},{64,32},{80,48},{96,64},{112,80},{1... | collective-permute-start | bytes 294920 | tf_op jit(solution)/shard_map/ppermute | solution.py:496
  127.7 16.9 %collective-permute-start.7 = (bf16[8,384,128]{2,1,0:T(8,128)(2,1)}, bf16[8,384,128]{2,1,0:T(8,128)(2,1)}, u32[]{:S(2)}, u32[]{:S(2)}) collective-permute-start(bf16[8,384,128]{2,1,0:T(8,128)(2,1)} %shard_map.140.own_ref), channel_id=1, source_target_pairs={{0,2},{1,3},{2,0},{3,1},{4,6},{5,7},{6,4},{7,5},{8,10},{9,11},{10,... | collective-permute-start | bytes 2359304 | tf_op jit(solution)/shard_map/ppermute | solution.py:498
  147.3 46.7 %collective-permute-start.14 = (bf16[2,8,384,128]{3,2,1,0:T(8,128)(2,1)}, bf16[2,8,384,128]{3,2,1,0:T(8,128)(2,1)}, u32[]{:S(2)}, u32[]{:S(2)}) collective-permute-start(bf16[2,8,384,128]{3,2,1,0:T(8,128)(2,1)} %shard_map.141.a_ref), channel_id=1, source_target_pairs={{0,4},{1,5},{2,6},{3,7},{4,8},{5,9},{6,10},{7,11},{8,12},{9,13},{1... | collective-permute-start | bytes 4718600 | tf_op jit(solution)/shard_map/ppermute | solution.py:502
  148.8 45.6 %collective-permute-start.10 = (bf16[2,8,384,128]{3,2,1,0:T(8,128)(2,1)}, bf16[2,8,384,128]{3,2,1,0:T(8,128)(2,1)}, u32[]{:S(2)}, u32[]{:S(2)}) collective-permute-start(bf16[2,8,384,128]{3,2,1,0:T(8,128)(2,1)} %shard_map.141.a_ref), channel_id=1, source_target_pairs={{0,12},{1,13},{2,14},{3,15},{4,0},{5,1},{6,2},{7,3},{8,4},{9,5},{1... | collective-permute-start | bytes 4718600 | tf_op jit(solution)/shard_map/ppermute | solution.py:502
  150.5 65.8 %collective-permute-start.8 = (bf16[2,8,384,128]{3,2,1,0:T(8,128)(2,1)}, bf16[2,8,384,128]{3,2,1,0:T(8,128)(2,1)}, u32[]{:S(2)}, u32[]{:S(2)}) collective-permute-start(bf16[2,8,384,128]{3,2,1,0:T(8,128)(2,1)} %shard_map.141.a_ref), channel_id=1, source_target_pairs={{0,8},{1,9},{2,10},{3,11},{4,12},{5,13},{6,14},{7,15},{8,0},{9,1},... | collective-permute-start | bytes 4718600 | tf_op jit(solution)/shard_map/ppermute | solution.py:502
  166.3 23.3 %all-to-all-start.2 = ((bf16[8,256,128]{2,1,0:T(8,128)(2,1)}), bf16[8,256,128]{2,1,0:T(8,128)(2,1)S(1)}, u32[]{:S(2)}, u32[]{:S(2)}) async-start(bf16[8,256,128]{2,1,0:T(8,128)(2,1)} %get-tuple-element.41.out_ref), calls=%async_computation.2 | async-start | bytes 1048576 | tf_op jit(solution)/shard_map/all_to_all | solution.py:530
  189.6 30.7 %all-to-all-start.3 = ((bf16[8,256,256]{2,1,0:T(8,128)(2,1)}), bf16[8,256,256]{2,1,0:T(8,128)(2,1)}, u32[]{:S(2)}, u32[]{:S(2)}) async-start(bf16[8,256,256]{2,1,0:T(8,128)(2,1)} %shard_map.139), calls=%async_computation.3 | async-start | bytes 2097152 | tf_op jit(solution)/shard_map/all_to_all | solution.py:530
  193.8 22.4 %collective-permute-start.13 = (bf16[2,8,384,128]{3,2,1,0:T(8,128)(2,1)S(1)}, bf16[2,8,384,128]{3,2,1,0:T(8,128)(2,1)S(1)}, u32[]{:S(2)}, u32[]{:S(2)}) collective-permute-start(bf16[2,8,384,128]{3,2,1,0:T(8,128)(2,1)S(1)} %copy-done.1), channel_id=1, source_target_pairs={{0,1},{1,0},{2,3},{3,2},{4,5},{5,4},{6,7},{7,6},{8,9},{9,8},{10,11... | collective-permute-start | bytes 4718600 | tf_op jit(solution)/shard_map/ppermute | solution.py:506
  194.0 23.5 %collective-permute-start.15 = (bf16[2,8,384,128]{3,2,1,0:T(8,128)(2,1)}, bf16[2,8,384,128]{3,2,1,0:T(8,128)(2,1)}, u32[]{:S(2)}, u32[]{:S(2)}) collective-permute-start(bf16[2,8,384,128]{3,2,1,0:T(8,128)(2,1)} %collective-permute-done.14.c_ref), channel_id=1, source_target_pairs={{0,1},{1,0},{2,3},{3,2},{4,5},{5,4},{6,7},{7,6},{8,9},{9,8},{10,11... | collective-permute-start | bytes 4718600 | tf_op jit(solution)/shard_map/ppermute | solution.py:506
  194.5 32.6 %collective-permute-start.11 = (bf16[2,8,384,128]{3,2,1,0:T(8,128)(2,1)}, bf16[2,8,384,128]{3,2,1,0:T(8,128)(2,1)}, u32[]{:S(2)}, u32[]{:S(2)}) collective-permute-start(bf16[2,8,384,128]{3,2,1,0:T(8,128)(2,1)} %collective-permute-done.10.c_ref), channel_id=1, source_target_pairs={{0,1},{1,0},{2,3},{3,2},{4,5},{5,4},{6,7},{7,6},{8,9},{9,8},{10,11... | collective-permute-start | bytes 4718600 | tf_op jit(solution)/shard_map/ppermute | solution.py:506
  226.8 16.5 %collective-permute-start.16 = (bf16[256,1024]{1,0:T(8,128)(2,1)}, bf16[256,1024]{1,0:T(8,128)(2,1)S(1)}, u32[]{:S(2)}, u32[]{:S(2)}) collective-permute-start(bf16[256,1024]{1,0:T(8,128)(2,1)} %terms.3.mine_ref), channel_id=1, source_target_pairs={{0,128},{16,144},{32,160},{48,176},{64,192},{80,208},{96,224},{112... | collective-permute-start | bytes 1572872 | tf_op jit(solution)/shard_map/ppermute | solution.py:559
  233.6 17.7 %collective-permute-start.12 = (bf16[256,1024]{1,0:T(8,128)(2,1)}, bf16[256,1024]{1,0:T(8,128)(2,1)S(1)}, u32[]{:S(2)}, u32[]{:S(2)}) collective-permute-start(bf16[256,1024]{1,0:T(8,128)(2,1)} %terms.2.mine_ref), channel_id=1, source_target_pairs={{0,128},{16,144},{32,160},{48,176},{64,192},{80,208},{96,224},{112... | collective-permute-start | bytes 1572872 | tf_op jit(solution)/shard_map/ppermute | solution.py:559
  257.5 27.7 %all-to-all-start.4 = ((bf16[8,264,128]{2,1,0:T(8,128)(2,1)}), bf16[8,264,128]{2,1,0:T(8,128)(2,1)S(1)}, u32[]{:S(2)}, u32[]{:S(2)}) async-start(bf16[8,264,128]{2,1,0:T(8,128)(2,1)} %get-tuple-element.44), calls=%async_computation.4 | async-start | bytes 1081344 | tf_op jit(solution)/shard_map/all_to_all | solution.py:530
  274.3 25.8 %collective-permute-start.17 = (bf16[4,2,8,128,128]{4,3,2,1,0:T(8,128)(2,1)}, bf16[4,2,8,128,128]{4,3,2,1,0:T(8,128)(2,1)}, u32[]{:S(2)}, u32[]{:S(2)}) collective-permute-start(bf16[4,2,8,128,128]{4,3,2,1,0:T(8,128)(2,1)} %get-tuple-element.50), channel_id=1, source_target_pairs={{0,1},{1,0},{2,3},{3,2},{4,5},{5,4},{6,7},{7,6},{8,9},{9,8},{10,11... | collective-permute-start | bytes 6291464 | tf_op jit(solution)/shard_map/ppermute | solution.py:464
  295.3 70.1 %all-to-all-start.5 = ((bf16[16,128,384]{2,1,0:T(8,128)(2,1)}), bf16[16,128,384]{2,1,0:T(8,128)(2,1)S(1)}, u32[]{:S(2)}, u32[]{:S(2)}) async-start(bf16[16,128,384]{2,1,0:T(8,128)(2,1)} %get-tuple-element.65), calls=%async_computation.5 | async-start | bytes 3145728 | tf_op jit(solution)/shard_map/all_to_all | solution.py:527
  304.1 15.0 %collective-permute-start.18 = (bf16[2,8,128,128]{3,2,1,0:T(8,128)(2,1)}, bf16[2,8,128,128]{3,2,1,0:T(8,128)(2,1)S(1)}, u32[]{:S(2)}, u32[]{:S(2)}) collective-permute-start(bf16[2,8,128,128]{3,2,1,0:T(8,128)(2,1)} %get-tuple-element.52), channel_id=1, source_target_pairs={{0,12},{1,13},{2,14},{3,15},{4,0},{5,1},{6,2},{7,3},{8,4},{9,5},{1... | collective-permute-start | bytes 1572872 | tf_op jit(solution)/shard_map/ppermute | solution.py:469
  305.5 16.7 %collective-permute-start.19 = (bf16[2,8,128,128]{3,2,1,0:T(8,128)(2,1)}, bf16[2,8,128,128]{3,2,1,0:T(8,128)(2,1)}, u32[]{:S(2)}, u32[]{:S(2)}) collective-permute-start(bf16[2,8,128,128]{3,2,1,0:T(8,128)(2,1)} %get-tuple-element.53), channel_id=1, source_target_pairs={{0,8},{1,9},{2,10},{3,11},{4,12},{5,13},{6,14},{7,15},{8,0},{9,1},... | collective-permute-start | bytes 1572872 | tf_op jit(solution)/shard_map/ppermute | solution.py:469
  307.4 23.1 %collective-permute-start.20 = (bf16[2,8,128,128]{3,2,1,0:T(8,128)(2,1)}, bf16[2,8,128,128]{3,2,1,0:T(8,128)(2,1)}, u32[]{:S(2)}, u32[]{:S(2)}) collective-permute-start(bf16[2,8,128,128]{3,2,1,0:T(8,128)(2,1)} %get-tuple-element.54), channel_id=1, source_target_pairs={{0,4},{1,5},{2,6},{3,7},{4,8},{5,9},{6,10},{7,11},{8,12},{9,13},{1... | collective-permute-start | bytes 1572872 | tf_op jit(solution)/shard_map/ppermute | solution.py:469
  (33 other events, 346.8 us)

commit v8 on v5

--- a/solution.py
+++ b/solution.py
@@ -244,7 +244,7 @@
             attn_ref[group, BOTH:, :] = rows.astype(jnp.bfloat16)
 
 
-def weight_kernel(place_ref, sout_ref, first_ref, second_ref, keep_ref, send_ref, turned):
+def weight_kernel(away, place_ref, sout_ref, first_ref, second_ref, part_ref, turned):
     step = pl.program_id(0)
 
     @pl.when(step == 0)
@@ -253,15 +253,19 @@
             turned[group] = sout_ref[group].T
 
     grad = jnp.where(step < CHUNK, first_ref[...], second_ref[...])
-    swapped = place_ref[2] == 1
+    high = jnp.bitwise_xor(place_ref[2], away) == 1
+    cols = jnp.concatenate(
+        [
+            jnp.where(high, grad[:, (side + 1) * D : (side + 2) * D], grad[:, side * D : (side + 1) * D])
+            for side in (0, 2)
+        ],
+        axis=1,
+    )
     for group in range(RING):
-        part = nn(turned[group], grad)
+        part = nn(turned[group], cols).astype(jnp.bfloat16)
         for side in range(2):
-            low = part[:, 2 * side * D : (2 * side + 1) * D]
-            high = part[:, (2 * side + 1) * D : (2 * side + 2) * D]
             across = jnp.bitwise_xor(place_ref[1], side)
-            keep_ref[0, across, group] = jnp.where(swapped, high, low).astype(jnp.bfloat16)
-            send_ref[0, across, group] = jnp.where(swapped, low, high).astype(jnp.bfloat16)
+            part_ref[0, across, group] = part[:, side * D : (side + 1) * D]
 
 
 def plus(*values):
@@ -269,6 +273,9 @@
     for value in values[1:]:
         total += value.astype(jnp.float32)
     return total.astype(jnp.bfloat16)
+
+
+ADD = 4
 
 
 def add_core_kernel(keep_ref, other_ref, *out_refs):
@@ -280,7 +287,7 @@
                 )
         return carry
 
-    lax.fori_loop(0, RING, one, 0)
+    lax.fori_loop(0, ADD, one, 0)
 
 
 def add_rows_kernel(own_ref, a_ref, b_ref, c_ref, keep_ref, send_ref):
@@ -411,12 +418,12 @@
     )(mine, other, weights, attn, square)
 
 
-def weight_parts(place, sout, grad_first, grad_second, interpret=False):
+def weight_parts(place, sout, grad_first, grad_second, away, interpret=False):
     turned = pl.BlockSpec(
         (1, 2, RING, D, D), lambda r, at: (lax.rem(r - at[0] + SIDES, SIDES), 0, 0, 0, 0)
     )
     return pl.pallas_call(
-        weight_kernel,
+        functools.partial(weight_kernel, away),
         grid_spec=pltpu.PrefetchScalarGridSpec(
             num_scalar_prefetch=1,
             grid=(SIDES,),
@@ -425,19 +432,32 @@
                 pl.BlockSpec((BOTH, COLS * D), lambda r, at: (0, jnp.minimum(r, CHUNK - 1))),
                 pl.BlockSpec((BOTH, COLS * D), lambda r, at: (0, jnp.maximum(r - CHUNK, 0))),
             ],
-            out_specs=(turned, turned),
+            out_specs=turned,
             scratch_shapes=[pltpu.VMEM((RING, D, BOTH), jnp.bfloat16)],
         ),
-        out_shape=(bf(SIDES, 2, RING, D, D),) * 2,
+        out_shape=bf(SIDES, 2, RING, D, D),
         name="weight_parts",
         interpret=interpret,
     )(place, sout, grad_first, grad_second)
 
 
-def reduce_parts(place, keep, send, run):
+def add_core(keep, other, interpret=False):
+    taken = pl.BlockSpec((SIDES, 2, ADD, D, D), lambda r: (0, 0, r, 0, 0))
+    given = pl.BlockSpec((2, ADD, D, D), lambda r: (0, r, 0, 0))
+    return pl.pallas_call(
+        add_core_kernel,
+        grid=(RING // ADD,),
+        out_shape=(bf(2, RING, D, D),) * SIDES,
+        in_specs=[taken, taken],
+        out_specs=(given,) * SIDES,
+        name="add_core_kernel",
+        interpret=interpret,
+    )(keep, other)
+
+
+def reduce_parts(place, keep, other, run):
     reps = range(GROUPS)
-    other = lax.ppermute(send, "rep", [(rep, rep ^ 1) for rep in reps])
-    own, *rest = run(add_core_kernel, (bf(2, RING, D, D),) * SIDES, (keep, other))
+    own, *rest = add_core(keep, other, **run.keywords)
     moved = []
     for turn, part in enumerate(rest, 1):
         moved.append(
@@ -538,8 +558,10 @@
         mine[1], other[1], weights, attn, square, interpret=interpret
     )
     grads = swap_ring(d_attn)
-    keep, send = weight_parts(place, s_tokens, grad_a, grad_b, interpret=interpret)
-    d_wo = reduce_parts(place, keep, send, run)
+    away = weight_parts(place, s_tokens, grad_a, grad_b, 1, interpret=interpret)
+    other = lax.ppermute(away, "rep", [(rep, rep ^ 1) for rep in range(GROUPS)])
+    keep = weight_parts(place, s_tokens, grad_a, grad_b, 0, interpret=interpret)
+    d_wo = reduce_parts(place, keep, other, run)
     back, loss = run(
         backward_kernel,
         (bf(GROUPS, TOKENS, 3 * D), fl(1, D)),

time: 340 us -> 344 us (1.012)
  Pallas kernels: 71 us -> 75 us
    pallas_call x1 -> x3, Pallas kernels: 5.88 us -> 13.9 us  [the longest x2 10.5 us: weight_parts(): pl.pallas_call(functools.partial(weight_kernel, away), grid_spec=pltpu.Pr...]
    pallas_call x10 -> x9, Pallas kernels: 46 us -> 42 us  [call(): pl.pallas_call(kernel, out_shape=outs, in_specs=specs, out_specs=VM if si...]
  transfers between devices with their start and end apart: 20 -> 20, of which waited for: 11 -> 11; matrix products, arithmetic and copies ran while one was open for 1% -> 1% of each run, Pallas kernels for 17% -> 18%
where the time goes in v8:
time: 344 us; the launch traced here: 342 us
  waiting for transfers between devices  123 us (36%)
  Pallas kernels  75 us (22%)
  blocking collectives  69.8 us (20%)
  starting transfers between devices  47.6 us (14%)
  between operations  14.2 us (4%)
  local copies, waits for them, and re-layouts  9.43 us (3%)
    all_gather x1, waiting for transfers between devices, gather_columns(): pieces = lax.all_gather(mine, 'seq', axis=0, axis_index_groups=RINGS)  42.3 us
    pallas_call x9, Pallas kernels, call(): pl.pallas_call(kernel, out_shape=outs, in_specs=specs, out_specs=VM if si...  42 us
    all_to_all x1, blocking collectives, swap(): lax.all_to_all(blocks, 'seq', split_axis=0, concat_axis=0, tiled=True)  40 us
    all_to_all x2, waiting for transfers between devices, swap(): lax.all_to_all(blocks, 'seq', split_axis=0, concat_axis=0, tiled=True)  32 us
    all_to_all x1, blocking collectives, swap_ring(): lax.all_to_all(blocks, 'seq', split_axis=0, concat_axis=0, tiled=True, ax...  29.8 us
    ppermute x3, waiting for transfers between devices, reduce_parts(): lax.ppermute(part, 'rep', [(rep, (rep + turn * COLS) % GROUPS) for rep in...  18.3 us
    ppermute x7, starting transfers between devices, reduce_parts(): lax.ppermute(part, 'seq', [(at, at // RING * RING + (at + turn) % RING) f...  16.6 us
    all_to_all x2, waiting for transfers between devices, swap_ring(): lax.all_to_all(blocks, 'seq', split_axis=0, concat_axis=0, tiled=True, ax...  13.7 us
  transfers between devices with their start and end apart: 20, of which 11 were waited for; matrix products, arithmetic and copies ran while one was open for 1% of the time, Pallas kernels for 18%

profile of v8, /device:TPU:4, one launch (start us, length us, event | category | flops | bytes accessed | tf_op | source)
XLA Modules:
  0.0 342.3 jit_solution(4138456368951001918)
XLA Ops:
  9.3 42.3 %all-gather.5.cloned.1.call-done = bf16[4224,128]{1,0:T(8,128)(2,1)} async-done(((bf16[528,128]{1,0:T(8,128)(2,1)}), bf16[4224,128]{1,0:T(8,128)(2,1)}) %all-gather.5.cloned.1.call-update) | async-done | bytes 1081360 | tf_op jit(solution)/shard_map/all_gather | solution.py:503
  53.8 3.8 %shard_map.137 = (bf16[16,128,384]{2,1,0:T(8,128)(2,1)}, bf16[16,128,512]{2,1,0:T(8,128)(2,1)}) custom-call(bf16[1,128,2048]{2,1,0:T(8,128)(2,1)} %sq_ref.1, bf16[1,128,512]{2,1,0:T(8,128)(2,1)} %sk_ref.1, bf16[1,128,512]{2,1,0:T(8,128)(2,1)} %sv_ref.1, bf16[1,128,4096]{2,1,0:T(8,128)(2,1)} %tq_ref.1, bf16[1,128,512]{2,1,0:T(8,128)(2,1)} %tk_ref.1, ...), custom_call_target="tpu_custom_call" | custom-call | tf_op jit(solution)/shard_map/pallas_call | solution.py:359
  57.7 40.0 %all_to_all.30.in_ref = bf16[16,128,384]{2,1,0:T(8,128)(2,1)} all-to-all(bf16[16,128,384]{2,1,0:T(8,128)(2,1)} %get-tuple-element.35), channel_id=1, replica_groups=mesh['seq'=16,'rep'=16] {'seq'}, dimensions={0} | all-to-all | bytes 3145728 | tf_op jit(solution)/shard_map/all_to_all | solution.py:523
  97.7 7.3 %all-to-all-start.1 = ((bf16[16,128,512]{2,1,0:T(8,128)(2,1)}), bf16[16,128,512]{2,1,0:T(8,128)(2,1)S(1)}, u32[]{:S(2)}, u32[]{:S(2)}) async-start(bf16[16,128,512]{2,1,0:T(8,128)(2,1)} %get-tuple-element.38), calls=%async_computation.1 | async-start | bytes 4194304 | tf_op jit(solution)/shard_map/all_to_all | solution.py:523
  108.7 8.7 %shard_map.138 = (bf16[8,256,128]{2,1,0:T(8,128)(2,1)}, bf16[8,256,768]{2,1,0:T(8,128)(2,1)}) custom-call(s32[32]{0:T(128)} %bitcast.20, s32[8]{0:T(128)} %slice.6.first_ref, s32[2048,1]{1,0:T(8,128)} %copy.17.start_ref, bf16[16,128,384]{2,1,0:T(8,128)(2,1)} %all_to_all.30.in_ref), custom_call_target="tpu_custom_call" | custom-call | tf_op jit(solution)/shard_map/pallas_call | solution.py:359
  117.4 32.0 %all-to-all-done.1.in_ref = bf16[16,128,512]{2,1,0:T(8,128)(2,1)S(1)} async-done(((bf16[16,128,512]{2,1,0:T(8,128)(2,1)}), bf16[16,128,512]{2,1,0:T(8,128)(2,1)S(1)}, u32[]{:S(2)}, u32[]{:S(2)}) %all-to-all-start.1) | async-done | bytes 2097184 | tf_op jit(solution)/shard_map/all_to_all | solution.py:523
  150.8 4.2 %all-to-all-start.2 = ((bf16[8,256,128]{2,1,0:T(8,128)(2,1)}), bf16[8,256,128]{2,1,0:T(8,128)(2,1)S(1)}, u32[]{:S(2)}, u32[]{:S(2)}) async-start(bf16[8,256,128]{2,1,0:T(8,128)(2,1)} %get-tuple-element.39.out_ref), calls=%async_computation.2 | async-start | bytes 1048576 | tf_op jit(solution)/shard_map/all_to_all | solution.py:526
  155.0 9.8 %shard_map.139 = bf16[8,256,256]{2,1,0:T(8,128)(2,1)} custom-call(s32[32]{0:T(128)} %bitcast.21, s32[8]{0:T(128)} %slice.6.first_ref, s32[2048,1]{1,0:T(8,128)} %copy.17.start_ref, bf16[16,128,512]{2,1,0:T(8,128)(2,1)} %copy-done.2), custom_call_target="tpu_custom_call" | custom-call | tf_op jit(solution)/shard_map/pallas_call | solution.py:359
  164.8 5.5 %all-to-all-done.2.sout_ref = bf16[8,256,128]{2,1,0:T(8,128)(2,1)S(1)} async-done(((bf16[8,256,128]{2,1,0:T(8,128)(2,1)}), bf16[8,256,128]{2,1,0:T(8,128)(2,1)S(1)}, u32[]{:S(2)}, u32[]{:S(2)}) %all-to-all-start.2) | async-done | bytes 524320 | tf_op jit(solution)/shard_map/all_to_all | solution.py:526
  170.2 29.8 %all_to_all.31.tout_ref = bf16[8,256,256]{2,1,0:T(8,128)(2,1)} all-to-all(bf16[8,256,256]{2,1,0:T(8,128)(2,1)} %shard_map.139), channel_id=1, replica_groups={{0,16,32,48,64,80,96,112},{128,144,160,176,192,208,224,240},{1,17,33,49..., dimensions={0} | all-to-all | bytes 2097152 | tf_op jit(solution)/shard_map/all_to_all | solution.py:526
  200.0 5.7 %terms.3.mine_ref = bf16[256,1024]{1,0:T(8,128)(2,1)} custom-call(bf16[8,256,128]{2,1,0:T(8,128)(2,1)} %copy-done.1, bf16[8,256,256]{2,1,0:T(8,128)(2,1)} %all_to_all.31.tout_ref, bf16[16,8,384,128]{3,2,1,0:T(8,128)(2,1)} %bitcast.14), custom_call_target="tpu_custom_call" | custom-call | tf_op jit(solution)/shard_map/terms/pallas_call | solution.py:382
  205.7 5.6 %terms.2.mine_ref = bf16[256,1024]{1,0:T(8,128)(2,1)} custom-call(bf16[8,256,128]{2,1,0:T(8,128)(2,1)} %copy-done.1, bf16[8,256,256]{2,1,0:T(8,128)(2,1)} %all_to_all.31.tout_ref, bf16[16,8,384,128]{3,2,1,0:T(8,128)(2,1)} %bitcast.15), custom_call_target="tpu_custom_call" | custom-call | tf_op jit(solution)/shard_map/terms/pallas_call | solution.py:382
  214.8 7.1 %collective-permute-done.1.other_ref = bf16[256,1024]{1,0:T(8,128)(2,1)S(1)} collective-permute-done((bf16[256,1024]{1,0:T(8,128)(2,1)}, bf16[256,1024]{1,0:T(8,128)(2,1)S(1)}, u32[]{:S(2)}, u32[]{:S(2)}) %collective-permute-start.1) | collective-permute-done | bytes 524320 | tf_op jit(solution)/shard_map/ppermute | solution.py:555
  222.8 3.7 %gradients_first.1 = (bf16[256,1024]{1,0:T(8,128)(2,1)}, f32[1024,256]{1,0:T(8,128)}, f32[1,128]{1,0:T(1,128)}) custom-call(bf16[256,1024]{1,0:T(8,128)(2,1)} %terms.3.mine_ref, bf16[256,1024]{1,0:T(8,128)(2,1)} %copy-done.7, bf16[16,8,384,128]{3,2,1,0:T(8,128)(2,1)} %bitcast.16), custom_call_target="tpu_custom_call" | custom-call | tf_op jit(solution)/shard_map/gradients_first/pallas_call | solution.py:394
  228.4 4.1 %gradients_second.1 = (bf16[256,1024]{1,0:T(8,128)(2,1)}, bf16[8,264,128]{2,1,0:T(8,128)(2,1)}) custom-call(bf16[256,1024]{1,0:T(8,128)(2,1)} %terms.2.mine_ref, bf16[256,1024]{1,0:T(8,128)(2,1)} %copy-done.5, bf16[16,8,384,128]{3,2,1,0:T(8,128)(2,1)} %bitcast.17, f32[1024,256]{1,0:T(8,128)} %get-tuple-element.40.attn_in, f32[1,128]{1,0:T(1,128)} %get-tuple-element.41.square_in), custom_call_target="tpu_custom_call" | custom-call | tf_op jit(solution)/shard_map/gradients_second/pallas_call | solution.py:406
  236.7 5.3 %weight_parts.3 = bf16[4,2,8,128,128]{4,3,2,1,0:T(8,128)(2,1)} custom-call(s32[4]{0:T(128)} %pad_add_fusion.place_ref, bf16[8,256,128]{2,1,0:T(8,128)(2,1)} %copy-done.1, bf16[256,1024]{1,0:T(8,128)(2,1)} %get-tuple-element.45.first_ref, bf16[256,1024]{1,0:T(8,128)(2,1)} %get-tuple-element.46.second_ref), custom_call_target="tpu_custom_call" | custom-call | tf_op jit(solution)/shard_map/weight_parts/pallas_call | solution.py:425
  241.9 8.2 %all-to-all-done.4.grad_ref = bf16[8,264,128]{2,1,0:T(8,128)(2,1)S(1)} async-done(((bf16[8,264,128]{2,1,0:T(8,128)(2,1)}), bf16[8,264,128]{2,1,0:T(8,128)(2,1)S(1)}, u32[]{:S(2)}, u32[]{:S(2)}) %all-to-all-start.4) | async-done | bytes 540704 | tf_op jit(solution)/shard_map/all_to_all | solution.py:526
  251.0 9.2 %shard_map.141 = (bf16[16,128,384]{2,1,0:T(8,128)(2,1)}, f32[1,128]{1,0:T(1,128)}) custom-call(s32[32]{0:T(128)} %bitcast.22, s32[8]{0:T(128)} %slice.6.first_ref, bf16[8,264,128]{2,1,0:T(8,128)(2,1)} %copy-done.4, bf16[8,256,128]{2,1,0:T(8,128)(2,1)} %get-tuple-element.39.out_ref, bf16[16,128,384]{2,1,0:T(8,128)(2,1)} %all_to_all.30.in_ref, ...), custom_call_target="tpu_custom_call" | custom-call | tf_op jit(solution)/shard_map/pallas_call | solution.py:359
  260.1 5.1 %all-to-all-start.5 = ((bf16[16,128,384]{2,1,0:T(8,128)(2,1)}), bf16[16,128,384]{2,1,0:T(8,128)(2,1)S(1)}, u32[]{:S(2)}, u32[]{:S(2)}) async-start(bf16[16,128,384]{2,1,0:T(8,128)(2,1)} %get-tuple-element.61), calls=%async_computation.5 | async-start | bytes 3145728 | tf_op jit(solution)/shard_map/all_to_all | solution.py:523
  265.3 5.3 %weight_parts.2.keep_ref = bf16[4,2,8,128,128]{4,3,2,1,0:T(8,128)(2,1)} custom-call(s32[4]{0:T(128)} %pad_add_fusion.place_ref, bf16[8,256,128]{2,1,0:T(8,128)(2,1)} %copy-done.1, bf16[256,1024]{1,0:T(8,128)(2,1)} %get-tuple-element.45.first_ref, bf16[256,1024]{1,0:T(8,128)(2,1)} %get-tuple-element.46.second_ref), custom_call_target="tpu_custom_call" | custom-call | tf_op jit(solution)/shard_map/weight_parts/pallas_call | solution.py:425
  280.2 8.7 %collective-permute-done.3.a_ref = bf16[2,8,128,128]{3,2,1,0:T(8,128)(2,1)S(1)} collective-permute-done((bf16[2,8,128,128]{3,2,1,0:T(8,128)(2,1)}, bf16[2,8,128,128]{3,2,1,0:T(8,128)(2,1)S(1)}, u32[]{:S(2)}, u32[]{:S(2)}) %collective-permute-start.3) | collective-permute-done | bytes 524320 | tf_op jit(solution)/shard_map/ppermute | solution.py:464
  288.9 9.6 %collective-permute-done.4.b_ref = bf16[2,8,128,128]{3,2,1,0:T(8,128)(2,1)} collective-permute-done((bf16[2,8,128,128]{3,2,1,0:T(8,128)(2,1)}, bf16[2,8,128,128]{3,2,1,0:T(8,128)(2,1)}, u32[]{:S(2)}, u32[]{:S(2)}) %collective-permute-start.4) | collective-permute-done | bytes 524320 | tf_op jit(solution)/shard_map/ppermute | solution.py:464
  302.1 5.8 %collective-permute-done.6.other_ref = bf16[8,128,128]{2,1,0:T(8,128)(2,1)S(1)} collective-permute-done((bf16[8,128,128]{2,1,0:T(8,128)(2,1)}, bf16[8,128,128]{2,1,0:T(8,128)(2,1)S(1)}, u32[]{:S(2)}, u32[]{:S(2)}) %collective-permute-start.6) | collective-permute-done | bytes 262176 | tf_op jit(solution)/shard_map/ppermute | solution.py:467
  322.0 3.6 %collective-permute-start.12 = (bf16[128,128]{1,0:T(8,128)(2,1)}, bf16[128,128]{1,0:T(8,128)(2,1)S(1)}, u32[]{:S(2)}, u32[]{:S(2)}) collective-permute-start(bf16[128,128]{1,0:T(8,128)(2,1)} %get-tuple-element.59), channel_id=1, source_target_pairs={{0,96},{16,112},{32,0},{48,16},{64,32},{80,48},{96,64},{112,80},{1... | collective-permute-start | bytes 98312 | tf_op jit(solution)/shard_map/ppermute | solution.py:470
  (79 shorter events, 57.8 us)
Async XLA Ops:
  7.2 44.5 %all-gather.5.cloned.1.call-start = ((), (), s32[]{:S(2)}) async-start(), calls=%async_computation.6 | async-start | bytes 1216512 | tf_op jit(solution)/shard_map/all_gather | solution.py:503
  9.3 190.7 %all-gather.7.cloned.1.call-start = ((), (), s32[]{:S(2)}) async-start(), calls=%async_computation.7 | async-start | bytes 13369344 | tf_op jit(solution)/shard_map/all_gather | solution.py:505
  97.7 7.3 %copy-start.16 = (s32[1,2048]{1,0:T(1,128)S(1)}, s32[1,2048]{1,0:T(1,128)}, u32[]{:S(2)}) copy-start(s32[1,2048]{1,0:T(1,128)} %param.18) | copy-start | bytes 24580
  97.7 51.7 %all-to-all-start.1 = ((bf16[16,128,512]{2,1,0:T(8,128)(2,1)}), bf16[16,128,512]{2,1,0:T(8,128)(2,1)S(1)}, u32[]{:S(2)}, u32[]{:S(2)}) async-start(bf16[16,128,512]{2,1,0:T(8,128)(2,1)} %get-tuple-element.38), calls=%async_computation.1 | async-start | bytes 4194304 | tf_op jit(solution)/shard_map/all_to_all | solution.py:523
  150.8 19.4 %all-to-all-start.2 = ((bf16[8,256,128]{2,1,0:T(8,128)(2,1)}), bf16[8,256,128]{2,1,0:T(8,128)(2,1)S(1)}, u32[]{:S(2)}, u32[]{:S(2)}) async-start(bf16[8,256,128]{2,1,0:T(8,128)(2,1)} %get-tuple-element.39.out_ref), calls=%async_computation.2 | async-start | bytes 1048576 | tf_op jit(solution)/shard_map/all_to_all | solution.py:526
  170.2 29.8 %copy-start.1 = (bf16[8,256,128]{2,1,0:T(8,128)(2,1)}, bf16[8,256,128]{2,1,0:T(8,128)(2,1)S(1)}, u32[]{:S(2)}) copy-start(bf16[8,256,128]{2,1,0:T(8,128)(2,1)S(1)} %all-to-all-done.2.sout_ref) | copy-start | bytes 1572868
  205.7 16.3 %collective-permute-start.1 = (bf16[256,1024]{1,0:T(8,128)(2,1)}, bf16[256,1024]{1,0:T(8,128)(2,1)S(1)}, u32[]{:S(2)}, u32[]{:S(2)}) collective-permute-start(bf16[256,1024]{1,0:T(8,128)(2,1)} %terms.3.mine_ref), channel_id=1, source_target_pairs={{0,128},{16,144},{32,160},{48,176},{64,192},{80,208},{96,224},{112... | collective-permute-start | bytes 1572872 | tf_op jit(solution)/shard_map/ppermute | solution.py:555
  211.3 16.3 %collective-permute-start = (bf16[256,1024]{1,0:T(8,128)(2,1)}, bf16[256,1024]{1,0:T(8,128)(2,1)S(1)}, u32[]{:S(2)}, u32[]{:S(2)}) collective-permute-start(bf16[256,1024]{1,0:T(8,128)(2,1)} %terms.2.mine_ref), channel_id=1, source_target_pairs={{0,128},{16,144},{32,160},{48,176},{64,192},{80,208},{96,224},{112... | collective-permute-start | bytes 1572872 | tf_op jit(solution)/shard_map/ppermute | solution.py:555
  232.5 17.7 %all-to-all-start.4 = ((bf16[8,264,128]{2,1,0:T(8,128)(2,1)}), bf16[8,264,128]{2,1,0:T(8,128)(2,1)S(1)}, u32[]{:S(2)}, u32[]{:S(2)}) async-start(bf16[8,264,128]{2,1,0:T(8,128)(2,1)} %get-tuple-element.42), calls=%async_computation.4 | async-start | bytes 1081344 | tf_op jit(solution)/shard_map/all_to_all | solution.py:526
  241.9 28.6 %collective-permute-start.2 = (bf16[4,2,8,128,128]{4,3,2,1,0:T(8,128)(2,1)}, bf16[4,2,8,128,128]{4,3,2,1,0:T(8,128)(2,1)}, u32[]{:S(2)}, u32[]{:S(2)}) collective-permute-start(bf16[4,2,8,128,128]{4,3,2,1,0:T(8,128)(2,1)} %weight_parts.3), channel_id=1, source_target_pairs={{0,1},{1,0},{2,3},{3,2},{4,5},{5,4},{6,7},{7,6},{8,9},{9,8},{10,11... | collective-permute-start | bytes 6291464 | tf_op jit(solution)/shard_map/ppermute | solution.py:562
  260.1 71.7 %all-to-all-start.5 = ((bf16[16,128,384]{2,1,0:T(8,128)(2,1)}), bf16[16,128,384]{2,1,0:T(8,128)(2,1)S(1)}, u32[]{:S(2)}, u32[]{:S(2)}) async-start(bf16[16,128,384]{2,1,0:T(8,128)(2,1)} %get-tuple-element.61), calls=%async_computation.5 | async-start | bytes 3145728 | tf_op jit(solution)/shard_map/all_to_all | solution.py:523
  273.9 15.0 %collective-permute-start.3 = (bf16[2,8,128,128]{3,2,1,0:T(8,128)(2,1)}, bf16[2,8,128,128]{3,2,1,0:T(8,128)(2,1)S(1)}, u32[]{:S(2)}, u32[]{:S(2)}) collective-permute-start(bf16[2,8,128,128]{3,2,1,0:T(8,128)(2,1)} %get-tuple-element.48), channel_id=1, source_target_pairs={{0,4},{1,5},{2,6},{3,7},{4,8},{5,9},{6,10},{7,11},{8,12},{9,13},{1... | collective-permute-start | bytes 1572872 | tf_op jit(solution)/shard_map/ppermute | solution.py:464
  276.1 22.4 %collective-permute-start.4 = (bf16[2,8,128,128]{3,2,1,0:T(8,128)(2,1)}, bf16[2,8,128,128]{3,2,1,0:T(8,128)(2,1)}, u32[]{:S(2)}, u32[]{:S(2)}) collective-permute-start(bf16[2,8,128,128]{3,2,1,0:T(8,128)(2,1)} %get-tuple-element.49), channel_id=1, source_target_pairs={{0,8},{1,9},{2,10},{3,11},{4,12},{5,13},{6,14},{7,15},{8,0},{9,1},... | collective-permute-start | bytes 1572872 | tf_op jit(solution)/shard_map/ppermute | solution.py:464
  278.3 20.2 %collective-permute-start.5 = (bf16[2,8,128,128]{3,2,1,0:T(8,128)(2,1)}, bf16[2,8,128,128]{3,2,1,0:T(8,128)(2,1)}, u32[]{:S(2)}, u32[]{:S(2)}) collective-permute-start(bf16[2,8,128,128]{3,2,1,0:T(8,128)(2,1)} %get-tuple-element.50), channel_id=1, source_target_pairs={{0,12},{1,13},{2,14},{3,15},{4,0},{5,1},{6,2},{7,3},{8,4},{9,5},{1... | collective-permute-start | bytes 1572872 | tf_op jit(solution)/shard_map/ppermute | solution.py:464
  288.9 9.6 %copy-start.6 = (bf16[2,8,128,128]{3,2,1,0:T(8,128)(2,1)}, bf16[2,8,128,128]{3,2,1,0:T(8,128)(2,1)S(1)}, u32[]{:S(2)}) copy-start(bf16[2,8,128,128]{3,2,1,0:T(8,128)(2,1)S(1)} %collective-permute-done.3.a_ref) | copy-start | bytes 1572868
  301.1 6.9 %collective-permute-start.6 = (bf16[8,128,128]{2,1,0:T(8,128)(2,1)}, bf16[8,128,128]{2,1,0:T(8,128)(2,1)S(1)}, u32[]{:S(2)}, u32[]{:S(2)}) collective-permute-start(bf16[8,128,128]{2,1,0:T(8,128)(2,1)} %get-tuple-element.52), channel_id=1, source_target_pairs={{0,2},{1,3},{2,0},{3,1},{4,6},{5,7},{6,4},{7,5},{8,10},{9,11},{10,... | collective-permute-start | bytes 786440 | tf_op jit(solution)/shard_map/ppermute | solution.py:467
  310.4 11.6 %collective-permute-start.7 = (bf16[128,128]{1,0:T(8,128)(2,1)}, bf16[128,128]{1,0:T(8,128)(2,1)S(1)}, u32[]{:S(2)}, u32[]{:S(2)}) collective-permute-start(bf16[128,128]{1,0:T(8,128)(2,1)} %get-tuple-element.54), channel_id=1, source_target_pairs={{0,16},{16,32},{32,48},{48,64},{64,80},{80,96},{96,112},{112,0},{1... | collective-permute-start | bytes 98312 | tf_op jit(solution)/shard_map/ppermute | solution.py:470
  311.9 13.6 %collective-permute-start.8 = (bf16[128,128]{1,0:T(8,128)(2,1)}, bf16[128,128]{1,0:T(8,128)(2,1)S(1)}, u32[]{:S(2)}, u32[]{:S(2)}) collective-permute-start(bf16[128,128]{1,0:T(8,128)(2,1)} %get-tuple-element.55), channel_id=1, source_target_pairs={{0,32},{16,48},{32,64},{48,80},{64,96},{80,112},{96,0},{112,16},{1... | collective-permute-start | bytes 98312 | tf_op jit(solution)/shard_map/ppermute | solution.py:470
  314.3 12.8 %collective-permute-start.9 = (bf16[128,128]{1,0:T(8,128)(2,1)}, bf16[128,128]{1,0:T(8,128)(2,1)S(1)}, u32[]{:S(2)}, u32[]{:S(2)}) collective-permute-start(bf16[128,128]{1,0:T(8,128)(2,1)} %get-tuple-element.56), channel_id=1, source_target_pairs={{0,48},{16,64},{32,80},{48,96},{64,112},{80,0},{96,16},{112,32},{1... | collective-permute-start | bytes 98312 | tf_op jit(solution)/shard_map/ppermute | solution.py:470
  317.0 10.1 %collective-permute-start.10 = (bf16[128,128]{1,0:T(8,128)(2,1)}, bf16[128,128]{1,0:T(8,128)(2,1)S(1)}, u32[]{:S(2)}, u32[]{:S(2)}) collective-permute-start(bf16[128,128]{1,0:T(8,128)(2,1)} %get-tuple-element.57), channel_id=1, source_target_pairs={{0,64},{16,80},{32,96},{48,112},{64,0},{80,16},{96,32},{112,48},{1... | collective-permute-start | bytes 98312 | tf_op jit(solution)/shard_map/ppermute | solution.py:470
  319.3 7.8 %collective-permute-start.11 = (bf16[128,128]{1,0:T(8,128)(2,1)}, bf16[128,128]{1,0:T(8,128)(2,1)S(1)}, u32[]{:S(2)}, u32[]{:S(2)}) collective-permute-start(bf16[128,128]{1,0:T(8,128)(2,1)} %get-tuple-element.58), channel_id=1, source_target_pairs={{0,80},{16,96},{32,112},{48,0},{64,16},{80,32},{96,48},{112,64},{1... | collective-permute-start | bytes 98312 | tf_op jit(solution)/shard_map/ppermute | solution.py:470
  322.0 7.7 %copy-start.9 = (bf16[128,128]{1,0:T(8,128)(2,1)}, bf16[128,128]{1,0:T(8,128)(2,1)S(1)}, u32[]{:S(2)}) copy-start(bf16[128,128]{1,0:T(8,128)(2,1)S(1)} %collective-permute-done.7.refs_1_) | copy-start | bytes 98308
  322.0 5.7 %collective-permute-start.12 = (bf16[128,128]{1,0:T(8,128)(2,1)}, bf16[128,128]{1,0:T(8,128)(2,1)S(1)}, u32[]{:S(2)}, u32[]{:S(2)}) collective-permute-start(bf16[128,128]{1,0:T(8,128)(2,1)} %get-tuple-element.59), channel_id=1, source_target_pairs={{0,96},{16,112},{32,0},{48,16},{64,32},{80,48},{96,64},{112,80},{1... | collective-permute-start | bytes 98312 | tf_op jit(solution)/shard_map/ppermute | solution.py:470
  325.6 4.1 %collective-permute-start.13 = (bf16[128,128]{1,0:T(8,128)(2,1)}, bf16[128,128]{1,0:T(8,128)(2,1)S(1)}, u32[]{:S(2)}, u32[]{:S(2)}) collective-permute-start(bf16[128,128]{1,0:T(8,128)(2,1)} %get-tuple-element.60), channel_id=1, source_target_pairs={{0,112},{16,0},{32,16},{48,32},{64,48},{80,64},{96,80},{112,96},{1... | collective-permute-start | bytes 98312 | tf_op jit(solution)/shard_map/ppermute | solution.py:470
  (13 other events, 21.5 us)
Sparse Core Ops, SparseCore 0:
  10.3 41.2 all-gather.4
  54.0 110.0 all-gather.6
